TPU v7x, 256 devices: a whole 4x4x8 slice. The times are simulated.
256 devices in a mesh: gx: 4 (over y), gy: 8 (over x, core), gz: 8 (over z).
Axes of the slice: x: 4, y: 4, z: 8, core: 2. Of those that a mesh axis runs over, the one named last changes fastest.
Arguments:
- gradient: float32 [4, 8, 8, 16, 512], P('gx', 'gy', 'gz'), may hold values from -60 to 60
- local_schur: bfloat16 [4, 8, 8, 2048, 2048], P('gx', 'gy', 'gz'), may hold values from -1 to 4
- inverse_rows: bfloat16 [4, 8, 8, 512, 2048], P('gx', 'gy', 'gz'), may hold values from -0.1 to 0.6
- face_maps: int32 [4, 8, 8, 6, 256], P('gx', 'gy', 'gz'), may hold values from 0 to 511, as said below
Outputs:
- adjoint: float32 [4, 8, 8, 16, 512], P('gx', 'gy', 'gz')
- residual_ratio: float32 [16], replicated
Inputs may be any that keep to these rules, and one draw needn't show every extreme that they name: `face_maps`: for each subdomain and face, 256 distinct owned rows of the neighbour across that face.
All inputs are finite; a program needn't handle non-finite values.
Results may differ from a plain program's by a relative error of at most 0.0038.
Values may be sent and summed in bfloat16 or wider, within the bound.
No kernel may reach another device: no remote copies, remote signals or barrier semaphores. Data moves between devices by JAX's collectives and lax.ppermute only.
A program may use at most 64 MiB of HBM per device.

v0:
```python
import functools

import jax
import jax.numpy as jnp
from jax import lax
from jax.sharding import Mesh
from jax.sharding import PartitionSpec as P

ITERS = 3
GY = ("gy_0", "gy_1")
GX_GY_GZ = ("gx", "gy_0", "gy_1", "gz")


EPSILON = 1e-06
FACE_SPOTS = ((0, 1, 1), (2, 1, 1), (1, 0, 1), (1, 2, 1), (1, 1, 0), (1, 1, 2))


def from_behind(array, axis, by):
    devices = lax.axis_size(axis)
    pairs = [(i, i + by) for i in range(devices) if 0 <= i + by < devices]
    return lax.ppermute(array, axis, pairs)


def padded(array, sides, width):
    edges = {}
    for axis, dim in sides:
        devices, length = (lax.axis_size(axis), array.shape[dim])
        up = [(i, (i + 1) % devices) for i in range(devices - 1)]
        last = lax.slice_in_dim(array, length - width, length, axis=dim)
        initial = lax.slice_in_dim(array, 0, width, axis=dim)
        edges[dim] = (
            lax.ppermute(last, axis, up),
            lax.ppermute(initial, axis, [(b, a) for a, b in up]),
        )
    done = []
    for _, dim in sides:
        low, high = edges[dim]
        around = [(width, width) if d in done else (0, 0) for d in range(array.ndim)]
        array = jnp.concatenate([jnp.pad(low, around), array, jnp.pad(high, around)], axis=dim)
        done.append(dim)
    return array


def one_axis_at_a_time(array, axes):
    return functools.reduce(lax.psum, axes, array)


def pass_sums(outgoing):
    incoming = [None] * 6
    for offset, source_face, target_face in ((-1, 0, 1), (1, 1, 0)):
        incoming[target_face] = from_behind(outgoing[source_face], "gx", offset)
        incoming[target_face + 2] = from_behind(outgoing[source_face + 2], GY, offset)
        incoming[target_face + 4] = from_behind(outgoing[source_face + 4], "gz", offset)
    return incoming


def gather_local(rounded, owned_maps):
    ghost_layer = padded(rounded[None, None, None], (("gx", 0), (GY, 1), ("gz", 2)), 1)
    ghosts = [
        jnp.take(ghost_layer[FACE_SPOTS[facing]], owned_maps[facing], axis=1) for facing in range(6)
    ]
    return jnp.concatenate([rounded] + ghosts, axis=1)


def assemble(products, owned_maps):
    face_width = owned_maps.shape[1]
    owned = products.shape[1] - 6 * face_width
    result = products[:, :owned]
    face_blocks = [
        products[:, owned + facing * face_width : owned + (facing + 1) * face_width]
        for facing in range(6)
    ]
    outgoing = [
        jnp.zeros_like(result).at[:, owned_maps[facing]].add(face_blocks[facing])
        for facing in range(6)
    ]
    incoming = pass_sums(outgoing)
    for facing in range(6):
        result = result + incoming[facing]
    return result


def inner_local(left_side, right_side):
    return jnp.sum(left_side * right_side, axis=1)


def rotate_solve(columns, beta_norm):
    num_cols = len(columns)
    rhs_vec = [beta_norm] + [jnp.zeros_like(beta_norm) for unused in range(num_cols)]
    cosines = []
    sines = []
    triangle = []
    for section in range(num_cols):
        column = [columns[section][row_at] for row_at in range(section + 2)]
        for earlier in range(section):
            rotated_a = cosines[earlier] * column[earlier] + sines[earlier] * column[earlier + 1]
            rotated_b = -sines[earlier] * column[earlier] + cosines[earlier] * column[earlier + 1]
            column[earlier] = rotated_a
            column[earlier + 1] = rotated_b
        radius = jnp.sqrt(
            column[section] * column[section] + column[section + 1] * column[section + 1]
        )
        cosine = column[section] / radius
        sine_val = column[section + 1] / radius
        column[section] = radius
        cosines.append(cosine)
        sines.append(sine_val)
        rhs_vec[section + 1] = -sine_val * rhs_vec[section]
        rhs_vec[section] = cosine * rhs_vec[section]
        triangle.append(column[: section + 1])
    coeffs = [None] * num_cols
    for section in reversed(range(num_cols)):
        running = rhs_vec[section]
        for onward in range(section + 1, num_cols):
            running = running - triangle[onward][section] * coeffs[onward]
        coeffs[section] = running / triangle[section][section]
    return (coeffs, jnp.abs(rhs_vec[num_cols]))


def local(gradient, local_schur, inverse_rows, face_maps):
    target = gradient[0, 0, 0]
    schur_block = local_schur[0, 0, 0]
    restricted = inverse_rows[0, 0, 0]
    owned_maps = face_maps[0, 0, 0]
    initial = one_axis_at_a_time(inner_local(target, target), GX_GY_GZ)
    beta_norm = jnp.sqrt(initial + EPSILON)
    krylov = [target / beta_norm[:, None]]
    directions = []
    columns = []
    gram_rows = []
    for section in range(ITERS):
        rounded = krylov[section].astype(jnp.bfloat16)
        prepared = assemble(
            jnp.dot(rounded, restricted, preferred_element_type=jnp.float32), owned_maps
        )
        directions.append(prepared)
        transposed_rounded = prepared.astype(jnp.bfloat16)
        intersected = gather_local(transposed_rounded, owned_maps)
        applied = assemble(
            jnp.dot(intersected, schur_block, preferred_element_type=jnp.float32), owned_maps
        )
        local_coeffs = jnp.stack([inner_local(vector, applied) for vector in krylov])
        local_gram = jnp.stack([inner_local(krylov[section], vector) for vector in krylov])
        coeffs, squares, gram_row = (
            one_axis_at_a_time(local_coeffs, GX_GY_GZ),
            one_axis_at_a_time(inner_local(applied, applied), GX_GY_GZ),
            one_axis_at_a_time(local_gram, GX_GY_GZ),
        )
        gram_rows.append(gram_row)
        residue = applied
        for position in range(section + 1):
            residue = residue - coeffs[position][:, None] * krylov[position]
        running = squares
        for earlier in range(section + 1):
            running = running - 2.0 * coeffs[earlier] * coeffs[earlier]
            for onward in range(section + 1):
                element = gram_rows[max(earlier, onward)][min(earlier, onward)]
                running = running + coeffs[earlier] * element * coeffs[onward]
        height = jnp.sqrt(jnp.maximum(running, 0.0) + EPSILON)
        columns.append([coeffs[position] for position in range(section + 1)] + [height])
        if section + 1 < ITERS:
            krylov.append(residue / height[:, None])
    weights, remainder = rotate_solve(columns, beta_norm)
    adjoint = weights[0][:, None] * directions[0]
    for position in range(1, ITERS):
        adjoint = adjoint + weights[position][:, None] * directions[position]
    return (adjoint[None, None, None], remainder / beta_norm)


def solution(mesh):
    torus = Mesh(
        mesh.devices.reshape(mesh.shape["gx"], 4, 2, mesh.shape["gz"]), ("gx", "gy_0", "gy_1", "gz")
    )
    placed = (
        P("gx", GY, "gz", None, None),
        P("gx", GY, "gz", None, None),
        P("gx", GY, "gz", None, None),
        P("gx", GY, "gz", None, None),
    )
    return jax.shard_map(
        local,
        mesh=torus,
        in_specs=placed,
        out_specs=(P("gx", GY, "gz", None, None), P()),
        check_vma=False,
    )
```

profile of v0, /device:TPU:10, one launch (start us, length us, event | category | flops | bytes accessed | tf_op | source)
XLA Modules:
  0.0 421.2 jit_solution(7336692105669959526)
XLA Ops:
  1.7 8.7 %psum.280 = f32[16]{0:T(128)S(1)} all-reduce(f32[16]{0:T(128)S(1)} %fusion.114), channel_id=1, replica_groups=mesh['gx'=4,'gy_0'=4,'gy_1'=2,'gz'=8] {'gx'}, use_global_device_ids=true, to_apply=%region_1.0 | all-reduce | flops 16 | bytes 128 | tf_op jit(solution)/shard_map/psum | solution.py:45
  10.4 9.4 %psum.281 = f32[16]{0:T(128)S(1)} all-reduce(f32[16]{0:T(128)S(1)} %psum.280), channel_id=1, replica_groups=mesh['gx'=4,'gy_0'=4,'gy_1'=2,'gz'=8] {'gy_0'}, use_global_device_ids=true, to_apply=%region_2.0 | all-reduce | flops 16 | bytes 128 | tf_op jit(solution)/shard_map/psum | solution.py:45
  22.2 19.2 %psum.283 = f32[16]{0:T(128)S(1)} all-reduce(f32[16]{0:T(128)S(1)} %psum.282), channel_id=1, replica_groups=mesh['gx'=4,'gy_0'=4,'gy_1'=2,'gz'=8] {'gz'}, use_global_device_ids=true, to_apply=%region_4.0 | all-reduce | flops 16 | bytes 128 | tf_op jit(solution)/shard_map/psum | solution.py:45
  53.0 4.5 %collective-permute-start.4 = (f32[16,512]{1,0:T(8,128)S(1)}, f32[16,512]{1,0:T(8,128)S(1)}, u32[]{:S(2)}, u32[]{:S(2)}) collective-permute-start(f32[16,512]{1,0:T(8,128)S(1)} %copy.123), channel_id=1, source_target_pairs={{0,1},{1,2},{2,3},{3,4},{4,5},{5,6},{6,7},{8,9},{9,10},{10,11},{11... | collective-permute-start | bytes 98312 | tf_op jit(solution)/shard_map/ppermute | solution.py:21
  77.5 4.5 %collective-permute-start.10 = (bf16[1,1,1,16,512]{4,3,2,1,0:T(8,128)(2,1)S(1)}, bf16[1,1,1,16,512]{4,3,2,1,0:T(8,128)(2,1)S(1)}, u32[]{:S(2)}, u32[]{:S(2)}) collective-permute-start(bf16[1,1,1,16,512]{4,3,2,1,0:T(8,128)(2,1)S(1)} %get-tuple-element.71), channel_id=1, source_target_pairs={{0,1},{1,2},{2,3},{3,4},{4,5},{5,6},{6,7},{8,9},{9,10},{10,11},{11... | collective-permute-start | bytes 49160 | tf_op jit(solution)/shard_map/ppermute | solution.py:32
  97.5 4.6 %fusion.4 = f32[16,2048]{1,0:T(8,128)S(1)} fusion(bf16[16,2048]{1,0:T(8,128)(2,1)S(1)} %constant_dynamic-update-slice_fusion, bf16[1,1,1,2048,2048]{4,3,2,1,0:T(8,128)(2,1)} %param.7), kind=kOutput, calls=%fused_computation.58 | convolution fusion | flops 134217728 | bytes 8585216 | tf_op jit(solution)/shard_map/dot_general | solution.py:140
  110.4 4.5 %collective-permute-start.16 = (f32[16,512]{1,0:T(8,128)S(1)}, f32[16,512]{1,0:T(8,128)S(1)}, u32[]{:S(2)}, u32[]{:S(2)}) collective-permute-start(f32[16,512]{1,0:T(8,128)S(1)} %copy.147), channel_id=1, source_target_pairs={{0,1},{1,2},{2,3},{3,4},{4,5},{5,6},{6,7},{8,9},{9,10},{10,11},{11... | collective-permute-start | bytes 98312 | tf_op jit(solution)/shard_map/ppermute | solution.py:21
  130.5 9.7 %all-reduce.8 = (f32[1,16]{1,0:T(1,128)S(1)}, f32[1,16]{1,0:T(1,128)S(1)}, f32[16]{0:T(128)S(1)}) all-reduce(f32[1,16]{1,0:T(1,128)S(1)} %bitcast.449, f32[1,16]{1,0:T(1,128)S(1)} %bitcast.448, f32[16]{0:T(128)S(1)} %get-tuple-element.11), channel_id=1, replica_groups=mesh['gx'=4,'gy_0'=4,'gy_1'=2,'gz'=8] {'gx'}, use_global_device_ids=true, to_apply=%region_18.20 | all-reduce | flops 48 | bytes 384 | tf_op jit(solution)/shard_map/psum | solution.py:45
  140.1 9.9 %all-reduce.5 = (f32[1,16]{1,0:T(1,128)S(1)}, f32[1,16]{1,0:T(1,128)S(1)}, f32[16]{0:T(128)S(1)}) all-reduce(f32[1,16]{1,0:T(1,128)S(1)} %get-tuple-element.42, f32[1,16]{1,0:T(1,128)S(1)} %get-tuple-element.43, f32[16]{0:T(128)S(1)} %get-tuple-element.44), channel_id=1, replica_groups=mesh['gx'=4,'gy_0'=4,'gy_1'=2,'gz'=8] {'gy_0'}, use_global_device_ids=true, to_apply=%region_19.21 | all-reduce | flops 48 | bytes 384 | tf_op jit(solution)/shard_map/psum | solution.py:45
  152.5 16.4 %all-reduce.2 = (f32[16]{0:T(128)S(1)}, f32[16]{0:T(128)S(1)}, f32[16]{0:T(128)S(1)}) all-reduce(f32[16]{0:T(128)S(1)} %bitcast.450, f32[16]{0:T(128)S(1)} %bitcast.451, f32[16]{0:T(128)S(1)} %get-tuple-element.53), channel_id=1, replica_groups=mesh['gx'=4,'gy_0'=4,'gy_1'=2,'gz'=8] {'gz'}, use_global_device_ids=true, to_apply=%region_21.23 | all-reduce | flops 48 | bytes 384 | tf_op jit(solution)/shard_map/psum | solution.py:45
  177.9 4.5 %collective-permute-start.22 = (f32[16,512]{1,0:T(8,128)S(1)}, f32[16,512]{1,0:T(8,128)S(1)}, u32[]{:S(2)}, u32[]{:S(2)}) collective-permute-start(f32[16,512]{1,0:T(8,128)S(1)} %copy.159), channel_id=1, source_target_pairs={{0,1},{1,2},{2,3},{3,4},{4,5},{5,6},{6,7},{8,9},{9,10},{10,11},{11... | collective-permute-start | bytes 98312 | tf_op jit(solution)/shard_map/ppermute | solution.py:21
  202.3 4.5 %collective-permute-start.28 = (bf16[1,1,1,16,512]{4,3,2,1,0:T(8,128)(2,1)S(1)}, bf16[1,1,1,16,512]{4,3,2,1,0:T(8,128)(2,1)S(1)}, u32[]{:S(2)}, u32[]{:S(2)}) collective-permute-start(bf16[1,1,1,16,512]{4,3,2,1,0:T(8,128)(2,1)S(1)} %get-tuple-element.68), channel_id=1, source_target_pairs={{0,1},{1,2},{2,3},{3,4},{4,5},{5,6},{6,7},{8,9},{9,10},{10,11},{11... | collective-permute-start | bytes 49160 | tf_op jit(solution)/shard_map/ppermute | solution.py:32
  222.2 4.6 %fusion.2 = f32[16,2048]{1,0:T(8,128)S(1)} fusion(bf16[16,2048]{1,0:T(8,128)(2,1)S(1)} %constant_dynamic-update-slice_fusion.7, bf16[1,1,1,2048,2048]{4,3,2,1,0:T(8,128)(2,1)} %param.7), kind=kOutput, calls=%fused_computation.56 | convolution fusion | flops 134217728 | bytes 8585216 | tf_op jit(solution)/shard_map/dot_general | solution.py:140
  235.4 4.5 %collective-permute-start.34 = (f32[16,512]{1,0:T(8,128)S(1)}, f32[16,512]{1,0:T(8,128)S(1)}, u32[]{:S(2)}, u32[]{:S(2)}) collective-permute-start(f32[16,512]{1,0:T(8,128)S(1)} %copy.183), channel_id=1, source_target_pairs={{0,1},{1,2},{2,3},{3,4},{4,5},{5,6},{6,7},{8,9},{9,10},{10,11},{11... | collective-permute-start | bytes 98312 | tf_op jit(solution)/shard_map/ppermute | solution.py:21
  255.4 9.7 %all-reduce.7 = (f32[16]{0:T(128)S(1)}, f32[2,16]{1,0:T(2,128)S(1)}, f32[2,16]{1,0:T(2,128)S(1)}) all-reduce(f32[16]{0:T(128)S(1)} %get-tuple-element.17, f32[2,16]{1,0:T(2,128)S(1)} %get-tuple-element.124, f32[2,16]{1,0:T(2,128)S(1)} %get-tuple-element.123), channel_id=1, replica_groups=mesh['gx'=4,'gy_0'=4,'gy_1'=2,'gz'=8] {'gx'}, use_global_device_ids=true, to_apply=%region_51.53 | all-reduce | flops 80 | bytes 640 | tf_op jit(solution)/shard_map/psum | solution.py:45
  265.1 7.7 %all-reduce.4 = (f32[16]{0:T(128)S(1)}, f32[2,16]{1,0:T(2,128)S(1)}, f32[2,16]{1,0:T(2,128)S(1)}) all-reduce(f32[16]{0:T(128)S(1)} %get-tuple-element.39, f32[2,16]{1,0:T(2,128)S(1)} %get-tuple-element.40, f32[2,16]{1,0:T(2,128)S(1)} %get-tuple-element.41), channel_id=1, replica_groups=mesh['gx'=4,'gy_0'=4,'gy_1'=2,'gz'=8] {'gy_0'}, use_global_device_ids=true, to_apply=%region_52.54 | all-reduce | flops 80 | bytes 640 | tf_op jit(solution)/shard_map/psum | solution.py:45
  275.3 17.8 %all-reduce.1 = (f32[16]{0:T(128)S(1)}, f32[2,16]{1,0:T(2,128)S(1)}, f32[2,16]{1,0:T(2,128)S(1)}) all-reduce(f32[16]{0:T(128)S(1)} %get-tuple-element.48, f32[2,16]{1,0:T(2,128)S(1)} %get-tuple-element.49, f32[2,16]{1,0:T(2,128)S(1)} %get-tuple-element.50), channel_id=1, replica_groups=mesh['gx'=4,'gy_0'=4,'gy_1'=2,'gz'=8] {'gz'}, use_global_device_ids=true, to_apply=%region_54.56 | all-reduce | flops 80 | bytes 640 | tf_op jit(solution)/shard_map/psum | solution.py:45
  301.9 4.5 %collective-permute-start.40 = (f32[16,512]{1,0:T(8,128)S(1)}, f32[16,512]{1,0:T(8,128)S(1)}, u32[]{:S(2)}, u32[]{:S(2)}) collective-permute-start(f32[16,512]{1,0:T(8,128)S(1)} %copy.195), channel_id=1, source_target_pairs={{0,1},{1,2},{2,3},{3,4},{4,5},{5,6},{6,7},{8,9},{9,10},{10,11},{11... | collective-permute-start | bytes 98312 | tf_op jit(solution)/shard_map/ppermute | solution.py:21
  326.6 4.3 %collective-permute-start.46 = (bf16[1,1,1,16,512]{4,3,2,1,0:T(8,128)(2,1)S(1)}, bf16[1,1,1,16,512]{4,3,2,1,0:T(8,128)(2,1)S(1)}, u32[]{:S(2)}, u32[]{:S(2)}) collective-permute-start(bf16[1,1,1,16,512]{4,3,2,1,0:T(8,128)(2,1)S(1)} %get-tuple-element.65), channel_id=1, source_target_pairs={{0,1},{1,2},{2,3},{3,4},{4,5},{5,6},{6,7},{8,9},{9,10},{10,11},{11... | collective-permute-start | bytes 49160 | tf_op jit(solution)/shard_map/ppermute | solution.py:32
  346.3 4.6 %fusion = f32[16,2048]{1,0:T(8,128)S(1)} fusion(bf16[16,2048]{1,0:T(8,128)(2,1)S(1)} %constant_dynamic-update-slice_fusion.14, bf16[1,1,1,2048,2048]{4,3,2,1,0:T(8,128)(2,1)} %param.7), kind=kOutput, calls=%fused_computation.54 | convolution fusion | flops 134217728 | bytes 8585216 | tf_op jit(solution)/shard_map/dot_general | solution.py:140
  359.2 4.5 %collective-permute-start.52 = (f32[16,512]{1,0:T(8,128)S(1)}, f32[16,512]{1,0:T(8,128)S(1)}, u32[]{:S(2)}, u32[]{:S(2)}) collective-permute-start(f32[16,512]{1,0:T(8,128)S(1)} %copy.219), channel_id=1, source_target_pairs={{0,1},{1,2},{2,3},{3,4},{4,5},{5,6},{6,7},{8,9},{9,10},{10,11},{11... | collective-permute-start | bytes 98312 | tf_op jit(solution)/shard_map/ppermute | solution.py:21
  379.3 9.8 %all-reduce.6 = (f32[3,16]{1,0:T(4,128)S(1)}, f32[3,16]{1,0:T(4,128)S(1)}, f32[16]{0:T(128)S(1)}) all-reduce(f32[3,16]{1,0:T(4,128)S(1)} %pad_maximum_fusion, f32[3,16]{1,0:T(4,128)S(1)} %pad_maximum_fusion.1, f32[16]{0:T(128)S(1)} %get-tuple-element.13), channel_id=1, replica_groups=mesh['gx'=4,'gy_0'=4,'gy_1'=2,'gz'=8] {'gx'}, use_global_device_ids=true, to_apply=%region_76.78 | all-reduce | flops 112 | bytes 896 | tf_op jit(solution)/shard_map/psum | solution.py:45
  389.1 9.8 %all-reduce.3 = (f32[3,16]{1,0:T(4,128)S(1)}, f32[3,16]{1,0:T(4,128)S(1)}, f32[16]{0:T(128)S(1)}) all-reduce(f32[3,16]{1,0:T(4,128)S(1)} %get-tuple-element.36, f32[3,16]{1,0:T(4,128)S(1)} %get-tuple-element.37, f32[16]{0:T(128)S(1)} %get-tuple-element.38), channel_id=1, replica_groups=mesh['gx'=4,'gy_0'=4,'gy_1'=2,'gz'=8] {'gy_0'}, use_global_device_ids=true, to_apply=%region_77.79 | all-reduce | flops 112 | bytes 896 | tf_op jit(solution)/shard_map/psum | solution.py:45
  401.4 18.0 %all-reduce = (f32[3,16]{1,0:T(4,128)S(1)}, f32[3,16]{1,0:T(4,128)S(1)}, f32[16]{0:T(128)S(1)}) all-reduce(f32[3,16]{1,0:T(4,128)S(1)} %get-tuple-element.45, f32[3,16]{1,0:T(4,128)S(1)} %get-tuple-element.46, f32[16]{0:T(128)S(1)} %get-tuple-element.47), channel_id=1, replica_groups=mesh['gx'=4,'gy_0'=4,'gy_1'=2,'gz'=8] {'gz'}, use_global_device_ids=true, to_apply=%region_79.81 | all-reduce | flops 112 | bytes 896 | tf_op jit(solution)/shard_map/psum | solution.py:45
  (338 shorter events, 218.0 us)
Async XLA Ops:
  45.1 22.8 %collective-permute-start = (f32[16,512]{1,0:T(8,128)S(1)}, f32[16,512]{1,0:T(8,128)S(1)}, u32[]{:S(2)}, u32[]{:S(2)}) collective-permute-start(f32[16,512]{1,0:T(8,128)S(1)} %copy.115), channel_id=1, source_target_pairs={{0,64},{64,128},{128,192},{1,65},{65,129},{129,193},{2,66},{66,130... | collective-permute-start | bytes 98312 | tf_op jit(solution)/shard_map/ppermute | solution.py:21
  50.0 20.6 %collective-permute-start.5 = (f32[16,512]{1,0:T(8,128)S(1)}, f32[16,512]{1,0:T(8,128)S(1)}, u32[]{:S(2)}, u32[]{:S(2)}) collective-permute-start(f32[16,512]{1,0:T(8,128)S(1)} %copy.125), channel_id=1, source_target_pairs={{1,0},{2,1},{3,2},{4,3},{5,4},{6,5},{7,6},{9,8},{10,9},{11,10},{12... | collective-permute-start | bytes 98312 | tf_op jit(solution)/shard_map/ppermute | solution.py:21
  53.0 17.6 %collective-permute-start.4 = (f32[16,512]{1,0:T(8,128)S(1)}, f32[16,512]{1,0:T(8,128)S(1)}, u32[]{:S(2)}, u32[]{:S(2)}) collective-permute-start(f32[16,512]{1,0:T(8,128)S(1)} %copy.123), channel_id=1, source_target_pairs={{0,1},{1,2},{2,3},{3,4},{4,5},{5,6},{6,7},{8,9},{9,10},{10,11},{11... | collective-permute-start | bytes 98312 | tf_op jit(solution)/shard_map/ppermute | solution.py:21
  76.2 20.1 %collective-permute-start.11 = (bf16[1,1,1,16,512]{4,3,2,1,0:T(8,128)(2,1)S(1)}, bf16[1,1,1,16,512]{4,3,2,1,0:T(8,128)(2,1)S(1)}, u32[]{:S(2)}, u32[]{:S(2)}) collective-permute-start(bf16[1,1,1,16,512]{4,3,2,1,0:T(8,128)(2,1)S(1)} %get-tuple-element.71), channel_id=1, source_target_pairs={{1,0},{2,1},{3,2},{4,3},{5,4},{6,5},{7,6},{9,8},{10,9},{11,10},{12... | collective-permute-start | bytes 49160 | tf_op jit(solution)/shard_map/ppermute | solution.py:33
  77.5 17.7 %collective-permute-start.10 = (bf16[1,1,1,16,512]{4,3,2,1,0:T(8,128)(2,1)S(1)}, bf16[1,1,1,16,512]{4,3,2,1,0:T(8,128)(2,1)S(1)}, u32[]{:S(2)}, u32[]{:S(2)}) collective-permute-start(bf16[1,1,1,16,512]{4,3,2,1,0:T(8,128)(2,1)S(1)} %get-tuple-element.71), channel_id=1, source_target_pairs={{0,1},{1,2},{2,3},{3,4},{4,5},{5,6},{6,7},{8,9},{9,10},{10,11},{11... | collective-permute-start | bytes 49160 | tf_op jit(solution)/shard_map/ppermute | solution.py:32
  103.8 20.6 %collective-permute-start.12 = (f32[16,512]{1,0:T(8,128)S(1)}, f32[16,512]{1,0:T(8,128)S(1)}, u32[]{:S(2)}, u32[]{:S(2)}) collective-permute-start(f32[16,512]{1,0:T(8,128)S(1)} %copy.139), channel_id=1, source_target_pairs={{0,64},{64,128},{128,192},{1,65},{65,129},{129,193},{2,66},{66,130... | collective-permute-start | bytes 98312 | tf_op jit(solution)/shard_map/ppermute | solution.py:21
  107.4 20.9 %collective-permute-start.17 = (f32[16,512]{1,0:T(8,128)S(1)}, f32[16,512]{1,0:T(8,128)S(1)}, u32[]{:S(2)}, u32[]{:S(2)}) collective-permute-start(f32[16,512]{1,0:T(8,128)S(1)} %copy.149), channel_id=1, source_target_pairs={{1,0},{2,1},{3,2},{4,3},{5,4},{6,5},{7,6},{9,8},{10,9},{11,10},{12... | collective-permute-start | bytes 98312 | tf_op jit(solution)/shard_map/ppermute | solution.py:21
  110.4 17.9 %collective-permute-start.16 = (f32[16,512]{1,0:T(8,128)S(1)}, f32[16,512]{1,0:T(8,128)S(1)}, u32[]{:S(2)}, u32[]{:S(2)}) collective-permute-start(f32[16,512]{1,0:T(8,128)S(1)} %copy.147), channel_id=1, source_target_pairs={{0,1},{1,2},{2,3},{3,4},{4,5},{5,6},{6,7},{8,9},{9,10},{10,11},{11... | collective-permute-start | bytes 98312 | tf_op jit(solution)/shard_map/ppermute | solution.py:21
  171.1 20.8 %collective-permute-start.18 = (f32[16,512]{1,0:T(8,128)S(1)}, f32[16,512]{1,0:T(8,128)S(1)}, u32[]{:S(2)}, u32[]{:S(2)}) collective-permute-start(f32[16,512]{1,0:T(8,128)S(1)} %copy.151), channel_id=1, source_target_pairs={{0,64},{64,128},{128,192},{1,65},{65,129},{129,193},{2,66},{66,130... | collective-permute-start | bytes 98312 | tf_op jit(solution)/shard_map/ppermute | solution.py:21
  174.9 20.9 %collective-permute-start.23 = (f32[16,512]{1,0:T(8,128)S(1)}, f32[16,512]{1,0:T(8,128)S(1)}, u32[]{:S(2)}, u32[]{:S(2)}) collective-permute-start(f32[16,512]{1,0:T(8,128)S(1)} %copy.161), channel_id=1, source_target_pairs={{1,0},{2,1},{3,2},{4,3},{5,4},{6,5},{7,6},{9,8},{10,9},{11,10},{12... | collective-permute-start | bytes 98312 | tf_op jit(solution)/shard_map/ppermute | solution.py:21
  177.9 17.9 %collective-permute-start.22 = (f32[16,512]{1,0:T(8,128)S(1)}, f32[16,512]{1,0:T(8,128)S(1)}, u32[]{:S(2)}, u32[]{:S(2)}) collective-permute-start(f32[16,512]{1,0:T(8,128)S(1)} %copy.159), channel_id=1, source_target_pairs={{0,1},{1,2},{2,3},{3,4},{4,5},{5,6},{6,7},{8,9},{9,10},{10,11},{11... | collective-permute-start | bytes 98312 | tf_op jit(solution)/shard_map/ppermute | solution.py:21
  201.0 20.1 %collective-permute-start.29 = (bf16[1,1,1,16,512]{4,3,2,1,0:T(8,128)(2,1)S(1)}, bf16[1,1,1,16,512]{4,3,2,1,0:T(8,128)(2,1)S(1)}, u32[]{:S(2)}, u32[]{:S(2)}) collective-permute-start(bf16[1,1,1,16,512]{4,3,2,1,0:T(8,128)(2,1)S(1)} %get-tuple-element.68), channel_id=1, source_target_pairs={{1,0},{2,1},{3,2},{4,3},{5,4},{6,5},{7,6},{9,8},{10,9},{11,10},{12... | collective-permute-start | bytes 49160 | tf_op jit(solution)/shard_map/ppermute | solution.py:33
  202.3 17.7 %collective-permute-start.28 = (bf16[1,1,1,16,512]{4,3,2,1,0:T(8,128)(2,1)S(1)}, bf16[1,1,1,16,512]{4,3,2,1,0:T(8,128)(2,1)S(1)}, u32[]{:S(2)}, u32[]{:S(2)}) collective-permute-start(bf16[1,1,1,16,512]{4,3,2,1,0:T(8,128)(2,1)S(1)} %get-tuple-element.68), channel_id=1, source_target_pairs={{0,1},{1,2},{2,3},{3,4},{4,5},{5,6},{6,7},{8,9},{9,10},{10,11},{11... | collective-permute-start | bytes 49160 | tf_op jit(solution)/shard_map/ppermute | solution.py:32
  228.5 20.8 %collective-permute-start.30 = (f32[16,512]{1,0:T(8,128)S(1)}, f32[16,512]{1,0:T(8,128)S(1)}, u32[]{:S(2)}, u32[]{:S(2)}) collective-permute-start(f32[16,512]{1,0:T(8,128)S(1)} %copy.175), channel_id=1, source_target_pairs={{0,64},{64,128},{128,192},{1,65},{65,129},{129,193},{2,66},{66,130... | collective-permute-start | bytes 98312 | tf_op jit(solution)/shard_map/ppermute | solution.py:21
  232.2 21.1 %collective-permute-start.35 = (f32[16,512]{1,0:T(8,128)S(1)}, f32[16,512]{1,0:T(8,128)S(1)}, u32[]{:S(2)}, u32[]{:S(2)}) collective-permute-start(f32[16,512]{1,0:T(8,128)S(1)} %copy.185), channel_id=1, source_target_pairs={{1,0},{2,1},{3,2},{4,3},{5,4},{6,5},{7,6},{9,8},{10,9},{11,10},{12... | collective-permute-start | bytes 98312 | tf_op jit(solution)/shard_map/ppermute | solution.py:21
  235.4 17.9 %collective-permute-start.34 = (f32[16,512]{1,0:T(8,128)S(1)}, f32[16,512]{1,0:T(8,128)S(1)}, u32[]{:S(2)}, u32[]{:S(2)}) collective-permute-start(f32[16,512]{1,0:T(8,128)S(1)} %copy.183), channel_id=1, source_target_pairs={{0,1},{1,2},{2,3},{3,4},{4,5},{5,6},{6,7},{8,9},{9,10},{10,11},{11... | collective-permute-start | bytes 98312 | tf_op jit(solution)/shard_map/ppermute | solution.py:21
  295.3 20.6 %collective-permute-start.36 = (f32[16,512]{1,0:T(8,128)S(1)}, f32[16,512]{1,0:T(8,128)S(1)}, u32[]{:S(2)}, u32[]{:S(2)}) collective-permute-start(f32[16,512]{1,0:T(8,128)S(1)} %copy.187), channel_id=1, source_target_pairs={{0,64},{64,128},{128,192},{1,65},{65,129},{129,193},{2,66},{66,130... | collective-permute-start | bytes 98312 | tf_op jit(solution)/shard_map/ppermute | solution.py:21
  298.9 20.9 %collective-permute-start.41 = (f32[16,512]{1,0:T(8,128)S(1)}, f32[16,512]{1,0:T(8,128)S(1)}, u32[]{:S(2)}, u32[]{:S(2)}) collective-permute-start(f32[16,512]{1,0:T(8,128)S(1)} %copy.197), channel_id=1, source_target_pairs={{1,0},{2,1},{3,2},{4,3},{5,4},{6,5},{7,6},{9,8},{10,9},{11,10},{12... | collective-permute-start | bytes 98312 | tf_op jit(solution)/shard_map/ppermute | solution.py:21
  301.9 17.9 %collective-permute-start.40 = (f32[16,512]{1,0:T(8,128)S(1)}, f32[16,512]{1,0:T(8,128)S(1)}, u32[]{:S(2)}, u32[]{:S(2)}) collective-permute-start(f32[16,512]{1,0:T(8,128)S(1)} %copy.195), channel_id=1, source_target_pairs={{0,1},{1,2},{2,3},{3,4},{4,5},{5,6},{6,7},{8,9},{9,10},{10,11},{11... | collective-permute-start | bytes 98312 | tf_op jit(solution)/shard_map/ppermute | solution.py:21
  325.0 20.1 %collective-permute-start.47 = (bf16[1,1,1,16,512]{4,3,2,1,0:T(8,128)(2,1)S(1)}, bf16[1,1,1,16,512]{4,3,2,1,0:T(8,128)(2,1)S(1)}, u32[]{:S(2)}, u32[]{:S(2)}) collective-permute-start(bf16[1,1,1,16,512]{4,3,2,1,0:T(8,128)(2,1)S(1)} %get-tuple-element.65), channel_id=1, source_target_pairs={{1,0},{2,1},{3,2},{4,3},{5,4},{6,5},{7,6},{9,8},{10,9},{11,10},{12... | collective-permute-start | bytes 49160 | tf_op jit(solution)/shard_map/ppermute | solution.py:33
  326.6 17.5 %collective-permute-start.46 = (bf16[1,1,1,16,512]{4,3,2,1,0:T(8,128)(2,1)S(1)}, bf16[1,1,1,16,512]{4,3,2,1,0:T(8,128)(2,1)S(1)}, u32[]{:S(2)}, u32[]{:S(2)}) collective-permute-start(bf16[1,1,1,16,512]{4,3,2,1,0:T(8,128)(2,1)S(1)} %get-tuple-element.65), channel_id=1, source_target_pairs={{0,1},{1,2},{2,3},{3,4},{4,5},{5,6},{6,7},{8,9},{9,10},{10,11},{11... | collective-permute-start | bytes 49160 | tf_op jit(solution)/shard_map/ppermute | solution.py:32
  352.6 20.6 %collective-permute-start.48 = (f32[16,512]{1,0:T(8,128)S(1)}, f32[16,512]{1,0:T(8,128)S(1)}, u32[]{:S(2)}, u32[]{:S(2)}) collective-permute-start(f32[16,512]{1,0:T(8,128)S(1)} %copy.211), channel_id=1, source_target_pairs={{0,64},{64,128},{128,192},{1,65},{65,129},{129,193},{2,66},{66,130... | collective-permute-start | bytes 98312 | tf_op jit(solution)/shard_map/ppermute | solution.py:21
  356.2 20.9 %collective-permute-start.53 = (f32[16,512]{1,0:T(8,128)S(1)}, f32[16,512]{1,0:T(8,128)S(1)}, u32[]{:S(2)}, u32[]{:S(2)}) collective-permute-start(f32[16,512]{1,0:T(8,128)S(1)} %copy.221), channel_id=1, source_target_pairs={{1,0},{2,1},{3,2},{4,3},{5,4},{6,5},{7,6},{9,8},{10,9},{11,10},{12... | collective-permute-start | bytes 98312 | tf_op jit(solution)/shard_map/ppermute | solution.py:21
  359.2 17.9 %collective-permute-start.52 = (f32[16,512]{1,0:T(8,128)S(1)}, f32[16,512]{1,0:T(8,128)S(1)}, u32[]{:S(2)}, u32[]{:S(2)}) collective-permute-start(f32[16,512]{1,0:T(8,128)S(1)} %copy.219), channel_id=1, source_target_pairs={{0,1},{1,2},{2,3},{3,4},{4,5},{5,6},{6,7},{8,9},{9,10},{10,11},{11... | collective-permute-start | bytes 98312 | tf_op jit(solution)/shard_map/ppermute | solution.py:21
  (32 other events, 346.8 us)
where the time goes:
time: 429 us; the launch traced here: 421 us
  blocking collectives  156 us (36%)
  starting transfers between devices  145 us (34%)
  other arithmetic  57.9 us (13%)
  local copies, waits for them, and re-layouts  26.8 us (6%)
  waiting for transfers between devices  17.3 us (4%)
  matrix products  15.7 us (4%)
    psum x16, blocking collectives, one_axis_at_a_time(): return functools.reduce(lax.psum, axes, array)  156 us
    ppermute x36, starting transfers between devices, from_behind(): return lax.ppermute(array, axis, pairs)  96.4 us
    scatter-add x36, other arithmetic, assemble(): jnp.zeros_like(result).at[:, owned_maps[facing]].add(face_blocks[facing])  53.5 us
    ppermute x9, starting transfers between devices, padded(): lax.ppermute(last, axis, up)  29.5 us
    ppermute x9, starting transfers between devices, padded(): lax.ppermute(initial, axis, [(b, a) for a, b in up])  19 us
    gather x36, local copies, waits for them, and re-layouts, gather_local(): jnp.take(ghost_layer[FACE_SPOTS[facing]], owned_maps[facing], axis=1)  16.6 us
    dot_general x3, matrix products, local(): jnp.dot(intersected, schur_block, preferred_element_type=jnp.float32)  13.7 us
    ppermute x36, waiting for transfers between devices, from_behind(): return lax.ppermute(array, axis, pairs)  12.6 us
  transfers between devices with their start and end apart: 54, of which 9 were waited for; matrix products, arithmetic and copies ran while one was open for 16% of the time, Pallas kernels for 0%

commit v1 on v0

v1 whole, which is shorter than its diff:
```python
import functools

import jax
import jax.numpy as jnp
from jax import lax
from jax.experimental import pallas as pl
from jax.experimental.pallas import tpu as pltpu
from jax.sharding import PartitionSpec as P

ITERS = 3
EPSILON = 1e-06
SCALE = 2.0**-12
AXES = ("gx", "gy", "gz")
BF16 = jnp.bfloat16
F32 = jnp.float32
VMEM = pltpu.VMEM


def ring(array, axis, by):
    n = lax.axis_size(axis)
    return lax.ppermute(array, axis, [(i, (i + by) % n) for i in range(n)])


def sends(face_sums):
    got = [None] * 6
    for dim in (1, 2, 0):
        got[2 * dim + 1] = ring(face_sums[2 * dim], AXES[dim], -1)
        got[2 * dim] = ring(face_sums[2 * dim + 1], AXES[dim], 1)
    return got


def split(x):
    high = x.astype(BF16)
    low = (x - high.astype(F32)).astype(BF16)
    return jnp.concatenate([high, low], axis=0)


def joined(x):
    rows = x.shape[0] // 2
    return x[:rows] + x[rows:]


def put_faces(products, picks, own_ref, face_refs):
    width = picks.shape[2]
    owned = picks.shape[1]
    own_ref[...] = products[:, :owned]
    for face in range(6):
        block = products[:, owned + face * width : owned + (face + 1) * width]
        face_refs[face][...] = joined(
            lax.dot_general(
                split(block),
                picks[face],
                (((1,), (1,)), ((), ())),
                preferred_element_type=F32,
            )
        )


def first_kernel(vector_ref, maps_ref, restricted_ref, picks_ref, own_ref, *face_refs):
    owned = vector_ref.shape[1]
    width = maps_ref.shape[1]
    place = lax.broadcasted_iota(jnp.int32, (owned, width), 0)
    for face in range(6):
        chosen = maps_ref[face : face + 1, :] == place
        picks_ref[face] = jnp.where(chosen, 1.0, 0.0).astype(BF16)
    products = joined(
        jnp.dot(split(vector_ref[...]), restricted_ref[...], preferred_element_type=F32)
    )
    put_faces(products, picks_ref, own_ref, face_refs)


def operator_kernel(*refs):
    vector_ref, got, (picks_ref, schur_ref, own_ref), face_refs = (
        refs[0],
        refs[1:7],
        refs[7:10],
        refs[10:],
    )
    parts = [split(vector_ref[...])]
    for face in range(6):
        parts.append(
            jnp.dot(split(got[face][...]), picks_ref[face], preferred_element_type=F32).astype(BF16)
        )
    products = joined(
        jnp.dot(jnp.concatenate(parts, axis=1), schur_ref[...], preferred_element_type=F32)
    )
    put_faces(products, picks_ref, own_ref, face_refs)


def gram_entries(basis):
    rows = basis[0].shape[0]
    lane = lax.broadcasted_iota(jnp.int32, (rows, 128), 1)
    total = jnp.zeros((rows, 128), F32)
    newest = len(basis) - 1
    for i, vector in enumerate(basis):
        value = jnp.sum(vector * basis[newest], axis=1, keepdims=True)
        total = total + jnp.where(lane == i * 4 + newest, value, 0.0)
    return total


def summed(own_ref, got):
    total = own_ref[...]
    for part in got:
        total = total + part[...]
    return total


def next_kernel(count, *refs):
    own, got, rest = refs[0], refs[1:7], refs[7:]
    older, rest = rest[:count], rest[count:]
    picks_ref, restricted_ref, vector_ref, own_ref = rest[:4]
    face_refs = rest[4:]
    vector = summed(own, got) * SCALE
    vector_ref[...] = vector
    products = joined(jnp.dot(split(vector), restricted_ref[...], preferred_element_type=F32))
    put_faces(products, picks_ref, own_ref, face_refs)


def gram_kernel(*refs):
    own, got = refs[0], refs[1:7]
    older, gram_ref = refs[7:-1], refs[-1]
    basis = [ref[...] for ref in older] + [summed(own, got) * SCALE]
    total = gram_entries(basis[:1])
    for newest in range(1, len(basis)):
        total = total + gram_entries(basis[: newest + 1])
    gram_ref[...] = total


def rotate_solve(columns, beta_norm):
    num_cols = len(columns)
    rhs_vec = [beta_norm] + [jnp.zeros_like(beta_norm) for unused in range(num_cols)]
    cosines = []
    sines = []
    triangle = []
    for section in range(num_cols):
        column = [columns[section][row_at] for row_at in range(section + 2)]
        for earlier in range(section):
            rotated_a = cosines[earlier] * column[earlier] + sines[earlier] * column[earlier + 1]
            rotated_b = -sines[earlier] * column[earlier] + cosines[earlier] * column[earlier + 1]
            column[earlier] = rotated_a
            column[earlier + 1] = rotated_b
        radius = jnp.sqrt(
            column[section] * column[section] + column[section + 1] * column[section + 1]
        )
        cosine = column[section] / radius
        sine_val = column[section + 1] / radius
        column[section] = radius
        cosines.append(cosine)
        sines.append(sine_val)
        rhs_vec[section + 1] = -sine_val * rhs_vec[section]
        rhs_vec[section] = cosine * rhs_vec[section]
        triangle.append(column[: section + 1])
    coeffs = [None] * num_cols
    for section in reversed(range(num_cols)):
        running = rhs_vec[section]
        for onward in range(section + 1, num_cols):
            running = running - triangle[onward][section] * coeffs[onward]
        coeffs[section] = running / triangle[section][section]
    return (coeffs, jnp.abs(rhs_vec[num_cols]))


def combine(gram):
    beta = jnp.sqrt(gram(0, 0) + EPSILON)
    made_of = [[1.0 / beta]]
    columns = []
    for k in range(ITERS):
        applied = [None] + [c * (1.0 / SCALE) for c in made_of[k]]
        against = [
            functools.reduce(
                jnp.add, [gram(a, b) * applied[b] for b in range(1, k + 2)]
            )
            for a in range(k + 1)
        ]
        heights = [
            functools.reduce(jnp.add, [made_of[j][a] * against[a] for a in range(j + 1)])
            for j in range(k + 1)
        ]
        rest = [jnp.zeros_like(beta)] + applied[1:]
        for j in range(k + 1):
            for a in range(j + 1):
                rest[a] = rest[a] - heights[j] * made_of[j][a]
        square = jnp.zeros_like(beta)
        for a in range(k + 2):
            square = square + rest[a] * functools.reduce(
                jnp.add, [gram(a, b) * rest[b] for b in range(k + 2)]
            )
        height = jnp.sqrt(jnp.maximum(square, 0.0) + EPSILON)
        columns.append(heights + [height])
        made_of.append([r / height for r in rest])
    weights, remainder = rotate_solve(columns, beta)
    shares = [
        functools.reduce(jnp.add, [weights[k] * made_of[k][i] for k in range(i, ITERS)])
        for i in range(ITERS)
    ]
    return shares, remainder / beta


def last_kernel(*refs):
    gram_ref, directions = refs[0], refs[1:-2]
    adjoint_ref, ratio_ref = refs[-2:]
    sums = gram_ref[...]

    def gram(a, b):
        at = min(a, b) * 4 + max(a, b)
        return sums[:, at : at + 1]

    shares, ratio = combine(gram)
    total = shares[0] * directions[0][...]
    for i in range(1, ITERS):
        total = total + shares[i] * directions[i][...]
    adjoint_ref[...] = total
    ratio_ref[...] = jnp.broadcast_to(ratio, ratio_ref.shape)


def call(kernel, operands, outputs, name, flops=0, limit=16 << 20):
    bytes_moved = sum(x.size * x.dtype.itemsize for x in operands)
    return pl.pallas_call(
        kernel,
        out_shape=tuple(VMEM(shape, dtype) for shape, dtype in outputs),
        in_specs=[pl.BlockSpec(memory_space=VMEM)] * len(operands),
        out_specs=tuple(pl.BlockSpec(memory_space=VMEM) for _ in outputs),
        compiler_params=pltpu.CompilerParams(vmem_limit_bytes=limit),
        cost_estimate=pl.CostEstimate(flops=flops, bytes_accessed=bytes_moved, transcendentals=0),
        name=name,
    )(*[pltpu.with_memory_space_constraint(x, VMEM) for x in operands])


def all_sum(array, stages):
    for axis in stages:
        n = lax.axis_size(axis)
        spread = jnp.broadcast_to(array[None], (n,) + array.shape)
        array = jnp.sum(lax.all_to_all(spread, axis, 0, 0), axis=0)
    return array


def local(gradient, local_schur, inverse_rows, face_maps):
    vector = gradient[0, 0, 0]
    schur = local_schur[0, 0, 0]
    restricted = inverse_rows[0, 0, 0]
    rows, owned = vector.shape
    width = face_maps.shape[-1]
    exists = []
    for axis in AXES:
        at = lax.axis_index(axis)
        exists += [at > 0, at < lax.axis_size(axis) - 1]
    maps = jnp.where(jnp.stack(exists)[:, None], face_maps[0, 0, 0], -1)

    block = ((rows, owned), F32)
    picks, own, *faces = call(
        first_kernel,
        (vector, maps, restricted),
        (((6, owned, width), BF16),) + (block,) * 7,
        "first",
    )
    basis = [vector]
    directions = []
    for section in range(ITERS):
        got = sends(faces)
        direction = own
        for part in got:
            direction = direction + part
        directions.append(direction)
        got = sends([direction] * 6)
        own, *faces = call(
            operator_kernel, (direction, *got, picks, schur), (block,) * 7, "operator"
        )
        got = sends(faces)
        if section + 1 < ITERS:
            vector, own, *faces = call(
                functools.partial(next_kernel, 0),
                (own, *got, picks, restricted),
                (block,) * 8,
                "next",
            )
            basis.append(vector)
    (gram,) = call(gram_kernel, (own, *got, *basis), (((rows, 128), F32),), "gram")
    gram = all_sum(gram, (("gx", "gy"), "gz"))
    adjoint, ratio = call(
        last_kernel, (gram, *directions), (block, ((rows, 128), F32)), "last"
    )
    return (adjoint[None, None, None], ratio[:, 0])


def solution(mesh):
    placed = P("gx", "gy", "gz", None, None)
    return jax.shard_map(
        local,
        mesh=mesh,
        in_specs=(placed,) * 4,
        out_specs=(placed, P()),
        check_vma=False,
    )
```

time: 429 us -> 148 us (0.34); the launches traced: 421 us -> 146 us
  blocking collectives: 156 us -> 31.2 us
  starting transfers between devices: 145 us -> 70.4 us
  other arithmetic: 57.9 us -> 0.86 us
  local copies, waits for them, and re-layouts: 26.8 us -> 7.11 us
  matrix products: 15.7 us -> 0 us
  Pallas kernels: 0 us -> 10.9 us
  waiting for transfers between devices: 17.3 us -> 25.1 us
    psum x16 -> x0, blocking collectives: 156 us -> none  [one_axis_at_a_time(): return functools.reduce(lax.psum, axes, array)]
    ppermute x54, starting transfers between devices: 145 us -> 70.4 us  [ring(): return lax.ppermute(array, axis, [(i, (i + by) % n) for i in range(n)])]
    scatter-add x36 -> x0, other arithmetic: 53.5 us -> none  [assemble(): jnp.zeros_like(result).at[:, owned_maps[facing]].add(face_blocks[facing])]
    all_to_all x0 -> x2, blocking collectives: none -> 31.2 us  [all_sum(): array = jnp.sum(lax.all_to_all(spread, axis, 0, 0), axis=0)]
    gather x36 -> x0, local copies, waits for them, and re-layouts: 16.6 us -> none  [gather_local(): jnp.take(ghost_layer[FACE_SPOTS[facing]], owned_maps[facing], axis=1)]
    dot_general x6 -> x0, matrix products: 15.7 us -> none  [the longest x3 13.7 us: local(): jnp.dot(intersected, schur_block, preferred_element_type=jnp.float32)]
    pallas_call x0 -> x8, Pallas kernels: none -> 10.9 us  [call(): pl.pallas_call(kernel, out_shape=tuple((VMEM(shape, dtype) for shape, dty...]
    ppermute x54, waiting for transfers between devices: 17.3 us -> 25.1 us  [ring(): return lax.ppermute(array, axis, [(i, (i + by) % n) for i in range(n)])]
  transfers between devices with their start and end apart: 54 -> 54, of which waited for: 9 -> 18; matrix products, arithmetic and copies ran while one was open for 16% -> 0% of each run, Pallas kernels for 0% -> 0%
where the time goes in v1:
time: 148 us; the launch traced here: 146 us
  starting transfers between devices  70.4 us (48%)
  blocking collectives  31.2 us (21%)
  waiting for transfers between devices  25.1 us (17%)
  Pallas kernels  10.9 us (7%)
  local copies, waits for them, and re-layouts  7.11 us (5%)
    ppermute x54, starting transfers between devices, ring(): return lax.ppermute(array, axis, [(i, (i + by) % n) for i in range(n)])  70.4 us
    all_to_all x2, blocking collectives, all_sum(): array = jnp.sum(lax.all_to_all(spread, axis, 0, 0), axis=0)  31.2 us
    ppermute x54, waiting for transfers between devices, ring(): return lax.ppermute(array, axis, [(i, (i + by) % n) for i in range(n)])  25.1 us
    pallas_call x8, Pallas kernels, call(): pl.pallas_call(kernel, out_shape=tuple((VMEM(shape, dtype) for shape, dty...  10.9 us
    unnamed x11, local copies, waits for them, and re-layouts  6.35 us
  transfers between devices with their start and end apart: 54, of which 18 were waited for; matrix products, arithmetic and copies ran while one was open for 0% of the time, Pallas kernels for 0%

profile of v1, /device:TPU:10, one launch (start us, length us, event | category | flops | bytes accessed | tf_op | source)
XLA Modules:
  0.0 146.3 jit_solution(4995262639321437131)
XLA Ops:
  10.7 4.1 %collective-permute-start.5 = (f32[16,512]{1,0:T(8,128)S(1)}, f32[16,512]{1,0:T(8,128)S(1)}, u32[]{:S(2)}, u32[]{:S(2)}) collective-permute-start(f32[16,512]{1,0:T(8,128)S(1)} %get-tuple-element.55), channel_id=1, source_target_pairs={{0,7},{1,0},{2,1},{3,2},{4,3},{5,4},{6,5},{7,6},{8,15},{9,8},{10,9... | collective-permute-start | bytes 98312 | tf_op jit(solution)/shard_map/ppermute | solution.py:21
  16.6 3.4 %collective-permute-start.11 = (f32[16,512]{1,0:T(8,128)S(1)}, f32[16,512]{1,0:T(8,128)S(1)}, u32[]{:S(2)}, u32[]{:S(2)}) collective-permute-start(f32[16,512]{1,0:T(8,128)S(1)} %add_add_fusion.2.refs_0_.refs_1_), channel_id=1, source_target_pairs={{0,7},{1,0},{2,1},{3,2},{4,3},{5,4},{6,5},{7,6},{8,15},{9,8},{10,9... | collective-permute-start | bytes 98312 | tf_op jit(solution)/shard_map/ppermute | solution.py:21
  23.2 1.9 %collective-permute-done.10.refs_5_ = f32[16,512]{1,0:T(8,128)S(1)} collective-permute-done((f32[16,512]{1,0:T(8,128)S(1)}, f32[16,512]{1,0:T(8,128)S(1)}, u32[]{:S(2)}, u32[]{:S(2)}) %collective-permute-start.10) | collective-permute-done | bytes 32800 | tf_op jit(solution)/shard_map/ppermute | solution.py:21
  26.4 3.4 %copy-done = bf16[1,1,1,2048,2048]{4,3,2,1,0:T(8,128)(2,1)S(1)} copy-done((bf16[1,1,1,2048,2048]{4,3,2,1,0:T(8,128)(2,1)S(1)}, bf16[1,1,1,2048,2048]{4,3,2,1,0:T(8,128)(2,1)}, u32[]{:S(2)}) %copy-start) | copy-done | bytes 8388632
  29.8 2.2 %operator.3 = (f32[16,512]{1,0:T(8,128)S(1)}, f32[16,512]{1,0:T(8,128)S(1)}, f32[16,512]{1,0:T(8,128)S(1)}, f32[16,512]{1,0:T(8,128)S(1)}, f32[16,512]{1,0:T(8,1...) custom-call(f32[16,512]{1,0:T(8,128)S(1)} %add_add_fusion.2.refs_0_.refs_1_, ...), custom_call_target="tpu_custom_call" | custom-call | bytes 10190848 | tf_op jit(solution)/shard_map/operator/pallas_call | solution.py:217
  32.7 2.3 %collective-permute-start.13 = (f32[16,512]{1,0:T(8,128)S(1)}, f32[16,512]{1,0:T(8,128)S(1)}, u32[]{:S(2)}, u32[]{:S(2)}) collective-permute-start(f32[16,512]{1,0:T(8,128)S(1)} %get-tuple-element.59), channel_id=1, source_target_pairs={{0,192},{64,0},{128,64},{192,128},{1,193},{65,1},{129,65},{193,129... | collective-permute-start | bytes 98312 | tf_op jit(solution)/shard_map/ppermute | solution.py:21
  36.8 3.2 %collective-permute-start.17 = (f32[16,512]{1,0:T(8,128)S(1)}, f32[16,512]{1,0:T(8,128)S(1)}, u32[]{:S(2)}, u32[]{:S(2)}) collective-permute-start(f32[16,512]{1,0:T(8,128)S(1)} %get-tuple-element.63), channel_id=1, source_target_pairs={{0,7},{1,0},{2,1},{3,2},{4,3},{5,4},{6,5},{7,6},{8,15},{9,8},{10,9... | collective-permute-start | bytes 98312 | tf_op jit(solution)/shard_map/ppermute | solution.py:21
  42.8 3.2 %collective-permute-start.19 = (f32[16,512]{1,0:T(8,128)S(1)}, f32[16,512]{1,0:T(8,128)S(1)}, u32[]{:S(2)}, u32[]{:S(2)}) collective-permute-start(f32[16,512]{1,0:T(8,128)S(1)} %get-tuple-element.66), channel_id=1, source_target_pairs={{0,192},{64,0},{128,64},{192,128},{1,193},{65,1},{129,65},{193,129... | collective-permute-start | bytes 98312 | tf_op jit(solution)/shard_map/ppermute | solution.py:21
  47.7 2.9 %collective-permute-start.22 = (f32[16,512]{1,0:T(8,128)S(1)}, f32[16,512]{1,0:T(8,128)S(1)}, u32[]{:S(2)}, u32[]{:S(2)}) collective-permute-start(f32[16,512]{1,0:T(8,128)S(1)} %get-tuple-element.69), channel_id=1, source_target_pairs={{0,1},{1,2},{2,3},{3,4},{4,5},{5,6},{6,7},{7,0},{8,9},{9,10},{10,1... | collective-permute-start | bytes 98312 | tf_op jit(solution)/shard_map/ppermute | solution.py:21
  57.3 3.2 %collective-permute-start.25 = (f32[16,512]{1,0:T(8,128)S(1)}, f32[16,512]{1,0:T(8,128)S(1)}, u32[]{:S(2)}, u32[]{:S(2)}) collective-permute-start(f32[16,512]{1,0:T(8,128)S(1)} %add_add_fusion.1.refs_0_.refs_2_), channel_id=1, source_target_pairs={{0,192},{64,0},{128,64},{192,128},{1,193},{65,1},{129,65},{193,129... | collective-permute-start | bytes 98312 | tf_op jit(solution)/shard_map/ppermute | solution.py:21
  62.4 1.9 %collective-permute-done.24.refs_1_ = f32[16,512]{1,0:T(8,128)S(1)} collective-permute-done((f32[16,512]{1,0:T(8,128)S(1)}, f32[16,512]{1,0:T(8,128)S(1)}, u32[]{:S(2)}, u32[]{:S(2)}) %collective-permute-start.24) | collective-permute-done | bytes 32800 | tf_op jit(solution)/shard_map/ppermute | solution.py:21
  64.4 2.2 %operator.4 = (f32[16,512]{1,0:T(8,128)S(1)}, f32[16,512]{1,0:T(8,128)S(1)}, f32[16,512]{1,0:T(8,128)S(1)}, f32[16,512]{1,0:T(8,128)S(1)}, f32[16,512]{1,0:T(8,1...) custom-call(f32[16,512]{1,0:T(8,128)S(1)} %add_add_fusion.1.refs_0_.refs_2_, ...), custom_call_target="tpu_custom_call" | custom-call | bytes 10190848 | tf_op jit(solution)/shard_map/operator/pallas_call | solution.py:217
  66.9 2.3 %collective-permute-start.31 = (f32[16,512]{1,0:T(8,128)S(1)}, f32[16,512]{1,0:T(8,128)S(1)}, u32[]{:S(2)}, u32[]{:S(2)}) collective-permute-start(f32[16,512]{1,0:T(8,128)S(1)} %get-tuple-element.73), channel_id=1, source_target_pairs={{0,192},{64,0},{128,64},{192,128},{1,193},{65,1},{129,65},{193,129... | collective-permute-start | bytes 98312 | tf_op jit(solution)/shard_map/ppermute | solution.py:21
  70.9 2.0 %collective-permute-start.34 = (f32[16,512]{1,0:T(8,128)S(1)}, f32[16,512]{1,0:T(8,128)S(1)}, u32[]{:S(2)}, u32[]{:S(2)}) collective-permute-start(f32[16,512]{1,0:T(8,128)S(1)} %get-tuple-element.76), channel_id=1, source_target_pairs={{0,1},{1,2},{2,3},{3,4},{4,5},{5,6},{6,7},{7,0},{8,9},{9,10},{10,1... | collective-permute-start | bytes 98312 | tf_op jit(solution)/shard_map/ppermute | solution.py:21
  77.9 3.3 %collective-permute-start.37 = (f32[16,512]{1,0:T(8,128)S(1)}, f32[16,512]{1,0:T(8,128)S(1)}, u32[]{:S(2)}, u32[]{:S(2)}) collective-permute-start(f32[16,512]{1,0:T(8,128)S(1)} %get-tuple-element.80), channel_id=1, source_target_pairs={{0,192},{64,0},{128,64},{192,128},{1,193},{65,1},{129,65},{193,129... | collective-permute-start | bytes 98312 | tf_op jit(solution)/shard_map/ppermute | solution.py:21
  88.8 2.6 %collective-permute-start.47 = (f32[16,512]{1,0:T(8,128)S(1)}, f32[16,512]{1,0:T(8,128)S(1)}, u32[]{:S(2)}, u32[]{:S(2)}) collective-permute-start(f32[16,512]{1,0:T(8,128)S(1)} %add_add_fusion.refs_0_.refs_3_), channel_id=1, source_target_pairs={{0,7},{1,0},{2,1},{3,2},{4,3},{5,4},{6,5},{7,6},{8,15},{9,8},{10,9... | collective-permute-start | bytes 98312 | tf_op jit(solution)/shard_map/ppermute | solution.py:21
  93.2 3.1 %collective-permute-start.43 = (f32[16,512]{1,0:T(8,128)S(1)}, f32[16,512]{1,0:T(8,128)S(1)}, u32[]{:S(2)}, u32[]{:S(2)}) collective-permute-start(f32[16,512]{1,0:T(8,128)S(1)} %add_add_fusion.refs_0_.refs_3_), channel_id=1, source_target_pairs={{0,192},{64,0},{128,64},{192,128},{1,193},{65,1},{129,65},{193,129... | collective-permute-start | bytes 98312 | tf_op jit(solution)/shard_map/ppermute | solution.py:21
  96.5 3.0 %collective-permute-done.44.refs_3_ = f32[16,512]{1,0:T(8,128)S(1)} collective-permute-done((f32[16,512]{1,0:T(8,128)S(1)}, f32[16,512]{1,0:T(8,128)S(1)}, u32[]{:S(2)}, u32[]{:S(2)}) %collective-permute-start.44) | collective-permute-done | bytes 32800 | tf_op jit(solution)/shard_map/ppermute | solution.py:21
  100.3 2.2 %operator.5 = (f32[16,512]{1,0:T(8,128)S(1)}, f32[16,512]{1,0:T(8,128)S(1)}, f32[16,512]{1,0:T(8,128)S(1)}, f32[16,512]{1,0:T(8,128)S(1)}, f32[16,512]{1,0:T(8,1...) custom-call(f32[16,512]{1,0:T(8,128)S(1)} %add_add_fusion.refs_0_.refs_3_, ...), custom_call_target="tpu_custom_call" | custom-call | bytes 10190848 | tf_op jit(solution)/shard_map/operator/pallas_call | solution.py:217
  102.5 2.4 %collective-permute-start.49 = (f32[16,512]{1,0:T(8,128)S(1)}, f32[16,512]{1,0:T(8,128)S(1)}, u32[]{:S(2)}, u32[]{:S(2)}) collective-permute-start(f32[16,512]{1,0:T(8,128)S(1)} %get-tuple-element.87), channel_id=1, source_target_pairs={{0,192},{64,0},{128,64},{192,128},{1,193},{65,1},{129,65},{193,129... | collective-permute-start | bytes 98312 | tf_op jit(solution)/shard_map/ppermute | solution.py:21
  104.9 2.3 %collective-permute-start.51 = (f32[16,512]{1,0:T(8,128)S(1)}, f32[16,512]{1,0:T(8,128)S(1)}, u32[]{:S(2)}, u32[]{:S(2)}) collective-permute-start(f32[16,512]{1,0:T(8,128)S(1)} %get-tuple-element.89), channel_id=1, source_target_pairs={{0,56},{8,0},{16,8},{24,16},{32,24},{40,32},{48,40},{56,48},{1,57}... | collective-permute-start | bytes 98312 | tf_op jit(solution)/shard_map/ppermute | solution.py:21
  108.4 2.0 %collective-permute-start.53 = (f32[16,512]{1,0:T(8,128)S(1)}, f32[16,512]{1,0:T(8,128)S(1)}, u32[]{:S(2)}, u32[]{:S(2)}) collective-permute-start(f32[16,512]{1,0:T(8,128)S(1)} %get-tuple-element.91), channel_id=1, source_target_pairs={{0,7},{1,0},{2,1},{3,2},{4,3},{5,4},{6,5},{7,6},{8,15},{9,8},{10,9... | collective-permute-start | bytes 98312 | tf_op jit(solution)/shard_map/ppermute | solution.py:21
  112.5 17.8 %all_to_all.10 = f32[32,16,128]{2,1,0:T(8,128)S(1)} all-to-all(f32[32,16,128]{2,1,0:T(8,128)S(1)} %broadcast_in_dim.30), channel_id=1, replica_groups=mesh['gx'=4,'gy'=8,'gz'=8] {'gx','gy'}, dimensions={0} | all-to-all | bytes 524288 | tf_op jit(solution)/shard_map/all_to_all | solution.py:232
  130.4 13.4 %all_to_all.11 = f32[8,16,128]{2,1,0:T(8,128)S(1)} all-to-all(f32[8,16,128]{2,1,0:T(8,128)S(1)} %broadcast_in_dim.31), channel_id=1, replica_groups=mesh['gx'=4,'gy'=8,'gz'=8] {'gz'}, dimensions={0} | all-to-all | bytes 131072 | tf_op jit(solution)/shard_map/all_to_all | solution.py:232
  (115 shorter events, 55.2 us)
Async XLA Ops:
  5.0 5.7 %collective-permute-start = (f32[16,512]{1,0:T(8,128)S(1)}, f32[16,512]{1,0:T(8,128)S(1)}, u32[]{:S(2)}, u32[]{:S(2)}) collective-permute-start(f32[16,512]{1,0:T(8,128)S(1)} %get-tuple-element.50), channel_id=1, source_target_pairs={{0,64},{64,128},{128,192},{192,0},{1,65},{65,129},{129,193},{193,1... | collective-permute-start | bytes 98312 | tf_op jit(solution)/shard_map/ppermute | solution.py:21
  6.6 8.2 %collective-permute-start.1 = (f32[16,512]{1,0:T(8,128)S(1)}, f32[16,512]{1,0:T(8,128)S(1)}, u32[]{:S(2)}, u32[]{:S(2)}) collective-permute-start(f32[16,512]{1,0:T(8,128)S(1)} %get-tuple-element.51), channel_id=1, source_target_pairs={{0,192},{64,0},{128,64},{192,128},{1,193},{65,1},{129,65},{193,129... | collective-permute-start | bytes 98312 | tf_op jit(solution)/shard_map/ppermute | solution.py:21
  7.0 7.8 %collective-permute-start.2 = (f32[16,512]{1,0:T(8,128)S(1)}, f32[16,512]{1,0:T(8,128)S(1)}, u32[]{:S(2)}, u32[]{:S(2)}) collective-permute-start(f32[16,512]{1,0:T(8,128)S(1)} %get-tuple-element.52), channel_id=1, source_target_pairs={{0,8},{8,16},{16,24},{24,32},{32,40},{40,48},{48,56},{56,0},{1,9},... | collective-permute-start | bytes 98312 | tf_op jit(solution)/shard_map/ppermute | solution.py:21
  7.1 7.8 %collective-permute-start.3 = (f32[16,512]{1,0:T(8,128)S(1)}, f32[16,512]{1,0:T(8,128)S(1)}, u32[]{:S(2)}, u32[]{:S(2)}) collective-permute-start(f32[16,512]{1,0:T(8,128)S(1)} %get-tuple-element.53), channel_id=1, source_target_pairs={{0,56},{8,0},{16,8},{24,16},{32,24},{40,32},{48,40},{56,48},{1,57}... | collective-permute-start | bytes 98312 | tf_op jit(solution)/shard_map/ppermute | solution.py:21
  8.8 7.7 %collective-permute-start.4 = (f32[16,512]{1,0:T(8,128)S(1)}, f32[16,512]{1,0:T(8,128)S(1)}, u32[]{:S(2)}, u32[]{:S(2)}) collective-permute-start(f32[16,512]{1,0:T(8,128)S(1)} %get-tuple-element.54), channel_id=1, source_target_pairs={{0,1},{1,2},{2,3},{3,4},{4,5},{5,6},{6,7},{7,0},{8,9},{9,10},{10,1... | collective-permute-start | bytes 98312 | tf_op jit(solution)/shard_map/ppermute | solution.py:21
  10.7 5.8 %collective-permute-start.5 = (f32[16,512]{1,0:T(8,128)S(1)}, f32[16,512]{1,0:T(8,128)S(1)}, u32[]{:S(2)}, u32[]{:S(2)}) collective-permute-start(f32[16,512]{1,0:T(8,128)S(1)} %get-tuple-element.55), channel_id=1, source_target_pairs={{0,7},{1,0},{2,1},{3,2},{4,3},{5,4},{6,5},{7,6},{8,15},{9,8},{10,9... | collective-permute-start | bytes 98312 | tf_op jit(solution)/shard_map/ppermute | solution.py:21
  16.6 5.6 %collective-permute-start.11 = (f32[16,512]{1,0:T(8,128)S(1)}, f32[16,512]{1,0:T(8,128)S(1)}, u32[]{:S(2)}, u32[]{:S(2)}) collective-permute-start(f32[16,512]{1,0:T(8,128)S(1)} %add_add_fusion.2.refs_0_.refs_1_), channel_id=1, source_target_pairs={{0,7},{1,0},{2,1},{3,2},{4,3},{5,4},{6,5},{7,6},{8,15},{9,8},{10,9... | collective-permute-start | bytes 98312 | tf_op jit(solution)/shard_map/ppermute | solution.py:21
  32.7 7.3 %collective-permute-start.13 = (f32[16,512]{1,0:T(8,128)S(1)}, f32[16,512]{1,0:T(8,128)S(1)}, u32[]{:S(2)}, u32[]{:S(2)}) collective-permute-start(f32[16,512]{1,0:T(8,128)S(1)} %get-tuple-element.59), channel_id=1, source_target_pairs={{0,192},{64,0},{128,64},{192,128},{1,193},{65,1},{129,65},{193,129... | collective-permute-start | bytes 98312 | tf_op jit(solution)/shard_map/ppermute | solution.py:21
  42.7 7.9 %collective-permute-start.18 = (f32[16,512]{1,0:T(8,128)S(1)}, f32[16,512]{1,0:T(8,128)S(1)}, u32[]{:S(2)}, u32[]{:S(2)}) collective-permute-start(f32[16,512]{1,0:T(8,128)S(1)} %get-tuple-element.65), channel_id=1, source_target_pairs={{0,64},{64,128},{128,192},{192,0},{1,65},{65,129},{129,193},{193,1... | collective-permute-start | bytes 98312 | tf_op jit(solution)/shard_map/ppermute | solution.py:21
  42.8 8.4 %collective-permute-start.19 = (f32[16,512]{1,0:T(8,128)S(1)}, f32[16,512]{1,0:T(8,128)S(1)}, u32[]{:S(2)}, u32[]{:S(2)}) collective-permute-start(f32[16,512]{1,0:T(8,128)S(1)} %get-tuple-element.66), channel_id=1, source_target_pairs={{0,192},{64,0},{128,64},{192,128},{1,193},{65,1},{129,65},{193,129... | collective-permute-start | bytes 98312 | tf_op jit(solution)/shard_map/ppermute | solution.py:21
  47.7 5.3 %collective-permute-start.22 = (f32[16,512]{1,0:T(8,128)S(1)}, f32[16,512]{1,0:T(8,128)S(1)}, u32[]{:S(2)}, u32[]{:S(2)}) collective-permute-start(f32[16,512]{1,0:T(8,128)S(1)} %get-tuple-element.69), channel_id=1, source_target_pairs={{0,1},{1,2},{2,3},{3,4},{4,5},{5,6},{6,7},{7,0},{8,9},{9,10},{10,1... | collective-permute-start | bytes 98312 | tf_op jit(solution)/shard_map/ppermute | solution.py:21
  54.6 5.9 %collective-permute-start.29 = (f32[16,512]{1,0:T(8,128)S(1)}, f32[16,512]{1,0:T(8,128)S(1)}, u32[]{:S(2)}, u32[]{:S(2)}) collective-permute-start(f32[16,512]{1,0:T(8,128)S(1)} %add_add_fusion.1.refs_0_.refs_2_), channel_id=1, source_target_pairs={{0,7},{1,0},{2,1},{3,2},{4,3},{5,4},{6,5},{7,6},{8,15},{9,8},{10,9... | collective-permute-start | bytes 98312 | tf_op jit(solution)/shard_map/ppermute | solution.py:21
  56.8 5.7 %collective-permute-start.26 = (f32[16,512]{1,0:T(8,128)S(1)}, f32[16,512]{1,0:T(8,128)S(1)}, u32[]{:S(2)}, u32[]{:S(2)}) collective-permute-start(f32[16,512]{1,0:T(8,128)S(1)} %add_add_fusion.1.refs_0_.refs_2_), channel_id=1, source_target_pairs={{0,8},{8,16},{16,24},{24,32},{32,40},{40,48},{48,56},{56,0},{1,9},... | collective-permute-start | bytes 98312 | tf_op jit(solution)/shard_map/ppermute | solution.py:21
  66.6 6.3 %collective-permute-start.30 = (f32[16,512]{1,0:T(8,128)S(1)}, f32[16,512]{1,0:T(8,128)S(1)}, u32[]{:S(2)}, u32[]{:S(2)}) collective-permute-start(f32[16,512]{1,0:T(8,128)S(1)} %get-tuple-element.72), channel_id=1, source_target_pairs={{0,64},{64,128},{128,192},{192,0},{1,65},{65,129},{129,193},{193,1... | collective-permute-start | bytes 98312 | tf_op jit(solution)/shard_map/ppermute | solution.py:21
  66.9 7.3 %collective-permute-start.31 = (f32[16,512]{1,0:T(8,128)S(1)}, f32[16,512]{1,0:T(8,128)S(1)}, u32[]{:S(2)}, u32[]{:S(2)}) collective-permute-start(f32[16,512]{1,0:T(8,128)S(1)} %get-tuple-element.73), channel_id=1, source_target_pairs={{0,192},{64,0},{128,64},{192,128},{1,193},{65,1},{129,65},{193,129... | collective-permute-start | bytes 98312 | tf_op jit(solution)/shard_map/ppermute | solution.py:21
  77.7 7.1 %collective-permute-start.36 = (f32[16,512]{1,0:T(8,128)S(1)}, f32[16,512]{1,0:T(8,128)S(1)}, u32[]{:S(2)}, u32[]{:S(2)}) collective-permute-start(f32[16,512]{1,0:T(8,128)S(1)} %get-tuple-element.79), channel_id=1, source_target_pairs={{0,64},{64,128},{128,192},{192,0},{1,65},{65,129},{129,193},{193,1... | collective-permute-start | bytes 98312 | tf_op jit(solution)/shard_map/ppermute | solution.py:21
  77.9 8.3 %collective-permute-start.37 = (f32[16,512]{1,0:T(8,128)S(1)}, f32[16,512]{1,0:T(8,128)S(1)}, u32[]{:S(2)}, u32[]{:S(2)}) collective-permute-start(f32[16,512]{1,0:T(8,128)S(1)} %get-tuple-element.80), channel_id=1, source_target_pairs={{0,192},{64,0},{128,64},{192,128},{1,193},{65,1},{129,65},{193,129... | collective-permute-start | bytes 98312 | tf_op jit(solution)/shard_map/ppermute | solution.py:21
  88.8 7.6 %collective-permute-start.47 = (f32[16,512]{1,0:T(8,128)S(1)}, f32[16,512]{1,0:T(8,128)S(1)}, u32[]{:S(2)}, u32[]{:S(2)}) collective-permute-start(f32[16,512]{1,0:T(8,128)S(1)} %add_add_fusion.refs_0_.refs_3_), channel_id=1, source_target_pairs={{0,7},{1,0},{2,1},{3,2},{4,3},{5,4},{6,5},{7,6},{8,15},{9,8},{10,9... | collective-permute-start | bytes 98312 | tf_op jit(solution)/shard_map/ppermute | solution.py:21
  93.2 6.3 %collective-permute-start.44 = (f32[16,512]{1,0:T(8,128)S(1)}, f32[16,512]{1,0:T(8,128)S(1)}, u32[]{:S(2)}, u32[]{:S(2)}) collective-permute-start(f32[16,512]{1,0:T(8,128)S(1)} %add_add_fusion.refs_0_.refs_3_), channel_id=1, source_target_pairs={{0,8},{8,16},{16,24},{24,32},{32,40},{40,48},{48,56},{56,0},{1,9},... | collective-permute-start | bytes 98312 | tf_op jit(solution)/shard_map/ppermute | solution.py:21
  93.2 6.3 %collective-permute-start.43 = (f32[16,512]{1,0:T(8,128)S(1)}, f32[16,512]{1,0:T(8,128)S(1)}, u32[]{:S(2)}, u32[]{:S(2)}) collective-permute-start(f32[16,512]{1,0:T(8,128)S(1)} %add_add_fusion.refs_0_.refs_3_), channel_id=1, source_target_pairs={{0,192},{64,0},{128,64},{192,128},{1,193},{65,1},{129,65},{193,129... | collective-permute-start | bytes 98312 | tf_op jit(solution)/shard_map/ppermute | solution.py:21
  102.5 5.9 %collective-permute-start.48 = (f32[16,512]{1,0:T(8,128)S(1)}, f32[16,512]{1,0:T(8,128)S(1)}, u32[]{:S(2)}, u32[]{:S(2)}) collective-permute-start(f32[16,512]{1,0:T(8,128)S(1)} %get-tuple-element.86), channel_id=1, source_target_pairs={{0,64},{64,128},{128,192},{192,0},{1,65},{65,129},{129,193},{193,1... | collective-permute-start | bytes 98312 | tf_op jit(solution)/shard_map/ppermute | solution.py:21
  102.5 8.0 %collective-permute-start.49 = (f32[16,512]{1,0:T(8,128)S(1)}, f32[16,512]{1,0:T(8,128)S(1)}, u32[]{:S(2)}, u32[]{:S(2)}) collective-permute-start(f32[16,512]{1,0:T(8,128)S(1)} %get-tuple-element.87), channel_id=1, source_target_pairs={{0,192},{64,0},{128,64},{192,128},{1,193},{65,1},{129,65},{193,129... | collective-permute-start | bytes 98312 | tf_op jit(solution)/shard_map/ppermute | solution.py:21
  104.9 5.5 %collective-permute-start.50 = (f32[16,512]{1,0:T(8,128)S(1)}, f32[16,512]{1,0:T(8,128)S(1)}, u32[]{:S(2)}, u32[]{:S(2)}) collective-permute-start(f32[16,512]{1,0:T(8,128)S(1)} %get-tuple-element.88), channel_id=1, source_target_pairs={{0,8},{8,16},{16,24},{24,32},{32,40},{40,48},{48,56},{56,0},{1,9},... | collective-permute-start | bytes 98312 | tf_op jit(solution)/shard_map/ppermute | solution.py:21
  104.9 5.5 %collective-permute-start.51 = (f32[16,512]{1,0:T(8,128)S(1)}, f32[16,512]{1,0:T(8,128)S(1)}, u32[]{:S(2)}, u32[]{:S(2)}) collective-permute-start(f32[16,512]{1,0:T(8,128)S(1)} %get-tuple-element.89), channel_id=1, source_target_pairs={{0,56},{8,0},{16,8},{24,16},{32,24},{40,32},{48,40},{56,48},{1,57}... | collective-permute-start | bytes 98312 | tf_op jit(solution)/shard_map/ppermute | solution.py:21
  (35 other events, 222.3 us)

commit v2 on v1

--- a/solution.py
+++ b/solution.py
@@ -11,22 +11,34 @@
 EPSILON = 1e-06
 SCALE = 2.0**-12
 AXES = ("gx", "gy", "gz")
+EARLY = (0, 1, 2, 3)
+LATE = (4, 5)
+HOLD = True
 BF16 = jnp.bfloat16
 F32 = jnp.float32
 VMEM = pltpu.VMEM
 
 
-def ring(array, axis, by):
+def swap(array, axis, start):
     n = lax.axis_size(axis)
-    return lax.ppermute(array, axis, [(i, (i + by) % n) for i in range(n)])
-
-
-def sends(face_sums):
-    got = [None] * 6
-    for dim in (1, 2, 0):
-        got[2 * dim + 1] = ring(face_sums[2 * dim], AXES[dim], -1)
-        got[2 * dim] = ring(face_sums[2 * dim + 1], AXES[dim], 1)
-    return got
+    pairs = []
+    for i in range(start, n + start, 2):
+        pairs += [(i % n, (i + 1) % n), ((i + 1) % n, i % n)]
+    return lax.ppermute(array, axis, sorted(pairs))
+
+
+def trade(slots):
+    return [swap(slots[slot], AXES[slot // 2], slot % 2) for slot in range(6)]
+
+
+def even_at(dim):
+    return lax.rem(lax.axis_index(AXES[dim]), 2) == 0
+
+
+def face_of(slot):
+    dim = slot // 2
+    upper = even_at(dim) if slot % 2 == 0 else jnp.logical_not(even_at(dim))
+    return 2 * dim + upper.astype(jnp.int32)
 
 
 def split(x):
@@ -40,51 +52,110 @@
     return x[:rows] + x[rows:]
 
 
-def put_faces(products, picks, own_ref, face_refs):
+def put_faces(products, picks, own_ref, slot_refs):
     width = picks.shape[2]
     owned = picks.shape[1]
     own_ref[...] = products[:, :owned]
+    placed = []
     for face in range(6):
         block = products[:, owned + face * width : owned + (face + 1) * width]
-        face_refs[face][...] = joined(
-            lax.dot_general(
-                split(block),
-                picks[face],
-                (((1,), (1,)), ((), ())),
-                preferred_element_type=F32,
+        placed.append(
+            joined(
+                lax.dot_general(
+                    split(block),
+                    picks[face],
+                    (((1,), (1,)), ((), ())),
+                    preferred_element_type=F32,
+                )
             )
         )
-
-
-def first_kernel(vector_ref, maps_ref, restricted_ref, picks_ref, own_ref, *face_refs):
+    for dim in range(3):
+        even = even_at(dim)
+        lower, upper = placed[2 * dim], placed[2 * dim + 1]
+        slot_refs[2 * dim][...] = jnp.where(even, upper, lower)
+        slot_refs[2 * dim + 1][...] = jnp.where(even, lower, upper)
+
+
+def first_kernel(*refs):
+    sources, outputs, scratch = refs[:3], refs[3:11], refs[11:]
+    picks_ref, own_ref, slot_refs = outputs[0], outputs[1], outputs[2:]
+    maps_ref, vector_ref, restricted_ref, sems = scratch
+    copies = [
+        pltpu.make_async_copy(source, target, sems.at[i])
+        for i, (source, target) in enumerate(zip(sources, scratch[:3]))
+    ]
+    for copy in copies:
+        copy.start()
     owned = vector_ref.shape[1]
-    width = maps_ref.shape[1]
+    width = maps_ref.shape[2]
     place = lax.broadcasted_iota(jnp.int32, (owned, width), 0)
-    for face in range(6):
-        chosen = maps_ref[face : face + 1, :] == place
-        picks_ref[face] = jnp.where(chosen, 1.0, 0.0).astype(BF16)
-    products = joined(
-        jnp.dot(split(vector_ref[...]), restricted_ref[...], preferred_element_type=F32)
-    )
-    put_faces(products, picks_ref, own_ref, face_refs)
-
-
-def operator_kernel(*refs):
-    vector_ref, got, (picks_ref, schur_ref, own_ref), face_refs = (
-        refs[0],
-        refs[1:7],
-        refs[7:10],
-        refs[10:],
-    )
-    parts = [split(vector_ref[...])]
-    for face in range(6):
-        parts.append(
-            jnp.dot(split(got[face][...]), picks_ref[face], preferred_element_type=F32).astype(BF16)
-        )
-    products = joined(
-        jnp.dot(jnp.concatenate(parts, axis=1), schur_ref[...], preferred_element_type=F32)
-    )
-    put_faces(products, picks_ref, own_ref, face_refs)
+    copies[0].wait()
+    for dim, axis in enumerate(AXES):
+        at = lax.axis_index(axis)
+        for side, exists in ((0, at > 0), (1, at < lax.axis_size(axis) - 1)):
+            face = 2 * dim + side
+            wanted = jnp.where(exists, maps_ref[face], -1)
+            picks_ref[face] = jnp.where(wanted == place, 1.0, 0.0).astype(BF16)
+    copies[1].wait()
+    vector = split(vector_ref[...])
+    copies[2].wait()
+    products = joined(jnp.dot(vector, restricted_ref[...], preferred_element_type=F32))
+    put_faces(products, picks_ref, own_ref, slot_refs)
+
+
+def hold_kernel(own_ref, schur_ref, out_ref):
+    out_ref[...] = own_ref[...]
+
+
+def own_rows_kernel(vector_ref, schur_ref, total_ref):
+    owned = vector_ref.shape[1]
+    vector = split(vector_ref[...])
+    step = schur_ref.shape[1] // 2
+
+    @pl.loop(0, 2)
+    def _(i):
+        columns = pl.ds(pl.multiple_of(i * step, step), step)
+        total_ref[:, columns] = jnp.dot(
+            vector, schur_ref[:owned, columns], preferred_element_type=F32
+        )
+
+
+def picked(slots, got, picks_ref):
+    owned, width = picks_ref.shape[1:]
+    rows, starts = [], []
+    for slot, part in zip(slots, got):
+        face = face_of(slot)
+        rows.append(
+            jnp.dot(split(part[...]), picks_ref[face], preferred_element_type=F32).astype(BF16)
+        )
+        starts.append(pl.multiple_of(owned + face * width, width))
+    return rows, starts
+
+
+def add_rows(total, rows, starts, schur_ref, columns):
+    for row, start in zip(rows, starts):
+        block = schur_ref[pl.ds(start, row.shape[1]), columns]
+        total = total + jnp.dot(row, block, preferred_element_type=F32)
+    return total
+
+
+def some_rows_kernel(slots, *refs):
+    got, (sofar_ref, picks_ref, schur_ref, total_ref) = refs[: len(slots)], refs[len(slots) :]
+    rows, starts = picked(slots, got, picks_ref)
+    step = schur_ref.shape[1] // 4
+
+    @pl.loop(0, 4)
+    def _(i):
+        columns = pl.ds(pl.multiple_of(i * step, step), step)
+        total_ref[:, columns] = add_rows(sofar_ref[:, columns], rows, starts, schur_ref, columns)
+
+
+def last_rows_kernel(slots, *refs):
+    got, rest = refs[: len(slots)], refs[len(slots) :]
+    sofar_ref, picks_ref, schur_ref, own_ref = rest[:4]
+    rows, starts = picked(slots, got, picks_ref)
+    total = add_rows(sofar_ref[...], rows, starts, schur_ref, slice(None))
+    put_faces(joined(total), picks_ref, own_ref, rest[4:])
 
 
 def gram_entries(basis):
@@ -105,9 +176,8 @@
     return total
 
 
-def next_kernel(count, *refs):
+def next_kernel(*refs):
     own, got, rest = refs[0], refs[1:7], refs[7:]
-    older, rest = rest[:count], rest[count:]
     picks_ref, restricted_ref, vector_ref, own_ref = rest[:4]
     face_refs = rest[4:]
     vector = summed(own, got) * SCALE
@@ -123,7 +193,8 @@
     total = gram_entries(basis[:1])
     for newest in range(1, len(basis)):
         total = total + gram_entries(basis[: newest + 1])
-    gram_ref[...] = total
+    half = total.shape[0] // 2
+    gram_ref[...] = total[:half] + pltpu.roll(total[half:], 64, 1)
 
 
 def rotate_solve(columns, beta_norm):
@@ -198,7 +269,8 @@
 def last_kernel(*refs):
     gram_ref, directions = refs[0], refs[1:-2]
     adjoint_ref, ratio_ref = refs[-2:]
-    sums = gram_ref[...]
+    packed = gram_ref[...]
+    sums = jnp.concatenate([packed, pltpu.roll(packed, 64, 1)], axis=0)
 
     def gram(a, b):
         at = min(a, b) * 4 + max(a, b)
@@ -209,20 +281,30 @@
     for i in range(1, ITERS):
         total = total + shares[i] * directions[i][...]
     adjoint_ref[...] = total
-    ratio_ref[...] = jnp.broadcast_to(ratio, ratio_ref.shape)
-
-
-def call(kernel, operands, outputs, name, flops=0, limit=16 << 20):
-    bytes_moved = sum(x.size * x.dtype.itemsize for x in operands)
+    rows = ratio.shape[0]
+    here = lax.broadcasted_iota(jnp.int32, (rows, rows), 0)
+    there = lax.broadcasted_iota(jnp.int32, (rows, rows), 1)
+    ratio_ref[...] = jnp.sum(jnp.where(here == there, ratio, 0.0), axis=0, keepdims=True)
+
+
+def call(kernel, operands, outputs, name, keep=True, scratch=(), limit=8 << 20):
+    space = pltpu.HBM if scratch else VMEM
+    make = VMEM if keep else jax.ShapeDtypeStruct
+    operands = [pltpu.with_memory_space_constraint(x, space) for x in operands]
     return pl.pallas_call(
         kernel,
-        out_shape=tuple(VMEM(shape, dtype) for shape, dtype in outputs),
-        in_specs=[pl.BlockSpec(memory_space=VMEM)] * len(operands),
+        out_shape=tuple(make(shape, dtype) for shape, dtype in outputs),
+        in_specs=[pl.BlockSpec(memory_space=space)] * len(operands),
         out_specs=tuple(pl.BlockSpec(memory_space=VMEM) for _ in outputs),
+        scratch_shapes=scratch,
         compiler_params=pltpu.CompilerParams(vmem_limit_bytes=limit),
-        cost_estimate=pl.CostEstimate(flops=flops, bytes_accessed=bytes_moved, transcendentals=0),
+        cost_estimate=pl.CostEstimate(
+            flops=0,
+            bytes_accessed=sum(x.size * x.dtype.itemsize for x in operands),
+            transcendentals=0,
+        ),
         name=name,
-    )(*[pltpu.with_memory_space_constraint(x, VMEM) for x in operands])
+    )(*operands)
 
 
 def all_sum(array, stages):
@@ -239,46 +321,58 @@
     restricted = inverse_rows[0, 0, 0]
     rows, owned = vector.shape
     width = face_maps.shape[-1]
-    exists = []
-    for axis in AXES:
-        at = lax.axis_index(axis)
-        exists += [at > 0, at < lax.axis_size(axis) - 1]
-    maps = jnp.where(jnp.stack(exists)[:, None], face_maps[0, 0, 0], -1)
+    maps = face_maps.reshape(6, 1, width)
 
     block = ((rows, owned), F32)
-    picks, own, *faces = call(
+    wide = ((2 * rows, schur.shape[1]), F32)
+    picks, own, *slots = call(
         first_kernel,
-        (vector, maps, restricted),
+        (maps, vector, restricted),
         (((6, owned, width), BF16),) + (block,) * 7,
         "first",
+        scratch=[
+            VMEM(maps.shape, maps.dtype),
+            VMEM(vector.shape, vector.dtype),
+            VMEM(restricted.shape, restricted.dtype),
+            pltpu.SemaphoreType.DMA((3,)),
+        ],
     )
     basis = [vector]
     directions = []
     for section in range(ITERS):
-        got = sends(faces)
+        if section == 0 and HOLD:
+            (own,) = call(hold_kernel, (own, schur), (block,), "hold")
+        got = trade(slots)
         direction = own
         for part in got:
             direction = direction + part
         directions.append(direction)
-        got = sends([direction] * 6)
-        own, *faces = call(
-            operator_kernel, (direction, *got, picks, schur), (block,) * 7, "operator"
-        )
-        got = sends(faces)
+        got = trade([direction] * 6)
+        (total,) = call(own_rows_kernel, (direction, schur), (wide,), "own_rows")
+        (total,) = call(
+            functools.partial(some_rows_kernel, EARLY),
+            (*[got[slot] for slot in EARLY], total, picks, schur),
+            (wide,),
+            "some_rows",
+        )
+        own, *slots = call(
+            functools.partial(last_rows_kernel, LATE),
+            (*[got[slot] for slot in LATE], total, picks, schur),
+            (block,) * 7,
+            "last_rows",
+        )
+        got = trade(slots)
         if section + 1 < ITERS:
-            vector, own, *faces = call(
-                functools.partial(next_kernel, 0),
-                (own, *got, picks, restricted),
-                (block,) * 8,
-                "next",
+            vector, own, *slots = call(
+                next_kernel, (own, *got, picks, restricted), (block,) * 8, "next"
             )
             basis.append(vector)
-    (gram,) = call(gram_kernel, (own, *got, *basis), (((rows, 128), F32),), "gram")
+    (gram,) = call(gram_kernel, (own, *got, *basis), (((rows // 2, 128), F32),), "gram")
     gram = all_sum(gram, (("gx", "gy"), "gz"))
     adjoint, ratio = call(
-        last_kernel, (gram, *directions), (block, ((rows, 128), F32)), "last"
+        last_kernel, (gram, *directions), (block, ((1, rows), F32)), "last", keep=False
     )
-    return (adjoint[None, None, None], ratio[:, 0])
+    return (adjoint[None, None, None], ratio.reshape(rows))
 
 
 def solution(mesh):

time: 148 us -> 125 us (0.84)
  starting transfers between devices: 70.4 us -> 56.8 us
  blocking collectives: 31.2 us -> 23.8 us
  Pallas kernels: 10.9 us -> 15.6 us
  local copies, waits for them, and re-layouts: 7.11 us -> 3.41 us
  waiting for transfers between devices: 25.1 us -> 22.7 us
    ppermute x54, starting transfers between devices: 70.4 us -> 56.8 us  [swap(): return lax.ppermute(array, axis, sorted(pairs))]
    all_to_all x2, blocking collectives: 31.2 us -> 23.8 us  [all_sum(): array = jnp.sum(lax.all_to_all(spread, axis, 0, 0), axis=0)]
    pallas_call x8 -> x15, Pallas kernels: 10.9 us -> 15.6 us  [call(): pl.pallas_call(kernel, out_shape=tuple((make(shape, dtype) for shape, dty...]
    unnamed x11 -> x8, local copies, waits for them, and re-layouts: 6.35 us -> 3.39 us
    ppermute x54, waiting for transfers between devices: 25.1 us -> 22.7 us  [swap(): return lax.ppermute(array, axis, sorted(pairs))]
  transfers between devices with their start and end apart: 54 -> 54, of which waited for: 18 -> 17; matrix products, arithmetic and copies ran while one was open for 0% -> 0% of each run, Pallas kernels for 0% -> 5%
where the time goes in v2:
time: 125 us; the launch traced here: 123 us
  starting transfers between devices  56.8 us (45%)
  blocking collectives  23.8 us (19%)
  waiting for transfers between devices  22.7 us (18%)
  Pallas kernels  15.6 us (12%)
  local copies, waits for them, and re-layouts  3.41 us (3%)
    ppermute x54, starting transfers between devices, swap(): return lax.ppermute(array, axis, sorted(pairs))  56.8 us
    all_to_all x2, blocking collectives, all_sum(): array = jnp.sum(lax.all_to_all(spread, axis, 0, 0), axis=0)  23.8 us
    ppermute x54, waiting for transfers between devices, swap(): return lax.ppermute(array, axis, sorted(pairs))  22.7 us
    pallas_call x15, Pallas kernels, call(): pl.pallas_call(kernel, out_shape=tuple((make(shape, dtype) for shape, dty...  15.6 us
    unnamed x8, local copies, waits for them, and re-layouts  3.39 us
  transfers between devices with their start and end apart: 54, of which 17 were waited for; matrix products, arithmetic and copies ran while one was open for 0% of the time, Pallas kernels for 5%

profile of v2, /device:TPU:10, one launch (start us, length us, event | category | flops | bytes accessed | tf_op | source)
XLA Modules:
  0.0 123.2 jit_solution(4542603873936019640)
XLA Ops:
  0.6 2.6 %first.1 = (bf16[6,512,256]{2,1,0:T(8,128)(2,1)S(1)}, f32[16,512]{1,0:T(8,128)S(1)}, f32[16,512]{1,0:T(8,128)S(1)}, f32[16,512]{1,0:T(8,128)S(1)}, f32[16,512]{1...) custom-call(s32[6,1,256]{2,1,0:T(1,128)} %bitcast.21, f32[16,512]{1,0:T(8,128)} %bitcast.19, ...), custom_call_target="tpu_custom_call" | custom-call | bytes 2136064 | tf_op jit(solution)/shard_map/first/pallas_call | solution.py:294
  3.7 2.4 %collective-permute-start.1 = (f32[16,512]{1,0:T(8,128)S(1)}, f32[16,512]{1,0:T(8,128)S(1)}, u32[]{:S(2)}, u32[]{:S(2)}) collective-permute-start(f32[16,512]{1,0:T(8,128)S(1)} %get-tuple-element.51), channel_id=1, source_target_pairs={{0,192},{64,128},{128,64},{192,0},{1,193},{65,129},{129,65},{193,1... | collective-permute-start | bytes 98312 | tf_op jit(solution)/shard_map/ppermute | solution.py:27
  6.8 1.9 %collective-permute-start.4 = (f32[16,512]{1,0:T(8,128)S(1)}, f32[16,512]{1,0:T(8,128)S(1)}, u32[]{:S(2)}, u32[]{:S(2)}) collective-permute-start(f32[16,512]{1,0:T(8,128)S(1)} %get-tuple-element.54), channel_id=1, source_target_pairs={{0,1},{1,0},{2,3},{3,2},{4,5},{5,4},{6,7},{7,6},{8,9},{9,8},{10,11... | collective-permute-start | bytes 98312 | tf_op jit(solution)/shard_map/ppermute | solution.py:27
  8.7 4.9 %collective-permute-start.5 = (f32[16,512]{1,0:T(8,128)S(1)}, f32[16,512]{1,0:T(8,128)S(1)}, u32[]{:S(2)}, u32[]{:S(2)}) collective-permute-start(f32[16,512]{1,0:T(8,128)S(1)} %get-tuple-element.55), channel_id=1, source_target_pairs={{0,7},{1,2},{2,1},{3,4},{4,3},{5,6},{6,5},{7,0},{8,15},{9,10},{10,... | collective-permute-start | bytes 98312 | tf_op jit(solution)/shard_map/ppermute | solution.py:27
  13.7 3.4 %copy-done = bf16[1,1,1,2048,2048]{4,3,2,1,0:T(8,128)(2,1)S(1)} copy-done((bf16[1,1,1,2048,2048]{4,3,2,1,0:T(8,128)(2,1)S(1)}, bf16[1,1,1,2048,2048]{4,3,2,1,0:T(8,128)(2,1)}, u32[]{:S(2)}) %copy-start) | copy-done | bytes 8388632
  17.6 2.5 %collective-permute-start.11 = (f32[16,512]{1,0:T(8,128)S(1)}, f32[16,512]{1,0:T(8,128)S(1)}, u32[]{:S(2)}, u32[]{:S(2)}) collective-permute-start(f32[16,512]{1,0:T(8,128)S(1)} %add_add_fusion.2.vector_ref.refs_1_), channel_id=1, source_target_pairs={{0,56},{8,16},{16,8},{24,32},{32,24},{40,48},{48,40},{56,0},{1,57}... | collective-permute-start | bytes 98312 | tf_op jit(solution)/shard_map/ppermute | solution.py:27
  21.9 2.0 %collective-permute-start.7 = (f32[16,512]{1,0:T(8,128)S(1)}, f32[16,512]{1,0:T(8,128)S(1)}, u32[]{:S(2)}, u32[]{:S(2)}) collective-permute-start(f32[16,512]{1,0:T(8,128)S(1)} %add_add_fusion.2.vector_ref.refs_1_), channel_id=1, source_target_pairs={{0,7},{1,2},{2,1},{3,4},{4,3},{5,6},{6,5},{7,0},{8,15},{9,10},{10,... | collective-permute-start | bytes 98312 | tf_op jit(solution)/shard_map/ppermute | solution.py:27
  28.0 1.8 %collective-permute-start.12 = (f32[16,512]{1,0:T(8,128)S(1)}, f32[16,512]{1,0:T(8,128)S(1)}, u32[]{:S(2)}, u32[]{:S(2)}) collective-permute-start(f32[16,512]{1,0:T(8,128)S(1)} %get-tuple-element.58), channel_id=1, source_target_pairs={{0,64},{64,0},{128,192},{192,128},{1,65},{65,1},{129,193},{193,129... | collective-permute-start | bytes 98312 | tf_op jit(solution)/shard_map/ppermute | solution.py:27
  32.7 1.7 %collective-permute-start.17 = (f32[16,512]{1,0:T(8,128)S(1)}, f32[16,512]{1,0:T(8,128)S(1)}, u32[]{:S(2)}, u32[]{:S(2)}) collective-permute-start(f32[16,512]{1,0:T(8,128)S(1)} %get-tuple-element.63), channel_id=1, source_target_pairs={{0,7},{1,2},{2,1},{3,4},{4,3},{5,6},{6,5},{7,0},{8,15},{9,10},{10,... | collective-permute-start | bytes 98312 | tf_op jit(solution)/shard_map/ppermute | solution.py:27
  35.8 2.0 %collective-permute-done.17.refs_6_ = f32[16,512]{1,0:T(8,128)S(1)} collective-permute-done((f32[16,512]{1,0:T(8,128)S(1)}, f32[16,512]{1,0:T(8,128)S(1)}, u32[]{:S(2)}, u32[]{:S(2)}) %collective-permute-start.17) | collective-permute-done | bytes 32800 | tf_op jit(solution)/shard_map/ppermute | solution.py:27
  42.7 1.7 %collective-permute-start.23 = (f32[16,512]{1,0:T(8,128)S(1)}, f32[16,512]{1,0:T(8,128)S(1)}, u32[]{:S(2)}, u32[]{:S(2)}) collective-permute-start(f32[16,512]{1,0:T(8,128)S(1)} %get-tuple-element.70), channel_id=1, source_target_pairs={{0,7},{1,2},{2,1},{3,4},{4,3},{5,6},{6,5},{7,0},{8,15},{9,10},{10,... | collective-permute-start | bytes 98312 | tf_op jit(solution)/shard_map/ppermute | solution.py:27
  45.8 2.0 %collective-permute-done.23 = f32[16,512]{1,0:T(8,128)S(1)} collective-permute-done((f32[16,512]{1,0:T(8,128)S(1)}, f32[16,512]{1,0:T(8,128)S(1)}, u32[]{:S(2)}, u32[]{:S(2)}) %collective-permute-start.23) | collective-permute-done | bytes 32800 | tf_op jit(solution)/shard_map/ppermute | solution.py:27
  51.8 1.7 %collective-permute-start.25 = (f32[16,512]{1,0:T(8,128)S(1)}, f32[16,512]{1,0:T(8,128)S(1)}, u32[]{:S(2)}, u32[]{:S(2)}) collective-permute-start(f32[16,512]{1,0:T(8,128)S(1)} %add_add_fusion.1.vector_ref.refs_2_), channel_id=1, source_target_pairs={{0,7},{1,2},{2,1},{3,4},{4,3},{5,6},{6,5},{7,0},{8,15},{9,10},{10,... | collective-permute-start | bytes 98312 | tf_op jit(solution)/shard_map/ppermute | solution.py:27
  62.0 1.7 %collective-permute-start.35 = (f32[16,512]{1,0:T(8,128)S(1)}, f32[16,512]{1,0:T(8,128)S(1)}, u32[]{:S(2)}, u32[]{:S(2)}) collective-permute-start(f32[16,512]{1,0:T(8,128)S(1)} %get-tuple-element.77), channel_id=1, source_target_pairs={{0,7},{1,2},{2,1},{3,4},{4,3},{5,6},{6,5},{7,0},{8,15},{9,10},{10,... | collective-permute-start | bytes 98312 | tf_op jit(solution)/shard_map/ppermute | solution.py:27
  63.7 1.9 %collective-permute-done.34.refs_5_ = f32[16,512]{1,0:T(8,128)S(1)} collective-permute-done((f32[16,512]{1,0:T(8,128)S(1)}, f32[16,512]{1,0:T(8,128)S(1)}, u32[]{:S(2)}, u32[]{:S(2)}) %collective-permute-start.34) | collective-permute-done | bytes 32800 | tf_op jit(solution)/shard_map/ppermute | solution.py:27
  67.9 1.7 %collective-permute-start.36 = (f32[16,512]{1,0:T(8,128)S(1)}, f32[16,512]{1,0:T(8,128)S(1)}, u32[]{:S(2)}, u32[]{:S(2)}) collective-permute-start(f32[16,512]{1,0:T(8,128)S(1)} %get-tuple-element.79), channel_id=1, source_target_pairs={{0,64},{64,0},{128,192},{192,128},{1,65},{65,1},{129,193},{193,129... | collective-permute-start | bytes 98312 | tf_op jit(solution)/shard_map/ppermute | solution.py:27
  72.5 1.7 %collective-permute-start.41 = (f32[16,512]{1,0:T(8,128)S(1)}, f32[16,512]{1,0:T(8,128)S(1)}, u32[]{:S(2)}, u32[]{:S(2)}) collective-permute-start(f32[16,512]{1,0:T(8,128)S(1)} %get-tuple-element.84), channel_id=1, source_target_pairs={{0,7},{1,2},{2,1},{3,4},{4,3},{5,6},{6,5},{7,0},{8,15},{9,10},{10,... | collective-permute-start | bytes 98312 | tf_op jit(solution)/shard_map/ppermute | solution.py:27
  75.7 1.9 %collective-permute-done.41 = f32[16,512]{1,0:T(8,128)S(1)} collective-permute-done((f32[16,512]{1,0:T(8,128)S(1)}, f32[16,512]{1,0:T(8,128)S(1)}, u32[]{:S(2)}, u32[]{:S(2)}) %collective-permute-start.41) | collective-permute-done | bytes 32800 | tf_op jit(solution)/shard_map/ppermute | solution.py:27
  81.7 1.7 %collective-permute-start.43 = (f32[16,512]{1,0:T(8,128)S(1)}, f32[16,512]{1,0:T(8,128)S(1)}, u32[]{:S(2)}, u32[]{:S(2)}) collective-permute-start(f32[16,512]{1,0:T(8,128)S(1)} %add_add_fusion.vector_ref.refs_3_), channel_id=1, source_target_pairs={{0,7},{1,2},{2,1},{3,4},{4,3},{5,6},{6,5},{7,0},{8,15},{9,10},{10,... | collective-permute-start | bytes 98312 | tf_op jit(solution)/shard_map/ppermute | solution.py:27
  92.0 1.7 %collective-permute-start.53 = (f32[16,512]{1,0:T(8,128)S(1)}, f32[16,512]{1,0:T(8,128)S(1)}, u32[]{:S(2)}, u32[]{:S(2)}) collective-permute-start(f32[16,512]{1,0:T(8,128)S(1)} %get-tuple-element.91), channel_id=1, source_target_pairs={{0,7},{1,2},{2,1},{3,4},{4,3},{5,6},{6,5},{7,0},{8,15},{9,10},{10,... | collective-permute-start | bytes 98312 | tf_op jit(solution)/shard_map/ppermute | solution.py:27
  95.2 1.9 %collective-permute-done.53.refs_6_ = f32[16,512]{1,0:T(8,128)S(1)} collective-permute-done((f32[16,512]{1,0:T(8,128)S(1)}, f32[16,512]{1,0:T(8,128)S(1)}, u32[]{:S(2)}, u32[]{:S(2)}) %collective-permute-start.53) | collective-permute-done | bytes 32800 | tf_op jit(solution)/shard_map/ppermute | solution.py:27
  97.3 11.5 %all_to_all.10 = f32[32,8,128]{2,1,0:T(8,128)S(1)} all-to-all(f32[32,8,128]{2,1,0:T(8,128)S(1)} %broadcast_in_dim.6), channel_id=1, replica_groups=mesh['gx'=4,'gy'=8,'gz'=8] {'gx','gy'}, dimensions={0} | all-to-all | bytes 262144 | tf_op jit(solution)/shard_map/all_to_all | solution.py:314
  108.9 12.3 %all_to_all.11 = f32[8,8,128]{2,1,0:T(8,128)S(1)} all-to-all(f32[8,8,128]{2,1,0:T(8,128)S(1)} %broadcast_in_dim.7), channel_id=1, replica_groups=mesh['gx'=4,'gy'=8,'gz'=8] {'gz'}, dimensions={0} | all-to-all | bytes 65536 | tf_op jit(solution)/shard_map/all_to_all | solution.py:314
  121.2 2.0 %last.1 = (f32[16,512]{1,0:T(8,128)}, f32[1,16]{1,0:T(1,128)}) custom-call(f32[8,128]{1,0:T(8,128)S(1)} %reduce_sum.19.refs_0_, f32[16,512]{1,0:T(8,128)S(1)} %add_add_fusion.2.vector_ref.refs_1_, f32[16,512]{1,0:T(8,128)S(1)} %add_add_fusion.1.vector_ref.refs_2_, f32[16,512]{1,0:T(8,128)S(1)} %add_add_fusion.vector_ref.refs_3_), custom_call_target="tpu_custom_call" | custom-call | bytes 102400 | tf_op jit(solution)/shard_map/last/pallas_call | solution.py:294
  (116 shorter events, 51.8 us)
Async XLA Ops:
  3.2 5.5 %collective-permute-start = (f32[16,512]{1,0:T(8,128)S(1)}, f32[16,512]{1,0:T(8,128)S(1)}, u32[]{:S(2)}, u32[]{:S(2)}) collective-permute-start(f32[16,512]{1,0:T(8,128)S(1)} %get-tuple-element.50), channel_id=1, source_target_pairs={{0,64},{64,0},{128,192},{192,128},{1,65},{65,1},{129,193},{193,129... | collective-permute-start | bytes 98312 | tf_op jit(solution)/shard_map/ppermute | solution.py:27
  3.7 13.3 %collective-permute-start.1 = (f32[16,512]{1,0:T(8,128)S(1)}, f32[16,512]{1,0:T(8,128)S(1)}, u32[]{:S(2)}, u32[]{:S(2)}) collective-permute-start(f32[16,512]{1,0:T(8,128)S(1)} %get-tuple-element.51), channel_id=1, source_target_pairs={{0,192},{64,128},{128,64},{192,0},{1,193},{65,129},{129,65},{193,1... | collective-permute-start | bytes 98312 | tf_op jit(solution)/shard_map/ppermute | solution.py:27
  6.2 10.9 %collective-permute-start.2 = (f32[16,512]{1,0:T(8,128)S(1)}, f32[16,512]{1,0:T(8,128)S(1)}, u32[]{:S(2)}, u32[]{:S(2)}) collective-permute-start(f32[16,512]{1,0:T(8,128)S(1)} %get-tuple-element.52), channel_id=1, source_target_pairs={{0,8},{8,0},{16,24},{24,16},{32,40},{40,32},{48,56},{56,48},{1,9},... | collective-permute-start | bytes 98312 | tf_op jit(solution)/shard_map/ppermute | solution.py:27
  6.2 10.9 %collective-permute-start.3 = (f32[16,512]{1,0:T(8,128)S(1)}, f32[16,512]{1,0:T(8,128)S(1)}, u32[]{:S(2)}, u32[]{:S(2)}) collective-permute-start(f32[16,512]{1,0:T(8,128)S(1)} %get-tuple-element.53), channel_id=1, source_target_pairs={{0,56},{8,16},{16,8},{24,32},{32,24},{40,48},{48,40},{56,0},{1,57}... | collective-permute-start | bytes 98312 | tf_op jit(solution)/shard_map/ppermute | solution.py:27
  6.8 10.3 %collective-permute-start.4 = (f32[16,512]{1,0:T(8,128)S(1)}, f32[16,512]{1,0:T(8,128)S(1)}, u32[]{:S(2)}, u32[]{:S(2)}) collective-permute-start(f32[16,512]{1,0:T(8,128)S(1)} %get-tuple-element.54), channel_id=1, source_target_pairs={{0,1},{1,0},{2,3},{3,2},{4,5},{5,4},{6,7},{7,6},{8,9},{9,8},{10,11... | collective-permute-start | bytes 98312 | tf_op jit(solution)/shard_map/ppermute | solution.py:27
  8.7 8.4 %collective-permute-start.5 = (f32[16,512]{1,0:T(8,128)S(1)}, f32[16,512]{1,0:T(8,128)S(1)}, u32[]{:S(2)}, u32[]{:S(2)}) collective-permute-start(f32[16,512]{1,0:T(8,128)S(1)} %get-tuple-element.55), channel_id=1, source_target_pairs={{0,7},{1,2},{2,1},{3,4},{4,3},{5,6},{6,5},{7,0},{8,15},{9,10},{10,... | collective-permute-start | bytes 98312 | tf_op jit(solution)/shard_map/ppermute | solution.py:27
  17.1 4.8 %collective-permute-start.10 = (f32[16,512]{1,0:T(8,128)S(1)}, f32[16,512]{1,0:T(8,128)S(1)}, u32[]{:S(2)}, u32[]{:S(2)}) collective-permute-start(f32[16,512]{1,0:T(8,128)S(1)} %add_add_fusion.2.vector_ref.refs_1_), channel_id=1, source_target_pairs={{0,8},{8,0},{16,24},{24,16},{32,40},{40,32},{48,56},{56,48},{1,9},... | collective-permute-start | bytes 98312 | tf_op jit(solution)/shard_map/ppermute | solution.py:27
  17.6 6.9 %collective-permute-start.11 = (f32[16,512]{1,0:T(8,128)S(1)}, f32[16,512]{1,0:T(8,128)S(1)}, u32[]{:S(2)}, u32[]{:S(2)}) collective-permute-start(f32[16,512]{1,0:T(8,128)S(1)} %add_add_fusion.2.vector_ref.refs_1_), channel_id=1, source_target_pairs={{0,56},{8,16},{16,8},{24,32},{32,24},{40,48},{48,40},{56,0},{1,57}... | collective-permute-start | bytes 98312 | tf_op jit(solution)/shard_map/ppermute | solution.py:27
  21.9 4.9 %collective-permute-start.6 = (f32[16,512]{1,0:T(8,128)S(1)}, f32[16,512]{1,0:T(8,128)S(1)}, u32[]{:S(2)}, u32[]{:S(2)}) collective-permute-start(f32[16,512]{1,0:T(8,128)S(1)} %add_add_fusion.2.vector_ref.refs_1_), channel_id=1, source_target_pairs={{0,1},{1,0},{2,3},{3,2},{4,5},{5,4},{6,7},{7,6},{8,9},{9,8},{10,11... | collective-permute-start | bytes 98312 | tf_op jit(solution)/shard_map/ppermute | solution.py:27
  21.9 5.1 %collective-permute-start.7 = (f32[16,512]{1,0:T(8,128)S(1)}, f32[16,512]{1,0:T(8,128)S(1)}, u32[]{:S(2)}, u32[]{:S(2)}) collective-permute-start(f32[16,512]{1,0:T(8,128)S(1)} %add_add_fusion.2.vector_ref.refs_1_), channel_id=1, source_target_pairs={{0,7},{1,2},{2,1},{3,4},{4,3},{5,6},{6,5},{7,0},{8,15},{9,10},{10,... | collective-permute-start | bytes 98312 | tf_op jit(solution)/shard_map/ppermute | solution.py:27
  28.0 4.7 %collective-permute-start.12 = (f32[16,512]{1,0:T(8,128)S(1)}, f32[16,512]{1,0:T(8,128)S(1)}, u32[]{:S(2)}, u32[]{:S(2)}) collective-permute-start(f32[16,512]{1,0:T(8,128)S(1)} %get-tuple-element.58), channel_id=1, source_target_pairs={{0,64},{64,0},{128,192},{192,128},{1,65},{65,1},{129,193},{193,129... | collective-permute-start | bytes 98312 | tf_op jit(solution)/shard_map/ppermute | solution.py:27
  29.8 4.6 %collective-permute-start.13 = (f32[16,512]{1,0:T(8,128)S(1)}, f32[16,512]{1,0:T(8,128)S(1)}, u32[]{:S(2)}, u32[]{:S(2)}) collective-permute-start(f32[16,512]{1,0:T(8,128)S(1)} %get-tuple-element.59), channel_id=1, source_target_pairs={{0,192},{64,128},{128,64},{192,0},{1,193},{65,129},{129,65},{193,1... | collective-permute-start | bytes 98312 | tf_op jit(solution)/shard_map/ppermute | solution.py:27
  32.7 5.1 %collective-permute-start.17 = (f32[16,512]{1,0:T(8,128)S(1)}, f32[16,512]{1,0:T(8,128)S(1)}, u32[]{:S(2)}, u32[]{:S(2)}) collective-permute-start(f32[16,512]{1,0:T(8,128)S(1)} %get-tuple-element.63), channel_id=1, source_target_pairs={{0,7},{1,2},{2,1},{3,4},{4,3},{5,6},{6,5},{7,0},{8,15},{9,10},{10,... | collective-permute-start | bytes 98312 | tf_op jit(solution)/shard_map/ppermute | solution.py:27
  42.7 5.1 %collective-permute-start.23 = (f32[16,512]{1,0:T(8,128)S(1)}, f32[16,512]{1,0:T(8,128)S(1)}, u32[]{:S(2)}, u32[]{:S(2)}) collective-permute-start(f32[16,512]{1,0:T(8,128)S(1)} %get-tuple-element.70), channel_id=1, source_target_pairs={{0,7},{1,2},{2,1},{3,4},{4,3},{5,6},{6,5},{7,0},{8,15},{9,10},{10,... | collective-permute-start | bytes 98312 | tf_op jit(solution)/shard_map/ppermute | solution.py:27
  49.3 4.8 %collective-permute-start.27 = (f32[16,512]{1,0:T(8,128)S(1)}, f32[16,512]{1,0:T(8,128)S(1)}, u32[]{:S(2)}, u32[]{:S(2)}) collective-permute-start(f32[16,512]{1,0:T(8,128)S(1)} %add_add_fusion.1.vector_ref.refs_2_), channel_id=1, source_target_pairs={{0,192},{64,128},{128,64},{192,0},{1,193},{65,129},{129,65},{193,1... | collective-permute-start | bytes 98312 | tf_op jit(solution)/shard_map/ppermute | solution.py:27
  51.0 4.6 %collective-permute-start.24 = (f32[16,512]{1,0:T(8,128)S(1)}, f32[16,512]{1,0:T(8,128)S(1)}, u32[]{:S(2)}, u32[]{:S(2)}) collective-permute-start(f32[16,512]{1,0:T(8,128)S(1)} %add_add_fusion.1.vector_ref.refs_2_), channel_id=1, source_target_pairs={{0,1},{1,0},{2,3},{3,2},{4,5},{5,4},{6,7},{7,6},{8,9},{9,8},{10,11... | collective-permute-start | bytes 98312 | tf_op jit(solution)/shard_map/ppermute | solution.py:27
  51.8 5.1 %collective-permute-start.25 = (f32[16,512]{1,0:T(8,128)S(1)}, f32[16,512]{1,0:T(8,128)S(1)}, u32[]{:S(2)}, u32[]{:S(2)}) collective-permute-start(f32[16,512]{1,0:T(8,128)S(1)} %add_add_fusion.1.vector_ref.refs_2_), channel_id=1, source_target_pairs={{0,7},{1,2},{2,1},{3,4},{4,3},{5,6},{6,5},{7,0},{8,15},{9,10},{10,... | collective-permute-start | bytes 98312 | tf_op jit(solution)/shard_map/ppermute | solution.py:27
  62.0 5.1 %collective-permute-start.35 = (f32[16,512]{1,0:T(8,128)S(1)}, f32[16,512]{1,0:T(8,128)S(1)}, u32[]{:S(2)}, u32[]{:S(2)}) collective-permute-start(f32[16,512]{1,0:T(8,128)S(1)} %get-tuple-element.77), channel_id=1, source_target_pairs={{0,7},{1,2},{2,1},{3,4},{4,3},{5,6},{6,5},{7,0},{8,15},{9,10},{10,... | collective-permute-start | bytes 98312 | tf_op jit(solution)/shard_map/ppermute | solution.py:27
  67.9 4.6 %collective-permute-start.36 = (f32[16,512]{1,0:T(8,128)S(1)}, f32[16,512]{1,0:T(8,128)S(1)}, u32[]{:S(2)}, u32[]{:S(2)}) collective-permute-start(f32[16,512]{1,0:T(8,128)S(1)} %get-tuple-element.79), channel_id=1, source_target_pairs={{0,64},{64,0},{128,192},{192,128},{1,65},{65,1},{129,193},{193,129... | collective-permute-start | bytes 98312 | tf_op jit(solution)/shard_map/ppermute | solution.py:27
  69.6 4.6 %collective-permute-start.37 = (f32[16,512]{1,0:T(8,128)S(1)}, f32[16,512]{1,0:T(8,128)S(1)}, u32[]{:S(2)}, u32[]{:S(2)}) collective-permute-start(f32[16,512]{1,0:T(8,128)S(1)} %get-tuple-element.80), channel_id=1, source_target_pairs={{0,192},{64,128},{128,64},{192,0},{1,193},{65,129},{129,65},{193,1... | collective-permute-start | bytes 98312 | tf_op jit(solution)/shard_map/ppermute | solution.py:27
  72.5 5.1 %collective-permute-start.41 = (f32[16,512]{1,0:T(8,128)S(1)}, f32[16,512]{1,0:T(8,128)S(1)}, u32[]{:S(2)}, u32[]{:S(2)}) collective-permute-start(f32[16,512]{1,0:T(8,128)S(1)} %get-tuple-element.84), channel_id=1, source_target_pairs={{0,7},{1,2},{2,1},{3,4},{4,3},{5,6},{6,5},{7,0},{8,15},{9,10},{10,... | collective-permute-start | bytes 98312 | tf_op jit(solution)/shard_map/ppermute | solution.py:27
  79.1 4.8 %collective-permute-start.45 = (f32[16,512]{1,0:T(8,128)S(1)}, f32[16,512]{1,0:T(8,128)S(1)}, u32[]{:S(2)}, u32[]{:S(2)}) collective-permute-start(f32[16,512]{1,0:T(8,128)S(1)} %add_add_fusion.vector_ref.refs_3_), channel_id=1, source_target_pairs={{0,192},{64,128},{128,64},{192,0},{1,193},{65,129},{129,65},{193,1... | collective-permute-start | bytes 98312 | tf_op jit(solution)/shard_map/ppermute | solution.py:27
  81.7 5.1 %collective-permute-start.43 = (f32[16,512]{1,0:T(8,128)S(1)}, f32[16,512]{1,0:T(8,128)S(1)}, u32[]{:S(2)}, u32[]{:S(2)}) collective-permute-start(f32[16,512]{1,0:T(8,128)S(1)} %add_add_fusion.vector_ref.refs_3_), channel_id=1, source_target_pairs={{0,7},{1,2},{2,1},{3,4},{4,3},{5,6},{6,5},{7,0},{8,15},{9,10},{10,... | collective-permute-start | bytes 98312 | tf_op jit(solution)/shard_map/ppermute | solution.py:27
  92.0 5.1 %collective-permute-start.53 = (f32[16,512]{1,0:T(8,128)S(1)}, f32[16,512]{1,0:T(8,128)S(1)}, u32[]{:S(2)}, u32[]{:S(2)}) collective-permute-start(f32[16,512]{1,0:T(8,128)S(1)} %get-tuple-element.91), channel_id=1, source_target_pairs={{0,7},{1,2},{2,1},{3,4},{4,3},{5,6},{6,5},{7,0},{8,15},{9,10},{10,... | collective-permute-start | bytes 98312 | tf_op jit(solution)/shard_map/ppermute | solution.py:27
  (34 other events, 149.1 us)

commit v3 on v2

--- a/solution.py
+++ b/solution.py
@@ -2,6 +2,7 @@
 
 import jax
 import jax.numpy as jnp
+import numpy as np
 from jax import lax
 from jax.experimental import pallas as pl
 from jax.experimental.pallas import tpu as pltpu
@@ -11,24 +12,36 @@
 EPSILON = 1e-06
 SCALE = 2.0**-12
 AXES = ("gx", "gy", "gz")
-EARLY = (0, 1, 2, 3)
-LATE = (4, 5)
+ASIDE = (1, 2, 1)
+ORDER = (4, 5, 0, 1, 3, 2)
+EARLY = ORDER[:4]
+LATE = ORDER[4:]
 HOLD = True
 BF16 = jnp.bfloat16
 F32 = jnp.float32
 VMEM = pltpu.VMEM
 
 
-def swap(array, axis, start):
-    n = lax.axis_size(axis)
+def partners(slot):
+    dim = slot // 2
+    sizes = [lax.axis_size(axis) for axis in AXES]
     pairs = []
-    for i in range(start, n + start, 2):
-        pairs += [(i % n, (i + 1) % n), ((i + 1) % n, i % n)]
-    return lax.ppermute(array, axis, sorted(pairs))
+    for place in np.ndindex(*sizes):
+        at = list(place)
+        step = 1 if (at[dim] - slot) % 2 == 0 else -1
+        if 0 <= at[dim] + step < sizes[dim]:
+            at[dim] += step
+        else:
+            beside = ASIDE[dim]
+            at[beside] += 1 - 2 * (at[beside] % 2)
+        pairs.append(
+            tuple(int(np.ravel_multi_index(position, sizes)) for position in (place, at))
+        )
+    return pairs
 
 
 def trade(slots):
-    return [swap(slots[slot], AXES[slot // 2], slot % 2) for slot in range(6)]
+    return [lax.ppermute(slots[slot], AXES, partners(slot)) for slot in range(6)]
 
 
 def even_at(dim):
@@ -344,8 +357,8 @@
             (own,) = call(hold_kernel, (own, schur), (block,), "hold")
         got = trade(slots)
         direction = own
-        for part in got:
-            direction = direction + part
+        for slot in ORDER:
+            direction = direction + got[slot]
         directions.append(direction)
         got = trade([direction] * 6)
         (total,) = call(own_rows_kernel, (direction, schur), (wide,), "own_rows")
@@ -364,10 +377,13 @@
         got = trade(slots)
         if section + 1 < ITERS:
             vector, own, *slots = call(
-                next_kernel, (own, *got, picks, restricted), (block,) * 8, "next"
+                next_kernel,
+                (own, *[got[slot] for slot in ORDER], picks, restricted),
+                (block,) * 8,
+                "next",
             )
             basis.append(vector)
-    (gram,) = call(gram_kernel, (own, *got, *basis), (((rows // 2, 128), F32),), "gram")
+    (gram,) = call(gram_kernel, (own, *[got[slot] for slot in ORDER], *basis), (((rows // 2, 128), F32),), "gram")
     gram = all_sum(gram, (("gx", "gy"), "gz"))
     adjoint, ratio = call(
         last_kernel, (gram, *directions), (block, ((1, rows), F32)), "last", keep=False

time: 125 us -> 111 us (0.89)
  waiting for transfers between devices: 22.7 us -> 11.9 us
  starting transfers between devices: 56.8 us -> 52.1 us
    ppermute x54, waiting for transfers between devices: 22.7 us -> 11.9 us  [trade(): lax.ppermute(slots[slot], AXES, partners(slot))]
    ppermute x54, starting transfers between devices: 56.8 us -> 52.1 us  [trade(): lax.ppermute(slots[slot], AXES, partners(slot))]
  transfers between devices with their start and end apart: 54 -> 54, of which waited for: 17 -> 16; matrix products, arithmetic and copies ran while one was open for 0% -> 0% of each run, Pallas kernels for 5% -> 6%
where the time goes in v3:
time: 111 us; the launch traced here: 109 us
  starting transfers between devices  52.1 us (47%)
  blocking collectives  24.8 us (22%)
  Pallas kernels  15.6 us (14%)
  waiting for transfers between devices  11.9 us (11%)
  local copies, waits for them, and re-layouts  3.41 us (3%)
    ppermute x54, starting transfers between devices, trade(): lax.ppermute(slots[slot], AXES, partners(slot))  52.1 us
    all_to_all x2, blocking collectives, all_sum(): array = jnp.sum(lax.all_to_all(spread, axis, 0, 0), axis=0)  24.8 us
    pallas_call x15, Pallas kernels, call(): pl.pallas_call(kernel, out_shape=tuple((make(shape, dtype) for shape, dty...  15.6 us
    ppermute x54, waiting for transfers between devices, trade(): lax.ppermute(slots[slot], AXES, partners(slot))  11.9 us
    unnamed x8, local copies, waits for them, and re-layouts  3.39 us
  transfers between devices with their start and end apart: 54, of which 16 were waited for; matrix products, arithmetic and copies ran while one was open for 0% of the time, Pallas kernels for 6%

profile of v3, /device:TPU:10, one launch (start us, length us, event | category | flops | bytes accessed | tf_op | source)
XLA Modules:
  0.0 108.8 jit_solution(15984139175704754827)
XLA Ops:
  0.6 2.6 %first.1 = (bf16[6,512,256]{2,1,0:T(8,128)(2,1)S(1)}, f32[16,512]{1,0:T(8,128)S(1)}, f32[16,512]{1,0:T(8,128)S(1)}, f32[16,512]{1,0:T(8,128)S(1)}, f32[16,512]{1...) custom-call(s32[6,1,256]{2,1,0:T(1,128)} %bitcast.21, f32[16,512]{1,0:T(8,128)} %bitcast.19, ...), custom_call_target="tpu_custom_call" | custom-call | bytes 2136064 | tf_op jit(solution)/shard_map/first/pallas_call | solution.py:307
  3.2 2.0 %collective-permute-start = (f32[16,512]{1,0:T(8,128)S(1)}, f32[16,512]{1,0:T(8,128)S(1)}, u32[]{:S(2)}, u32[]{:S(2)}) collective-permute-start(f32[16,512]{1,0:T(8,128)S(1)} %get-tuple-element.50), channel_id=1, source_target_pairs={{0,1},{1,0},{2,3},{3,2},{4,5},{5,4},{6,7},{7,6},{8,9},{9,8},{10,11... | collective-permute-start | bytes 98312 | tf_op jit(solution)/shard_map/ppermute | solution.py:44
  5.7 2.4 %collective-permute-start.3 = (f32[16,512]{1,0:T(8,128)S(1)}, f32[16,512]{1,0:T(8,128)S(1)}, u32[]{:S(2)}, u32[]{:S(2)}) collective-permute-start(f32[16,512]{1,0:T(8,128)S(1)} %get-tuple-element.53), channel_id=1, source_target_pairs={{0,8},{1,9},{2,10},{3,11},{4,12},{5,13},{6,14},{7,15},{8,0},{9,1},... | collective-permute-start | bytes 98312 | tf_op jit(solution)/shard_map/ppermute | solution.py:44
  8.2 1.5 %collective-permute-start.5 = (f32[16,512]{1,0:T(8,128)S(1)}, f32[16,512]{1,0:T(8,128)S(1)}, u32[]{:S(2)}, u32[]{:S(2)}) collective-permute-start(f32[16,512]{1,0:T(8,128)S(1)} %get-tuple-element.55), channel_id=1, source_target_pairs={{0,8},{1,9},{2,10},{3,11},{4,12},{5,13},{6,14},{7,15},{8,0},{9,1},... | collective-permute-start | bytes 98312 | tf_op jit(solution)/shard_map/ppermute | solution.py:44
  9.7 3.4 %copy-done = bf16[1,1,1,2048,2048]{4,3,2,1,0:T(8,128)(2,1)S(1)} copy-done((bf16[1,1,1,2048,2048]{4,3,2,1,0:T(8,128)(2,1)S(1)}, bf16[1,1,1,2048,2048]{4,3,2,1,0:T(8,128)(2,1)}, u32[]{:S(2)}) %copy-start) | copy-done | bytes 8388632
  14.2 3.6 %collective-permute-start.8 = (f32[16,512]{1,0:T(8,128)S(1)}, f32[16,512]{1,0:T(8,128)S(1)}, u32[]{:S(2)}, u32[]{:S(2)}) collective-permute-start(f32[16,512]{1,0:T(8,128)S(1)} %add_add_fusion.2.vector_ref.refs_1_), channel_id=1, source_target_pairs={{0,1},{1,0},{2,3},{3,2},{4,5},{5,4},{6,7},{7,6},{8,9},{9,8},{10,11... | collective-permute-start | bytes 98312 | tf_op jit(solution)/shard_map/ppermute | solution.py:44
  19.7 1.4 %some_rows.3.refs_2_ = f32[32,2048]{1,0:T(8,128)S(1)} custom-call(f32[16,512]{1,0:T(8,128)S(1)} %collective-permute-done.8.refs_0_, f32[16,512]{1,0:T(8,128)S(1)} %collective-permute-done.9.refs_1_, f32[16,512]{1,0:T(8,128)S(1)} %collective-permute-done.10.refs_2_, f32[16,512]{1,0:T(8,128)S(1)} %collective-permute-done.11.refs_3_, ...), custom_call_target="tpu_custom_call" | custom-call | bytes 10354688 | tf_op jit(solution)/shard_map/some_rows/pallas_call | solution.py:307
  22.3 4.2 %collective-permute-start.12 = (f32[16,512]{1,0:T(8,128)S(1)}, f32[16,512]{1,0:T(8,128)S(1)}, u32[]{:S(2)}, u32[]{:S(2)}) collective-permute-start(f32[16,512]{1,0:T(8,128)S(1)} %get-tuple-element.58), channel_id=1, source_target_pairs={{0,1},{1,0},{2,3},{3,2},{4,5},{5,4},{6,7},{7,6},{8,9},{9,8},{10,11... | collective-permute-start | bytes 98312 | tf_op jit(solution)/shard_map/ppermute | solution.py:44
  32.5 3.2 %collective-permute-start.18 = (f32[16,512]{1,0:T(8,128)S(1)}, f32[16,512]{1,0:T(8,128)S(1)}, u32[]{:S(2)}, u32[]{:S(2)}) collective-permute-start(f32[16,512]{1,0:T(8,128)S(1)} %get-tuple-element.65), channel_id=1, source_target_pairs={{0,1},{1,0},{2,3},{3,2},{4,5},{5,4},{6,7},{7,6},{8,9},{9,8},{10,11... | collective-permute-start | bytes 98312 | tf_op jit(solution)/shard_map/ppermute | solution.py:44
  40.9 2.0 %collective-permute-start.26 = (f32[16,512]{1,0:T(8,128)S(1)}, f32[16,512]{1,0:T(8,128)S(1)}, u32[]{:S(2)}, u32[]{:S(2)}) collective-permute-start(f32[16,512]{1,0:T(8,128)S(1)} %add_add_fusion.1.vector_ref.refs_2_), channel_id=1, source_target_pairs={{0,1},{1,0},{2,3},{3,2},{4,5},{5,4},{6,7},{7,6},{8,9},{9,8},{10,11... | collective-permute-start | bytes 98312 | tf_op jit(solution)/shard_map/ppermute | solution.py:44
  43.6 1.4 %collective-permute-start.29 = (f32[16,512]{1,0:T(8,128)S(1)}, f32[16,512]{1,0:T(8,128)S(1)}, u32[]{:S(2)}, u32[]{:S(2)}) collective-permute-start(f32[16,512]{1,0:T(8,128)S(1)} %add_add_fusion.1.vector_ref.refs_2_), channel_id=1, source_target_pairs={{0,8},{1,9},{2,10},{3,11},{4,12},{5,13},{6,14},{7,15},{8,0},{9,1},... | collective-permute-start | bytes 98312 | tf_op jit(solution)/shard_map/ppermute | solution.py:44
  47.5 1.4 %some_rows.4.refs_2_ = f32[32,2048]{1,0:T(8,128)S(1)} custom-call(f32[16,512]{1,0:T(8,128)S(1)} %collective-permute-done.26.refs_0_, f32[16,512]{1,0:T(8,128)S(1)} %collective-permute-done.27.refs_1_, f32[16,512]{1,0:T(8,128)S(1)} %collective-permute-done.28.refs_2_, f32[16,512]{1,0:T(8,128)S(1)} %collective-permute-done.29.refs_3_, ...), custom_call_target="tpu_custom_call" | custom-call | bytes 10354688 | tf_op jit(solution)/shard_map/some_rows/pallas_call | solution.py:307
  50.0 1.8 %collective-permute-start.30 = (f32[16,512]{1,0:T(8,128)S(1)}, f32[16,512]{1,0:T(8,128)S(1)}, u32[]{:S(2)}, u32[]{:S(2)}) collective-permute-start(f32[16,512]{1,0:T(8,128)S(1)} %get-tuple-element.72), channel_id=1, source_target_pairs={{0,1},{1,0},{2,3},{3,2},{4,5},{5,4},{6,7},{7,6},{8,9},{9,8},{10,11... | collective-permute-start | bytes 98312 | tf_op jit(solution)/shard_map/ppermute | solution.py:44
  53.3 1.5 %collective-permute-start.34 = (f32[16,512]{1,0:T(8,128)S(1)}, f32[16,512]{1,0:T(8,128)S(1)}, u32[]{:S(2)}, u32[]{:S(2)}) collective-permute-start(f32[16,512]{1,0:T(8,128)S(1)} %get-tuple-element.76), channel_id=1, source_target_pairs={{0,1},{1,0},{2,3},{3,2},{4,5},{5,4},{6,7},{7,6},{8,16},{9,17},{10,... | collective-permute-start | bytes 98312 | tf_op jit(solution)/shard_map/ppermute | solution.py:44
  57.5 2.3 %collective-permute-start.36 = (f32[16,512]{1,0:T(8,128)S(1)}, f32[16,512]{1,0:T(8,128)S(1)}, u32[]{:S(2)}, u32[]{:S(2)}) collective-permute-start(f32[16,512]{1,0:T(8,128)S(1)} %get-tuple-element.79), channel_id=1, source_target_pairs={{0,1},{1,0},{2,3},{3,2},{4,5},{5,4},{6,7},{7,6},{8,9},{9,8},{10,11... | collective-permute-start | bytes 98312 | tf_op jit(solution)/shard_map/ppermute | solution.py:44
  60.6 1.4 %collective-permute-start.39 = (f32[16,512]{1,0:T(8,128)S(1)}, f32[16,512]{1,0:T(8,128)S(1)}, u32[]{:S(2)}, u32[]{:S(2)}) collective-permute-start(f32[16,512]{1,0:T(8,128)S(1)} %get-tuple-element.82), channel_id=1, source_target_pairs={{0,8},{1,9},{2,10},{3,11},{4,12},{5,13},{6,14},{7,15},{8,0},{9,1},... | collective-permute-start | bytes 98312 | tf_op jit(solution)/shard_map/ppermute | solution.py:44
  62.1 1.6 %collective-permute-start.40 = (f32[16,512]{1,0:T(8,128)S(1)}, f32[16,512]{1,0:T(8,128)S(1)}, u32[]{:S(2)}, u32[]{:S(2)}) collective-permute-start(f32[16,512]{1,0:T(8,128)S(1)} %get-tuple-element.83), channel_id=1, source_target_pairs={{0,1},{1,0},{2,3},{3,2},{4,5},{5,4},{6,7},{7,6},{8,16},{9,17},{10,... | collective-permute-start | bytes 98312 | tf_op jit(solution)/shard_map/ppermute | solution.py:44
  65.4 2.1 %collective-permute-start.44 = (f32[16,512]{1,0:T(8,128)S(1)}, f32[16,512]{1,0:T(8,128)S(1)}, u32[]{:S(2)}, u32[]{:S(2)}) collective-permute-start(f32[16,512]{1,0:T(8,128)S(1)} %add_add_fusion.vector_ref.refs_3_), channel_id=1, source_target_pairs={{0,1},{1,0},{2,3},{3,2},{4,5},{5,4},{6,7},{7,6},{8,9},{9,8},{10,11... | collective-permute-start | bytes 98312 | tf_op jit(solution)/shard_map/ppermute | solution.py:44
  68.6 2.0 %collective-permute-start.42 = (f32[16,512]{1,0:T(8,128)S(1)}, f32[16,512]{1,0:T(8,128)S(1)}, u32[]{:S(2)}, u32[]{:S(2)}) collective-permute-start(f32[16,512]{1,0:T(8,128)S(1)} %add_add_fusion.vector_ref.refs_3_), channel_id=1, source_target_pairs={{0,1},{1,0},{2,3},{3,2},{4,5},{5,4},{6,7},{7,6},{8,16},{9,17},{10,... | collective-permute-start | bytes 98312 | tf_op jit(solution)/shard_map/ppermute | solution.py:44
  72.0 1.4 %some_rows.5.refs_2_ = f32[32,2048]{1,0:T(8,128)S(1)} custom-call(f32[16,512]{1,0:T(8,128)S(1)} %collective-permute-done.44.refs_0_, f32[16,512]{1,0:T(8,128)S(1)} %collective-permute-done.45.refs_1_, f32[16,512]{1,0:T(8,128)S(1)} %collective-permute-done.46.refs_2_, f32[16,512]{1,0:T(8,128)S(1)} %collective-permute-done.47.refs_3_, ...), custom_call_target="tpu_custom_call" | custom-call | bytes 10354688 | tf_op jit(solution)/shard_map/some_rows/pallas_call | solution.py:307
  74.5 2.0 %collective-permute-start.48 = (f32[16,512]{1,0:T(8,128)S(1)}, f32[16,512]{1,0:T(8,128)S(1)}, u32[]{:S(2)}, u32[]{:S(2)}) collective-permute-start(f32[16,512]{1,0:T(8,128)S(1)} %get-tuple-element.86), channel_id=1, source_target_pairs={{0,1},{1,0},{2,3},{3,2},{4,5},{5,4},{6,7},{7,6},{8,9},{9,8},{10,11... | collective-permute-start | bytes 98312 | tf_op jit(solution)/shard_map/ppermute | solution.py:44
  81.9 12.0 %all_to_all.10 = f32[32,8,128]{2,1,0:T(8,128)S(1)} all-to-all(f32[32,8,128]{2,1,0:T(8,128)S(1)} %broadcast_in_dim.6), channel_id=1, replica_groups=mesh['gx'=4,'gy'=8,'gz'=8] {'gx','gy'}, dimensions={0} | all-to-all | bytes 262144 | tf_op jit(solution)/shard_map/all_to_all | solution.py:327
  93.9 12.8 %all_to_all.11 = f32[8,8,128]{2,1,0:T(8,128)S(1)} all-to-all(f32[8,8,128]{2,1,0:T(8,128)S(1)} %broadcast_in_dim.7), channel_id=1, replica_groups=mesh['gx'=4,'gy'=8,'gz'=8] {'gz'}, dimensions={0} | all-to-all | bytes 65536 | tf_op jit(solution)/shard_map/all_to_all | solution.py:327
  106.8 2.0 %last.1 = (f32[16,512]{1,0:T(8,128)}, f32[1,16]{1,0:T(1,128)}) custom-call(f32[8,128]{1,0:T(8,128)S(1)} %reduce_sum.19.refs_0_, f32[16,512]{1,0:T(8,128)S(1)} %add_add_fusion.2.vector_ref.refs_1_, f32[16,512]{1,0:T(8,128)S(1)} %add_add_fusion.1.vector_ref.refs_2_, f32[16,512]{1,0:T(8,128)S(1)} %add_add_fusion.vector_ref.refs_3_), custom_call_target="tpu_custom_call" | custom-call | bytes 102400 | tf_op jit(solution)/shard_map/last/pallas_call | solution.py:307
  (116 shorter events, 35.7 us)
Async XLA Ops:
  3.2 5.0 %collective-permute-start = (f32[16,512]{1,0:T(8,128)S(1)}, f32[16,512]{1,0:T(8,128)S(1)}, u32[]{:S(2)}, u32[]{:S(2)}) collective-permute-start(f32[16,512]{1,0:T(8,128)S(1)} %get-tuple-element.50), channel_id=1, source_target_pairs={{0,1},{1,0},{2,3},{3,2},{4,5},{5,4},{6,7},{7,6},{8,9},{9,8},{10,11... | collective-permute-start | bytes 98312 | tf_op jit(solution)/shard_map/ppermute | solution.py:44
  5.2 7.9 %collective-permute-start.1 = (f32[16,512]{1,0:T(8,128)S(1)}, f32[16,512]{1,0:T(8,128)S(1)}, u32[]{:S(2)}, u32[]{:S(2)}) collective-permute-start(f32[16,512]{1,0:T(8,128)S(1)} %get-tuple-element.51), channel_id=1, source_target_pairs={{0,8},{1,2},{2,1},{3,4},{4,3},{5,6},{6,5},{7,15},{8,0},{9,10},{10,... | collective-permute-start | bytes 98312 | tf_op jit(solution)/shard_map/ppermute | solution.py:44
  5.2 7.9 %collective-permute-start.2 = (f32[16,512]{1,0:T(8,128)S(1)}, f32[16,512]{1,0:T(8,128)S(1)}, u32[]{:S(2)}, u32[]{:S(2)}) collective-permute-start(f32[16,512]{1,0:T(8,128)S(1)} %get-tuple-element.52), channel_id=1, source_target_pairs={{0,64},{1,65},{2,66},{3,67},{4,68},{5,69},{6,70},{7,71},{8,72},{9,... | collective-permute-start | bytes 98312 | tf_op jit(solution)/shard_map/ppermute | solution.py:44
  5.7 7.4 %collective-permute-start.3 = (f32[16,512]{1,0:T(8,128)S(1)}, f32[16,512]{1,0:T(8,128)S(1)}, u32[]{:S(2)}, u32[]{:S(2)}) collective-permute-start(f32[16,512]{1,0:T(8,128)S(1)} %get-tuple-element.53), channel_id=1, source_target_pairs={{0,8},{1,9},{2,10},{3,11},{4,12},{5,13},{6,14},{7,15},{8,0},{9,1},... | collective-permute-start | bytes 98312 | tf_op jit(solution)/shard_map/ppermute | solution.py:44
  8.1 5.0 %collective-permute-start.4 = (f32[16,512]{1,0:T(8,128)S(1)}, f32[16,512]{1,0:T(8,128)S(1)}, u32[]{:S(2)}, u32[]{:S(2)}) collective-permute-start(f32[16,512]{1,0:T(8,128)S(1)} %get-tuple-element.54), channel_id=1, source_target_pairs={{0,1},{1,0},{2,3},{3,2},{4,5},{5,4},{6,7},{7,6},{8,16},{9,17},{10,... | collective-permute-start | bytes 98312 | tf_op jit(solution)/shard_map/ppermute | solution.py:44
  8.2 5.0 %collective-permute-start.5 = (f32[16,512]{1,0:T(8,128)S(1)}, f32[16,512]{1,0:T(8,128)S(1)}, u32[]{:S(2)}, u32[]{:S(2)}) collective-permute-start(f32[16,512]{1,0:T(8,128)S(1)} %get-tuple-element.55), channel_id=1, source_target_pairs={{0,8},{1,9},{2,10},{3,11},{4,12},{5,13},{6,14},{7,15},{8,0},{9,1},... | collective-permute-start | bytes 98312 | tf_op jit(solution)/shard_map/ppermute | solution.py:44
  13.1 5.3 %collective-permute-start.10 = (f32[16,512]{1,0:T(8,128)S(1)}, f32[16,512]{1,0:T(8,128)S(1)}, u32[]{:S(2)}, u32[]{:S(2)}) collective-permute-start(f32[16,512]{1,0:T(8,128)S(1)} %add_add_fusion.2.vector_ref.refs_1_), channel_id=1, source_target_pairs={{0,64},{1,65},{2,66},{3,67},{4,68},{5,69},{6,70},{7,71},{8,72},{9,... | collective-permute-start | bytes 98312 | tf_op jit(solution)/shard_map/ppermute | solution.py:44
  13.2 6.5 %collective-permute-start.11 = (f32[16,512]{1,0:T(8,128)S(1)}, f32[16,512]{1,0:T(8,128)S(1)}, u32[]{:S(2)}, u32[]{:S(2)}) collective-permute-start(f32[16,512]{1,0:T(8,128)S(1)} %add_add_fusion.2.vector_ref.refs_1_), channel_id=1, source_target_pairs={{0,8},{1,9},{2,10},{3,11},{4,12},{5,13},{6,14},{7,15},{8,0},{9,1},... | collective-permute-start | bytes 98312 | tf_op jit(solution)/shard_map/ppermute | solution.py:44
  14.2 5.5 %collective-permute-start.8 = (f32[16,512]{1,0:T(8,128)S(1)}, f32[16,512]{1,0:T(8,128)S(1)}, u32[]{:S(2)}, u32[]{:S(2)}) collective-permute-start(f32[16,512]{1,0:T(8,128)S(1)} %add_add_fusion.2.vector_ref.refs_1_), channel_id=1, source_target_pairs={{0,1},{1,0},{2,3},{3,2},{4,5},{5,4},{6,7},{7,6},{8,9},{9,8},{10,11... | collective-permute-start | bytes 98312 | tf_op jit(solution)/shard_map/ppermute | solution.py:44
  22.3 6.5 %collective-permute-start.12 = (f32[16,512]{1,0:T(8,128)S(1)}, f32[16,512]{1,0:T(8,128)S(1)}, u32[]{:S(2)}, u32[]{:S(2)}) collective-permute-start(f32[16,512]{1,0:T(8,128)S(1)} %get-tuple-element.58), channel_id=1, source_target_pairs={{0,1},{1,0},{2,3},{3,2},{4,5},{5,4},{6,7},{7,6},{8,9},{9,8},{10,11... | collective-permute-start | bytes 98312 | tf_op jit(solution)/shard_map/ppermute | solution.py:44
  26.5 3.9 %collective-permute-start.14 = (f32[16,512]{1,0:T(8,128)S(1)}, f32[16,512]{1,0:T(8,128)S(1)}, u32[]{:S(2)}, u32[]{:S(2)}) collective-permute-start(f32[16,512]{1,0:T(8,128)S(1)} %get-tuple-element.60), channel_id=1, source_target_pairs={{0,64},{1,65},{2,66},{3,67},{4,68},{5,69},{6,70},{7,71},{8,72},{9,... | collective-permute-start | bytes 98312 | tf_op jit(solution)/shard_map/ppermute | solution.py:44
  27.8 3.9 %collective-permute-start.15 = (f32[16,512]{1,0:T(8,128)S(1)}, f32[16,512]{1,0:T(8,128)S(1)}, u32[]{:S(2)}, u32[]{:S(2)}) collective-permute-start(f32[16,512]{1,0:T(8,128)S(1)} %get-tuple-element.61), channel_id=1, source_target_pairs={{0,8},{1,9},{2,10},{3,11},{4,12},{5,13},{6,14},{7,15},{8,0},{9,1},... | collective-permute-start | bytes 98312 | tf_op jit(solution)/shard_map/ppermute | solution.py:44
  32.5 6.3 %collective-permute-start.18 = (f32[16,512]{1,0:T(8,128)S(1)}, f32[16,512]{1,0:T(8,128)S(1)}, u32[]{:S(2)}, u32[]{:S(2)}) collective-permute-start(f32[16,512]{1,0:T(8,128)S(1)} %get-tuple-element.65), channel_id=1, source_target_pairs={{0,1},{1,0},{2,3},{3,2},{4,5},{5,4},{6,7},{7,6},{8,9},{9,8},{10,11... | collective-permute-start | bytes 98312 | tf_op jit(solution)/shard_map/ppermute | solution.py:44
  35.8 3.9 %collective-permute-start.20 = (f32[16,512]{1,0:T(8,128)S(1)}, f32[16,512]{1,0:T(8,128)S(1)}, u32[]{:S(2)}, u32[]{:S(2)}) collective-permute-start(f32[16,512]{1,0:T(8,128)S(1)} %get-tuple-element.67), channel_id=1, source_target_pairs={{0,64},{1,65},{2,66},{3,67},{4,68},{5,69},{6,70},{7,71},{8,72},{9,... | collective-permute-start | bytes 98312 | tf_op jit(solution)/shard_map/ppermute | solution.py:44
  36.2 3.9 %collective-permute-start.21 = (f32[16,512]{1,0:T(8,128)S(1)}, f32[16,512]{1,0:T(8,128)S(1)}, u32[]{:S(2)}, u32[]{:S(2)}) collective-permute-start(f32[16,512]{1,0:T(8,128)S(1)} %get-tuple-element.68), channel_id=1, source_target_pairs={{0,8},{1,9},{2,10},{3,11},{4,12},{5,13},{6,14},{7,15},{8,0},{9,1},... | collective-permute-start | bytes 98312 | tf_op jit(solution)/shard_map/ppermute | solution.py:44
  40.9 5.1 %collective-permute-start.26 = (f32[16,512]{1,0:T(8,128)S(1)}, f32[16,512]{1,0:T(8,128)S(1)}, u32[]{:S(2)}, u32[]{:S(2)}) collective-permute-start(f32[16,512]{1,0:T(8,128)S(1)} %add_add_fusion.1.vector_ref.refs_2_), channel_id=1, source_target_pairs={{0,1},{1,0},{2,3},{3,2},{4,5},{5,4},{6,7},{7,6},{8,9},{9,8},{10,11... | collective-permute-start | bytes 98312 | tf_op jit(solution)/shard_map/ppermute | solution.py:44
  42.9 4.1 %collective-permute-start.27 = (f32[16,512]{1,0:T(8,128)S(1)}, f32[16,512]{1,0:T(8,128)S(1)}, u32[]{:S(2)}, u32[]{:S(2)}) collective-permute-start(f32[16,512]{1,0:T(8,128)S(1)} %add_add_fusion.1.vector_ref.refs_2_), channel_id=1, source_target_pairs={{0,8},{1,2},{2,1},{3,4},{4,3},{5,6},{6,5},{7,15},{8,0},{9,10},{10,... | collective-permute-start | bytes 98312 | tf_op jit(solution)/shard_map/ppermute | solution.py:44
  42.9 4.1 %collective-permute-start.28 = (f32[16,512]{1,0:T(8,128)S(1)}, f32[16,512]{1,0:T(8,128)S(1)}, u32[]{:S(2)}, u32[]{:S(2)}) collective-permute-start(f32[16,512]{1,0:T(8,128)S(1)} %add_add_fusion.1.vector_ref.refs_2_), channel_id=1, source_target_pairs={{0,64},{1,65},{2,66},{3,67},{4,68},{5,69},{6,70},{7,71},{8,72},{9,... | collective-permute-start | bytes 98312 | tf_op jit(solution)/shard_map/ppermute | solution.py:44
  45.0 3.9 %collective-permute-start.24 = (f32[16,512]{1,0:T(8,128)S(1)}, f32[16,512]{1,0:T(8,128)S(1)}, u32[]{:S(2)}, u32[]{:S(2)}) collective-permute-start(f32[16,512]{1,0:T(8,128)S(1)} %add_add_fusion.1.vector_ref.refs_2_), channel_id=1, source_target_pairs={{0,1},{1,0},{2,3},{3,2},{4,5},{5,4},{6,7},{7,6},{8,16},{9,17},{10,... | collective-permute-start | bytes 98312 | tf_op jit(solution)/shard_map/ppermute | solution.py:44
  50.0 4.8 %collective-permute-start.30 = (f32[16,512]{1,0:T(8,128)S(1)}, f32[16,512]{1,0:T(8,128)S(1)}, u32[]{:S(2)}, u32[]{:S(2)}) collective-permute-start(f32[16,512]{1,0:T(8,128)S(1)} %get-tuple-element.72), channel_id=1, source_target_pairs={{0,1},{1,0},{2,3},{3,2},{4,5},{5,4},{6,7},{7,6},{8,9},{9,8},{10,11... | collective-permute-start | bytes 98312 | tf_op jit(solution)/shard_map/ppermute | solution.py:44
  57.5 6.1 %collective-permute-start.36 = (f32[16,512]{1,0:T(8,128)S(1)}, f32[16,512]{1,0:T(8,128)S(1)}, u32[]{:S(2)}, u32[]{:S(2)}) collective-permute-start(f32[16,512]{1,0:T(8,128)S(1)} %get-tuple-element.79), channel_id=1, source_target_pairs={{0,1},{1,0},{2,3},{3,2},{4,5},{5,4},{6,7},{7,6},{8,9},{9,8},{10,11... | collective-permute-start | bytes 98312 | tf_op jit(solution)/shard_map/ppermute | solution.py:44
  65.4 5.2 %collective-permute-start.44 = (f32[16,512]{1,0:T(8,128)S(1)}, f32[16,512]{1,0:T(8,128)S(1)}, u32[]{:S(2)}, u32[]{:S(2)}) collective-permute-start(f32[16,512]{1,0:T(8,128)S(1)} %add_add_fusion.vector_ref.refs_3_), channel_id=1, source_target_pairs={{0,1},{1,0},{2,3},{3,2},{4,5},{5,4},{6,7},{7,6},{8,9},{9,8},{10,11... | collective-permute-start | bytes 98312 | tf_op jit(solution)/shard_map/ppermute | solution.py:44
  68.6 4.8 %collective-permute-start.42 = (f32[16,512]{1,0:T(8,128)S(1)}, f32[16,512]{1,0:T(8,128)S(1)}, u32[]{:S(2)}, u32[]{:S(2)}) collective-permute-start(f32[16,512]{1,0:T(8,128)S(1)} %add_add_fusion.vector_ref.refs_3_), channel_id=1, source_target_pairs={{0,1},{1,0},{2,3},{3,2},{4,5},{5,4},{6,7},{7,6},{8,16},{9,17},{10,... | collective-permute-start | bytes 98312 | tf_op jit(solution)/shard_map/ppermute | solution.py:44
  74.5 4.9 %collective-permute-start.48 = (f32[16,512]{1,0:T(8,128)S(1)}, f32[16,512]{1,0:T(8,128)S(1)}, u32[]{:S(2)}, u32[]{:S(2)}) collective-permute-start(f32[16,512]{1,0:T(8,128)S(1)} %get-tuple-element.86), channel_id=1, source_target_pairs={{0,1},{1,0},{2,3},{3,2},{4,5},{5,4},{6,7},{7,6},{8,9},{9,8},{10,11... | collective-permute-start | bytes 98312 | tf_op jit(solution)/shard_map/ppermute | solution.py:44
  (34 other events, 124.6 us)

commit v4 on v3

v4 whole, which is shorter than its diff:
```python
import functools

import jax
import jax.numpy as jnp
import numpy as np
from jax import lax
from jax.experimental import pallas as pl
from jax.experimental.pallas import tpu as pltpu
from jax.sharding import PartitionSpec as P

ITERS = 3
EPSILON = 1e-06
SCALE = 2.0**-12
AXES = ("gx", "gy", "gz")
ASIDE = (1, 2, 1)
ORDER = (4, 5, 0, 1, 3, 2)
EARLY = (2, 0)
LATE = 1
BF16 = jnp.bfloat16
F32 = jnp.float32
VMEM = pltpu.VMEM


def partners(slot):
    dim = slot // 2
    sizes = [lax.axis_size(axis) for axis in AXES]
    pairs = []
    for place in np.ndindex(*sizes):
        at = list(place)
        step = 1 if (at[dim] - slot) % 2 == 0 else -1
        if 0 <= at[dim] + step < sizes[dim]:
            at[dim] += step
        else:
            beside = ASIDE[dim]
            at[beside] += 1 - 2 * (at[beside] % 2)
        pairs.append(
            tuple(int(np.ravel_multi_index(position, sizes)) for position in (place, at))
        )
    return pairs


def trade(slots):
    return [lax.ppermute(slots[slot], AXES, partners(slot)) for slot in range(6)]


def even_at(dim):
    return lax.rem(lax.axis_index(AXES[dim]), 2) == 0


def sides_of(pair, dim):
    even, odd = pair
    here = even_at(dim)
    return jnp.where(here, odd, even), jnp.where(here, even, odd)


def meets(slot):
    at = lax.axis_index(AXES[slot // 2])
    if slot % 2 == 0:
        return at >= 0
    return jnp.logical_and(at > 0, at < lax.axis_size(AXES[slot // 2]) - 1)


def split(x):
    high = x.astype(BF16)
    low = (x - high.astype(F32)).astype(BF16)
    return jnp.concatenate([high, low], axis=0)


def joined(x):
    rows = x.shape[0] // 2
    return x[:rows] + x[rows:]


def ordered(got):
    return [got[slot] for slot in ORDER]


def slot_order(got):
    return [got[ORDER.index(slot)] for slot in range(6)]


def by_slot(products):
    width = products.shape[1] // 6
    blocks = [products[:, face * width : (face + 1) * width] for face in range(6)]
    slots = []
    for dim in range(3):
        slots += sides_of((blocks[2 * dim], blocks[2 * dim + 1]), dim)
    return slots


def put_split(slots, refs):
    for block, ref in zip(slots, refs):
        ref[...] = split(block)


def first_kernel(*refs):
    sources, own_ref, slot_refs, scratch = refs[:3], refs[3], refs[4:10], refs[10:]
    maps_ref, vector_ref, restricted_ref, sems = scratch
    copies = [
        pltpu.make_async_copy(source, target, sems.at[i])
        for i, (source, target) in enumerate(zip(sources, scratch[:3]))
    ]
    for copy in copies:
        copy.start()
    for copy in copies:
        copy.wait()
    rows, owned = vector_ref.shape
    products = joined(
        jnp.dot(split(vector_ref[...]), restricted_ref[...], preferred_element_type=F32)
    )
    own_ref[...] = products[:, :owned]
    maps = jnp.concatenate([maps_ref[face].astype(F32) for face in range(6)], axis=1)
    maps = jnp.broadcast_to(maps, (8, maps.shape[1]))
    for block, row, ref in zip(by_slot(products[:, owned:]), by_slot(maps), slot_refs):
        ref[:rows] = block
        ref[rows:] = row


def added(slots, got, places_ref):
    width = got[0].shape[1]
    total = None
    for slot, part in zip(slots, got):
        place = places_ref[slot * width : (slot + 1) * width, :]
        product = jnp.dot(part[...], place, preferred_element_type=F32)
        total = product if total is None else total + product
    return joined(total)


def early_kernel(*refs):
    own_ref, got, places_ref, sum_ref = refs[0], refs[1:5], refs[5], refs[6]
    sum_ref[...] = own_ref[...] + added(ORDER[:4], got, places_ref)


def turn_kernel(*refs):
    got, places_ref = refs[:6], refs[7]
    width = got[0].shape[1]
    owned = places_ref.shape[1]
    place = lax.broadcasted_iota(jnp.int32, (width, owned), 1)
    for slot in range(6):
        column = jnp.transpose(got[slot][got[slot].shape[0] - 8 :, :])[:, :1].astype(jnp.int32)
        wanted = jnp.where(meets(slot), column, -1)
        places_ref[slot * width : (slot + 1) * width, :] = jnp.where(
            wanted == place, 1.0, 0.0
        ).astype(BF16)


def offer(vector, picks_ref, slot_refs):
    taken = jnp.dot(split(vector), picks_ref[...], preferred_element_type=F32).astype(BF16)
    width = taken.shape[1] // 6
    for slot in range(6):
        slot_refs[slot][...] = taken[:, slot * width : (slot + 1) * width]


def meet_kernel(*refs):
    own_ref, got, direction_ref, picks_ref = refs[0], slot_order(refs[1:7]), refs[7], refs[8]
    rows, owned = own_ref.shape
    width = got[0].shape[1]
    place = lax.broadcasted_iota(jnp.int32, (owned, width), 0)
    for slot in range(6):
        row = got[slot][rows : rows + 1, :].astype(jnp.int32)
        wanted = jnp.where(meets(slot), row, -1)
        picks_ref[:, slot * width : (slot + 1) * width] = jnp.where(
            wanted == place, 1.0, 0.0
        ).astype(BF16)
    parts = jnp.concatenate([split(ref[:rows]) for ref in got], axis=1)
    direction = own_ref[...] + joined(
        lax.dot_general(
            parts, picks_ref[...], (((1,), (1,)), ((), ())), preferred_element_type=F32
        )
    )
    direction_ref[...] = direction
    offer(direction, picks_ref, refs[9:])


def direction_kernel(*refs):
    sum_ref, got, places_ref, picks_ref, direction_ref = refs[0], refs[1:3], *refs[3:6]
    direction = sum_ref[...] + added(ORDER[4:], got, places_ref)
    direction_ref[...] = direction
    offer(direction, picks_ref, refs[6:])


def hold_kernel(own_ref, schur_ref, out_ref):
    out_ref[...] = own_ref[...]


def own_rows_kernel(vector_ref, schur_ref, total_ref):
    owned = vector_ref.shape[1]
    vector = split(vector_ref[...])
    step = total_ref.shape[1] // 2

    @pl.loop(0, 2)
    def _(i):
        at = pl.multiple_of(i * step, step)
        block = schur_ref[:owned, pl.ds(pl.multiple_of(owned + at, 128), step)]
        total_ref[:, pl.ds(at, step)] = jnp.dot(vector, block, preferred_element_type=F32)


def of_dim(dim, got):
    return jnp.concatenate(sides_of([ref[...] for ref in got], dim), axis=1)


def rows_of(dim, row, owned):
    start = owned + dim * row.shape[1]
    return slice(start, start + row.shape[1])


def some_rows_kernel(*refs):
    got, (sofar_ref, schur_ref, total_ref) = refs[:4], refs[4:]
    wide = total_ref.shape[1]
    owned = schur_ref.shape[1] - wide
    parts = [(dim, of_dim(dim, got[2 * i : 2 * i + 2])) for i, dim in enumerate(EARLY)]
    step = wide // 3

    @pl.loop(0, 3)
    def _(i):
        at = pl.multiple_of(i * step, step)
        columns = pl.ds(pl.multiple_of(owned + at, 128), step)
        here = pl.ds(at, step)
        total = sofar_ref[:, here]
        for dim, row in parts:
            block = schur_ref[rows_of(dim, row, owned), columns]
            total = total + jnp.dot(row, block, preferred_element_type=F32)
        total_ref[:, here] = total


def last_rows_kernel(*refs):
    got, (sofar_ref, schur_ref), slot_refs = refs[:2], refs[2:4], refs[4:]
    owned = schur_ref.shape[1] - sofar_ref.shape[1]
    row = of_dim(LATE, got[::-1])
    block = schur_ref[rows_of(LATE, row, owned), owned:]
    total = sofar_ref[...] + jnp.dot(row, block, preferred_element_type=F32)
    put_split(by_slot(joined(total)), slot_refs)


def own_columns_kernel(*refs):
    vector_ref, got, schur_ref, own_ref = refs[0], slot_order(refs[1:7]), refs[7], refs[8]
    owned = vector_ref.shape[1]
    row = jnp.concatenate(
        [split(vector_ref[...])] + [of_dim(dim, got[2 * dim : 2 * dim + 2]) for dim in range(3)],
        axis=1,
    )
    step = owned // 2

    @pl.loop(0, 2)
    def _(i):
        columns = pl.ds(pl.multiple_of(i * step, step), step)
        own_ref[:, columns] = joined(
            jnp.dot(row, schur_ref[:, columns], preferred_element_type=F32)
        )


def gram_entries(basis):
    rows = basis[0].shape[0]
    lane = lax.broadcasted_iota(jnp.int32, (rows, 128), 1)
    total = jnp.zeros((rows, 128), F32)
    newest = len(basis) - 1
    for i, vector in enumerate(basis):
        value = jnp.sum(vector * basis[newest], axis=1, keepdims=True)
        total = total + jnp.where(lane == i * 4 + newest, value, 0.0)
    return total


def next_kernel(*refs):
    sum_ref, got, places_ref, restricted_ref = refs[0], refs[1:3], refs[3], refs[4]
    vector_ref, next_ref, slot_refs = refs[5], refs[6], refs[7:]
    vector = (sum_ref[...] + added(ORDER[4:], got, places_ref)) * SCALE
    vector_ref[...] = vector
    products = joined(jnp.dot(split(vector), restricted_ref[...], preferred_element_type=F32))
    owned = vector.shape[1]
    next_ref[...] = products[:, :owned]
    put_split(by_slot(products[:, owned:]), slot_refs)


def gram_kernel(*refs):
    sum_ref, got, places_ref = refs[0], refs[1:3], refs[3]
    older, gram_ref = refs[4:-1], refs[-1]
    last = (sum_ref[...] + added(ORDER[4:], got, places_ref)) * SCALE
    basis = [ref[...] for ref in older] + [last]
    total = gram_entries(basis[:1])
    for newest in range(1, len(basis)):
        total = total + gram_entries(basis[: newest + 1])
    half = total.shape[0] // 2
    gram_ref[...] = total[:half] + pltpu.roll(total[half:], 64, 1)


def rotate_solve(columns, beta_norm):
    num_cols = len(columns)
    rhs_vec = [beta_norm] + [jnp.zeros_like(beta_norm) for unused in range(num_cols)]
    cosines = []
    sines = []
    triangle = []
    for section in range(num_cols):
        column = [columns[section][row_at] for row_at in range(section + 2)]
        for earlier in range(section):
            rotated_a = cosines[earlier] * column[earlier] + sines[earlier] * column[earlier + 1]
            rotated_b = -sines[earlier] * column[earlier] + cosines[earlier] * column[earlier + 1]
            column[earlier] = rotated_a
            column[earlier + 1] = rotated_b
        radius = jnp.sqrt(
            column[section] * column[section] + column[section + 1] * column[section + 1]
        )
        inverse = 1.0 / radius
        cosine = column[section] * inverse
        sine_val = column[section + 1] * inverse
        column[section] = inverse
        cosines.append(cosine)
        sines.append(sine_val)
        rhs_vec[section + 1] = -sine_val * rhs_vec[section]
        rhs_vec[section] = cosine * rhs_vec[section]
        triangle.append(column[: section + 1])
    coeffs = [None] * num_cols
    for section in reversed(range(num_cols)):
        running = rhs_vec[section]
        for onward in range(section + 1, num_cols):
            running = running - triangle[onward][section] * coeffs[onward]
        coeffs[section] = running * triangle[section][section]
    return (coeffs, jnp.abs(rhs_vec[num_cols]))


def combine(gram):
    beta = jnp.sqrt(gram(0, 0) + EPSILON)
    inverse_beta = 1.0 / beta
    made_of = [[inverse_beta]]
    columns = []
    for k in range(ITERS):
        applied = [None] + [c * (1.0 / SCALE) for c in made_of[k]]
        against = [
            functools.reduce(
                jnp.add, [gram(a, b) * applied[b] for b in range(1, k + 2)]
            )
            for a in range(k + 1)
        ]
        heights = [
            functools.reduce(jnp.add, [made_of[j][a] * against[a] for a in range(j + 1)])
            for j in range(k + 1)
        ]
        rest = [jnp.zeros_like(beta)] + applied[1:]
        for j in range(k + 1):
            for a in range(j + 1):
                rest[a] = rest[a] - heights[j] * made_of[j][a]
        square = jnp.zeros_like(beta)
        for a in range(k + 2):
            square = square + rest[a] * functools.reduce(
                jnp.add, [gram(a, b) * rest[b] for b in range(k + 2)]
            )
        height = jnp.sqrt(jnp.maximum(square, 0.0) + EPSILON)
        columns.append(heights + [height])
        inverse = 1.0 / height
        made_of.append([r * inverse for r in rest])
    weights, remainder = rotate_solve(columns, beta)
    shares = [
        functools.reduce(jnp.add, [weights[k] * made_of[k][i] for k in range(i, ITERS)])
        for i in range(ITERS)
    ]
    return shares, remainder * inverse_beta


def last_kernel(*refs):
    gram_ref, directions = refs[0], refs[1:-2]
    adjoint_ref, ratio_ref = refs[-2:]
    packed = gram_ref[...]
    sums = jnp.concatenate([packed, pltpu.roll(packed, 64, 1)], axis=0)

    def gram(a, b):
        at = min(a, b) * 4 + max(a, b)
        return sums[:, at : at + 1]

    shares, ratio = combine(gram)
    total = shares[0] * directions[0][...]
    for i in range(1, ITERS):
        total = total + shares[i] * directions[i][...]
    adjoint_ref[...] = total
    rows = ratio.shape[0]
    here = lax.broadcasted_iota(jnp.int32, (rows, rows), 0)
    there = lax.broadcasted_iota(jnp.int32, (rows, rows), 1)
    ratio_ref[...] = jnp.sum(jnp.where(here == there, ratio, 0.0), axis=0, keepdims=True)


def call(kernel, operands, outputs, name, keep=True, scratch=(), limit=8 << 20):
    space = pltpu.HBM if scratch else VMEM
    make = VMEM if keep else jax.ShapeDtypeStruct
    operands = [pltpu.with_memory_space_constraint(x, space) for x in operands]
    return pl.pallas_call(
        kernel,
        out_shape=tuple(make(shape, dtype) for shape, dtype in outputs),
        in_specs=[pl.BlockSpec(memory_space=space)] * len(operands),
        out_specs=tuple(pl.BlockSpec(memory_space=VMEM) for _ in outputs),
        scratch_shapes=scratch,
        compiler_params=pltpu.CompilerParams(vmem_limit_bytes=limit),
        cost_estimate=pl.CostEstimate(
            flops=0,
            bytes_accessed=sum(x.size * x.dtype.itemsize for x in operands),
            transcendentals=0,
        ),
        name=name,
    )(*operands)


def all_sum(array, stages):
    for axis in stages:
        n = lax.axis_size(axis)
        spread = jnp.broadcast_to(array[None], (n,) + array.shape)
        array = jnp.sum(lax.all_to_all(spread, axis, 0, 0), axis=0)
    return array


def local(gradient, local_schur, inverse_rows, face_maps):
    vector = gradient[0, 0, 0]
    schur = local_schur[0, 0, 0]
    restricted = inverse_rows[0, 0, 0]
    rows, owned = vector.shape
    width = face_maps.shape[-1]
    maps = face_maps.reshape(6, 1, width)

    block = ((rows, owned), F32)
    wide = ((2 * rows, 6 * width), F32)
    parcel = ((2 * rows, width), BF16)
    own, *slots = call(
        first_kernel,
        (maps, vector, restricted),
        (block,) + (((rows + 8, width), F32),) * 6,
        "first",
        scratch=[
            VMEM(maps.shape, maps.dtype),
            VMEM(vector.shape, vector.dtype),
            VMEM(restricted.shape, restricted.dtype),
            pltpu.SemaphoreType.DMA((3,)),
        ],
    )
    basis = [vector]
    directions = []
    for section in range(ITERS):
        if section == 0:
            (own,) = call(hold_kernel, (own, schur), (block,), "hold")
        got = trade(slots)
        if section == 0:
            parcels = got
            direction, picks, *slots = call(
                meet_kernel,
                (own, *ordered(got)),
                (block, ((owned, 6 * width), BF16)) + (parcel,) * 6,
                "meet",
            )
        else:
            got = ordered(got)
            (own,) = call(early_kernel, (own, *got[:4], places), (block,), "early")
            direction, *slots = call(
                direction_kernel, (own, *got[4:], places, picks), (block,) + (parcel,) * 6,
                "direction",
            )
        directions.append(direction)
        got = trade(slots)
        (total,) = call(own_rows_kernel, (direction, schur), (wide,), "own_rows")
        early = [got[2 * dim + side] for dim in EARLY for side in range(2)]
        late = [got[2 * LATE + 1], got[2 * LATE]]
        (total,) = call(some_rows_kernel, (*early, total, schur), (wide,), "some_rows")
        slots = call(last_rows_kernel, (*late, total, schur), (parcel,) * 6, "last_rows")
        (own,) = call(
            own_columns_kernel, (direction, *ordered(got), schur), (block,), "own_columns"
        )
        if section == 0:
            (places,) = call(
                turn_kernel, (*parcels, slots[0]), (((6 * width, owned), BF16),), "turn"
            )
        got = ordered(trade(slots))
        (own,) = call(early_kernel, (own, *got[:4], places), (block,), "early")
        if section + 1 < ITERS:
            vector, own, *slots = call(
                next_kernel,
                (own, *got[4:], places, restricted),
                (block,) * 2 + (parcel,) * 6,
                "next",
            )
            basis.append(vector)
    (gram,) = call(
        gram_kernel, (own, *got[4:], places, *basis), (((rows // 2, 128), F32),), "gram"
    )
    gram = all_sum(gram, (("gx", "gy"), "gz"))
    adjoint, ratio = call(
        last_kernel, (gram, *directions), (block, ((1, rows), F32)), "last", keep=False
    )
    return (adjoint[None, None, None], ratio.reshape(rows))


def solution(mesh):
    placed = P("gx", "gy", "gz", None, None)
    return jax.shard_map(
        local,
        mesh=mesh,
        in_specs=(placed,) * 4,
        out_specs=(placed, P()),
        check_vma=False,
    )
```

time: 111 us -> 107 us (0.964)
  waiting for transfers between devices: 11.9 us -> 8.24 us
  starting transfers between devices: 52.1 us -> 50.8 us
  Pallas kernels: 15.6 us -> 16.8 us
    ppermute x54, waiting for transfers between devices: 11.9 us -> 8.24 us  [trade(): lax.ppermute(slots[slot], AXES, partners(slot))]
    ppermute x54, starting transfers between devices: 52.1 us -> 50.8 us  [trade(): lax.ppermute(slots[slot], AXES, partners(slot))]
    pallas_call x15 -> x27, Pallas kernels: 15.6 us -> 16.8 us  [call(): pl.pallas_call(kernel, out_shape=tuple((make(shape, dtype) for shape, dty...]
  transfers between devices with their start and end apart: 54 -> 54, of which waited for: 16 -> 15; matrix products, arithmetic and copies ran while one was open for 0% -> 0% of each run, Pallas kernels for 6% -> 7%
where the time goes in v4:
time: 107 us; the launch traced here: 105 us
  starting transfers between devices  50.8 us (47%)
  blocking collectives  25 us (23%)
  Pallas kernels  16.8 us (16%)
  waiting for transfers between devices  8.24 us (8%)
  local copies, waits for them, and re-layouts  3.41 us (3%)
    ppermute x54, starting transfers between devices, trade(): lax.ppermute(slots[slot], AXES, partners(slot))  50.8 us
    all_to_all x2, blocking collectives, all_sum(): array = jnp.sum(lax.all_to_all(spread, axis, 0, 0), axis=0)  25 us
    pallas_call x27, Pallas kernels, call(): pl.pallas_call(kernel, out_shape=tuple((make(shape, dtype) for shape, dty...  16.8 us
    ppermute x54, waiting for transfers between devices, trade(): lax.ppermute(slots[slot], AXES, partners(slot))  8.24 us
    unnamed x8, local copies, waits for them, and re-layouts  3.39 us
  transfers between devices with their start and end apart: 54, of which 15 were waited for; matrix products, arithmetic and copies ran while one was open for 0% of the time, Pallas kernels for 7%

profile of v4, /device:TPU:10, one launch (start us, length us, event | category | flops | bytes accessed | tf_op | source)
XLA Modules:
  0.0 105.1 jit_solution(4182952788635674018)
XLA Ops:
  0.6 2.1 %first.1 = (f32[16,512]{1,0:T(8,128)S(1)}, f32[24,256]{1,0:T(8,128)S(1)}, f32[24,256]{1,0:T(8,128)S(1)}, f32[24,256]{1,0:T(8,128)S(1)}, f32[24,256]{1,0:T(8,128)...) custom-call(s32[6,1,256]{2,1,0:T(1,128)} %bitcast.24, f32[16,512]{1,0:T(8,128)} %bitcast.22, bf16[512,2048]{1,0:T(8,128)(2,1)} %bitcast.19), custom_call_target="tpu_custom_call" | custom-call | bytes 2136064 | tf_op jit(solution)/shard_map/first/pallas_call | solution.py:383
  2.7 2.0 %collective-permute-start = (f32[24,256]{1,0:T(8,128)S(1)}, f32[24,256]{1,0:T(8,128)S(1)}, u32[]{:S(2)}, u32[]{:S(2)}) collective-permute-start(f32[24,256]{1,0:T(8,128)S(1)} %get-tuple-element.68), channel_id=1, source_target_pairs={{0,1},{1,0},{2,3},{3,2},{4,5},{5,4},{6,7},{7,6},{8,9},{9,8},{10,11... | collective-permute-start | bytes 73736 | tf_op jit(solution)/shard_map/ppermute | solution.py:43
  5.2 2.4 %collective-permute-start.3 = (f32[24,256]{1,0:T(8,128)S(1)}, f32[24,256]{1,0:T(8,128)S(1)}, u32[]{:S(2)}, u32[]{:S(2)}) collective-permute-start(f32[24,256]{1,0:T(8,128)S(1)} %get-tuple-element.71), channel_id=1, source_target_pairs={{0,8},{1,9},{2,10},{3,11},{4,12},{5,13},{6,14},{7,15},{8,0},{9,1},... | collective-permute-start | bytes 73736 | tf_op jit(solution)/shard_map/ppermute | solution.py:43
  7.7 1.5 %collective-permute-start.5 = (f32[24,256]{1,0:T(8,128)S(1)}, f32[24,256]{1,0:T(8,128)S(1)}, u32[]{:S(2)}, u32[]{:S(2)}) collective-permute-start(f32[24,256]{1,0:T(8,128)S(1)} %get-tuple-element.73), channel_id=1, source_target_pairs={{0,8},{1,9},{2,10},{3,11},{4,12},{5,13},{6,14},{7,15},{8,0},{9,1},... | collective-permute-start | bytes 73736 | tf_op jit(solution)/shard_map/ppermute | solution.py:43
  9.2 3.4 %copy-done = bf16[1,1,1,2048,2048]{4,3,2,1,0:T(8,128)(2,1)S(1)} copy-done((bf16[1,1,1,2048,2048]{4,3,2,1,0:T(8,128)(2,1)S(1)}, bf16[1,1,1,2048,2048]{4,3,2,1,0:T(8,128)(2,1)}, u32[]{:S(2)}) %copy-start) | copy-done | bytes 8388632
  13.8 3.9 %collective-permute-start.6 = (bf16[32,256]{1,0:T(8,128)(2,1)S(1)}, bf16[32,256]{1,0:T(8,128)(2,1)S(1)}, u32[]{:S(2)}, u32[]{:S(2)}) collective-permute-start(bf16[32,256]{1,0:T(8,128)(2,1)S(1)} %get-tuple-element.75), channel_id=1, source_target_pairs={{0,1},{1,0},{2,3},{3,2},{4,5},{5,4},{6,7},{7,6},{8,9},{9,8},{10,11... | collective-permute-start | bytes 49160 | tf_op jit(solution)/shard_map/ppermute | solution.py:43
  22.7 4.2 %collective-permute-start.12 = (bf16[32,256]{1,0:T(8,128)(2,1)S(1)}, bf16[32,256]{1,0:T(8,128)(2,1)S(1)}, u32[]{:S(2)}, u32[]{:S(2)}) collective-permute-start(bf16[32,256]{1,0:T(8,128)(2,1)S(1)} %get-tuple-element.81), channel_id=1, source_target_pairs={{0,1},{1,0},{2,3},{3,2},{4,5},{5,4},{6,7},{7,6},{8,9},{9,8},{10,11... | collective-permute-start | bytes 49160 | tf_op jit(solution)/shard_map/ppermute | solution.py:43
  32.4 1.9 %collective-permute-start.18 = (bf16[32,256]{1,0:T(8,128)(2,1)S(1)}, bf16[32,256]{1,0:T(8,128)(2,1)S(1)}, u32[]{:S(2)}, u32[]{:S(2)}) collective-permute-start(bf16[32,256]{1,0:T(8,128)(2,1)S(1)} %get-tuple-element.88), channel_id=1, source_target_pairs={{0,1},{1,0},{2,3},{3,2},{4,5},{5,4},{6,7},{7,6},{8,9},{9,8},{10,11... | collective-permute-start | bytes 49160 | tf_op jit(solution)/shard_map/ppermute | solution.py:43
  39.8 1.7 %collective-permute-start.24 = (bf16[32,256]{1,0:T(8,128)(2,1)S(1)}, bf16[32,256]{1,0:T(8,128)(2,1)S(1)}, u32[]{:S(2)}, u32[]{:S(2)}) collective-permute-start(bf16[32,256]{1,0:T(8,128)(2,1)S(1)} %get-tuple-element.96), channel_id=1, source_target_pairs={{0,1},{1,0},{2,3},{3,2},{4,5},{5,4},{6,7},{7,6},{8,9},{9,8},{10,11... | collective-permute-start | bytes 49160 | tf_op jit(solution)/shard_map/ppermute | solution.py:43
  41.7 1.5 %collective-permute-start.27 = (bf16[32,256]{1,0:T(8,128)(2,1)S(1)}, bf16[32,256]{1,0:T(8,128)(2,1)S(1)}, u32[]{:S(2)}, u32[]{:S(2)}) collective-permute-start(bf16[32,256]{1,0:T(8,128)(2,1)S(1)} %get-tuple-element.99), channel_id=1, source_target_pairs={{0,8},{1,9},{2,10},{3,11},{4,12},{5,13},{6,14},{7,15},{8,0},{9,1},... | collective-permute-start | bytes 49160 | tf_op jit(solution)/shard_map/ppermute | solution.py:43
  43.2 1.5 %collective-permute-start.28 = (bf16[32,256]{1,0:T(8,128)(2,1)S(1)}, bf16[32,256]{1,0:T(8,128)(2,1)S(1)}, u32[]{:S(2)}, u32[]{:S(2)}) collective-permute-start(bf16[32,256]{1,0:T(8,128)(2,1)S(1)} %get-tuple-element.100), channel_id=1, source_target_pairs={{0,1},{1,0},{2,3},{3,2},{4,5},{5,4},{6,7},{7,6},{8,16},{9,17},{10,... | collective-permute-start | bytes 49160 | tf_op jit(solution)/shard_map/ppermute | solution.py:43
  46.8 2.0 %collective-permute-start.30 = (bf16[32,256]{1,0:T(8,128)(2,1)S(1)}, bf16[32,256]{1,0:T(8,128)(2,1)S(1)}, u32[]{:S(2)}, u32[]{:S(2)}) collective-permute-start(bf16[32,256]{1,0:T(8,128)(2,1)S(1)} %get-tuple-element.102), channel_id=1, source_target_pairs={{0,1},{1,0},{2,3},{3,2},{4,5},{5,4},{6,7},{7,6},{8,9},{9,8},{10,11... | collective-permute-start | bytes 49160 | tf_op jit(solution)/shard_map/ppermute | solution.py:43
  50.5 1.8 %collective-permute-start.34 = (bf16[32,256]{1,0:T(8,128)(2,1)S(1)}, bf16[32,256]{1,0:T(8,128)(2,1)S(1)}, u32[]{:S(2)}, u32[]{:S(2)}) collective-permute-start(bf16[32,256]{1,0:T(8,128)(2,1)S(1)} %get-tuple-element.106), channel_id=1, source_target_pairs={{0,1},{1,0},{2,3},{3,2},{4,5},{5,4},{6,7},{7,6},{8,16},{9,17},{10,... | collective-permute-start | bytes 49160 | tf_op jit(solution)/shard_map/ppermute | solution.py:43
  54.3 2.1 %collective-permute-start.36 = (bf16[32,256]{1,0:T(8,128)(2,1)S(1)}, bf16[32,256]{1,0:T(8,128)(2,1)S(1)}, u32[]{:S(2)}, u32[]{:S(2)}) collective-permute-start(bf16[32,256]{1,0:T(8,128)(2,1)S(1)} %get-tuple-element.109), channel_id=1, source_target_pairs={{0,1},{1,0},{2,3},{3,2},{4,5},{5,4},{6,7},{7,6},{8,9},{9,8},{10,11... | collective-permute-start | bytes 49160 | tf_op jit(solution)/shard_map/ppermute | solution.py:43
  56.4 1.7 %collective-permute-start.38 = (bf16[32,256]{1,0:T(8,128)(2,1)S(1)}, bf16[32,256]{1,0:T(8,128)(2,1)S(1)}, u32[]{:S(2)}, u32[]{:S(2)}) collective-permute-start(bf16[32,256]{1,0:T(8,128)(2,1)S(1)} %get-tuple-element.111), channel_id=1, source_target_pairs={{0,64},{1,65},{2,66},{3,67},{4,68},{5,69},{6,70},{7,71},{8,72},{9,... | collective-permute-start | bytes 49160 | tf_op jit(solution)/shard_map/ppermute | solution.py:43
  59.0 1.7 %collective-permute-start.40 = (bf16[32,256]{1,0:T(8,128)(2,1)S(1)}, bf16[32,256]{1,0:T(8,128)(2,1)S(1)}, u32[]{:S(2)}, u32[]{:S(2)}) collective-permute-start(bf16[32,256]{1,0:T(8,128)(2,1)S(1)} %get-tuple-element.113), channel_id=1, source_target_pairs={{0,1},{1,0},{2,3},{3,2},{4,5},{5,4},{6,7},{7,6},{8,16},{9,17},{10,... | collective-permute-start | bytes 49160 | tf_op jit(solution)/shard_map/ppermute | solution.py:43
  62.8 1.7 %collective-permute-start.42 = (bf16[32,256]{1,0:T(8,128)(2,1)S(1)}, bf16[32,256]{1,0:T(8,128)(2,1)S(1)}, u32[]{:S(2)}, u32[]{:S(2)}) collective-permute-start(bf16[32,256]{1,0:T(8,128)(2,1)S(1)} %get-tuple-element.116), channel_id=1, source_target_pairs={{0,1},{1,0},{2,3},{3,2},{4,5},{5,4},{6,7},{7,6},{8,9},{9,8},{10,11... | collective-permute-start | bytes 49160 | tf_op jit(solution)/shard_map/ppermute | solution.py:43
  66.2 2.0 %collective-permute-start.46 = (bf16[32,256]{1,0:T(8,128)(2,1)S(1)}, bf16[32,256]{1,0:T(8,128)(2,1)S(1)}, u32[]{:S(2)}, u32[]{:S(2)}) collective-permute-start(bf16[32,256]{1,0:T(8,128)(2,1)S(1)} %get-tuple-element.120), channel_id=1, source_target_pairs={{0,1},{1,0},{2,3},{3,2},{4,5},{5,4},{6,7},{7,6},{8,16},{9,17},{10,... | collective-permute-start | bytes 49160 | tf_op jit(solution)/shard_map/ppermute | solution.py:43
  70.1 2.0 %collective-permute-start.48 = (bf16[32,256]{1,0:T(8,128)(2,1)S(1)}, bf16[32,256]{1,0:T(8,128)(2,1)S(1)}, u32[]{:S(2)}, u32[]{:S(2)}) collective-permute-start(bf16[32,256]{1,0:T(8,128)(2,1)S(1)} %get-tuple-element.122), channel_id=1, source_target_pairs={{0,1},{1,0},{2,3},{3,2},{4,5},{5,4},{6,7},{7,6},{8,9},{9,8},{10,11... | collective-permute-start | bytes 49160 | tf_op jit(solution)/shard_map/ppermute | solution.py:43
  72.1 1.4 %collective-permute-start.50 = (bf16[32,256]{1,0:T(8,128)(2,1)S(1)}, bf16[32,256]{1,0:T(8,128)(2,1)S(1)}, u32[]{:S(2)}, u32[]{:S(2)}) collective-permute-start(bf16[32,256]{1,0:T(8,128)(2,1)S(1)} %get-tuple-element.124), channel_id=1, source_target_pairs={{0,64},{1,65},{2,66},{3,67},{4,68},{5,69},{6,70},{7,71},{8,72},{9,... | collective-permute-start | bytes 49160 | tf_op jit(solution)/shard_map/ppermute | solution.py:43
  74.6 1.5 %collective-permute-start.52 = (bf16[32,256]{1,0:T(8,128)(2,1)S(1)}, bf16[32,256]{1,0:T(8,128)(2,1)S(1)}, u32[]{:S(2)}, u32[]{:S(2)}) collective-permute-start(bf16[32,256]{1,0:T(8,128)(2,1)S(1)} %get-tuple-element.126), channel_id=1, source_target_pairs={{0,1},{1,0},{2,3},{3,2},{4,5},{5,4},{6,7},{7,6},{8,16},{9,17},{10,... | collective-permute-start | bytes 49160 | tf_op jit(solution)/shard_map/ppermute | solution.py:43
  78.1 12.0 %all_to_all.10 = f32[32,8,128]{2,1,0:T(8,128)S(1)} all-to-all(f32[32,8,128]{2,1,0:T(8,128)S(1)} %broadcast_in_dim.6), channel_id=1, replica_groups=mesh['gx'=4,'gy'=8,'gz'=8] {'gx','gy'}, dimensions={0} | all-to-all | bytes 262144 | tf_op jit(solution)/shard_map/all_to_all | solution.py:403
  90.2 13.0 %all_to_all.11 = f32[8,8,128]{2,1,0:T(8,128)S(1)} all-to-all(f32[8,8,128]{2,1,0:T(8,128)S(1)} %broadcast_in_dim.7), channel_id=1, replica_groups=mesh['gx'=4,'gy'=8,'gz'=8] {'gz'}, dimensions={0} | all-to-all | bytes 65536 | tf_op jit(solution)/shard_map/all_to_all | solution.py:403
  103.2 2.0 %last.1 = (f32[16,512]{1,0:T(8,128)}, f32[1,16]{1,0:T(1,128)}) custom-call(f32[8,128]{1,0:T(8,128)S(1)} %reduce_sum.19.refs_0_, f32[16,512]{1,0:T(8,128)S(1)} %get-tuple-element.74.refs_0_.vector_ref.refs_1_, f32[16,512]{1,0:T(8,128)S(1)} %get-tuple-element.95.refs_0_.vector_ref.refs_2_, f32[16,512]{1,0:T(8,128)S(1)} %get-tuple-element.115.refs_0_.vector_ref.refs_3_), custom_call_target="tpu_custom_call" | custom-call | bytes 102400 | tf_op jit(solution)/shard_map/last/pallas_call | solution.py:383
  (125 shorter events, 33.2 us)
Async XLA Ops:
  2.7 5.0 %collective-permute-start = (f32[24,256]{1,0:T(8,128)S(1)}, f32[24,256]{1,0:T(8,128)S(1)}, u32[]{:S(2)}, u32[]{:S(2)}) collective-permute-start(f32[24,256]{1,0:T(8,128)S(1)} %get-tuple-element.68), channel_id=1, source_target_pairs={{0,1},{1,0},{2,3},{3,2},{4,5},{5,4},{6,7},{7,6},{8,9},{9,8},{10,11... | collective-permute-start | bytes 73736 | tf_op jit(solution)/shard_map/ppermute | solution.py:43
  4.8 7.9 %collective-permute-start.1 = (f32[24,256]{1,0:T(8,128)S(1)}, f32[24,256]{1,0:T(8,128)S(1)}, u32[]{:S(2)}, u32[]{:S(2)}) collective-permute-start(f32[24,256]{1,0:T(8,128)S(1)} %get-tuple-element.69), channel_id=1, source_target_pairs={{0,8},{1,2},{2,1},{3,4},{4,3},{5,6},{6,5},{7,15},{8,0},{9,10},{10,... | collective-permute-start | bytes 73736 | tf_op jit(solution)/shard_map/ppermute | solution.py:43
  4.8 7.9 %collective-permute-start.2 = (f32[24,256]{1,0:T(8,128)S(1)}, f32[24,256]{1,0:T(8,128)S(1)}, u32[]{:S(2)}, u32[]{:S(2)}) collective-permute-start(f32[24,256]{1,0:T(8,128)S(1)} %get-tuple-element.70), channel_id=1, source_target_pairs={{0,64},{1,65},{2,66},{3,67},{4,68},{5,69},{6,70},{7,71},{8,72},{9,... | collective-permute-start | bytes 73736 | tf_op jit(solution)/shard_map/ppermute | solution.py:43
  5.2 7.4 %collective-permute-start.3 = (f32[24,256]{1,0:T(8,128)S(1)}, f32[24,256]{1,0:T(8,128)S(1)}, u32[]{:S(2)}, u32[]{:S(2)}) collective-permute-start(f32[24,256]{1,0:T(8,128)S(1)} %get-tuple-element.71), channel_id=1, source_target_pairs={{0,8},{1,9},{2,10},{3,11},{4,12},{5,13},{6,14},{7,15},{8,0},{9,1},... | collective-permute-start | bytes 73736 | tf_op jit(solution)/shard_map/ppermute | solution.py:43
  7.6 5.0 %collective-permute-start.4 = (f32[24,256]{1,0:T(8,128)S(1)}, f32[24,256]{1,0:T(8,128)S(1)}, u32[]{:S(2)}, u32[]{:S(2)}) collective-permute-start(f32[24,256]{1,0:T(8,128)S(1)} %get-tuple-element.72), channel_id=1, source_target_pairs={{0,1},{1,0},{2,3},{3,2},{4,5},{5,4},{6,7},{7,6},{8,16},{9,17},{10,... | collective-permute-start | bytes 73736 | tf_op jit(solution)/shard_map/ppermute | solution.py:43
  7.7 5.0 %collective-permute-start.5 = (f32[24,256]{1,0:T(8,128)S(1)}, f32[24,256]{1,0:T(8,128)S(1)}, u32[]{:S(2)}, u32[]{:S(2)}) collective-permute-start(f32[24,256]{1,0:T(8,128)S(1)} %get-tuple-element.73), channel_id=1, source_target_pairs={{0,8},{1,9},{2,10},{3,11},{4,12},{5,13},{6,14},{7,15},{8,0},{9,1},... | collective-permute-start | bytes 73736 | tf_op jit(solution)/shard_map/ppermute | solution.py:43
  13.8 5.6 %collective-permute-start.6 = (bf16[32,256]{1,0:T(8,128)(2,1)S(1)}, bf16[32,256]{1,0:T(8,128)(2,1)S(1)}, u32[]{:S(2)}, u32[]{:S(2)}) collective-permute-start(bf16[32,256]{1,0:T(8,128)(2,1)S(1)} %get-tuple-element.75), channel_id=1, source_target_pairs={{0,1},{1,0},{2,3},{3,2},{4,5},{5,4},{6,7},{7,6},{8,9},{9,8},{10,11... | collective-permute-start | bytes 49160 | tf_op jit(solution)/shard_map/ppermute | solution.py:43
  18.4 3.9 %collective-permute-start.10 = (bf16[32,256]{1,0:T(8,128)(2,1)S(1)}, bf16[32,256]{1,0:T(8,128)(2,1)S(1)}, u32[]{:S(2)}, u32[]{:S(2)}) collective-permute-start(bf16[32,256]{1,0:T(8,128)(2,1)S(1)} %get-tuple-element.79), channel_id=1, source_target_pairs={{0,1},{1,0},{2,3},{3,2},{4,5},{5,4},{6,7},{7,6},{8,16},{9,17},{10,... | collective-permute-start | bytes 49160 | tf_op jit(solution)/shard_map/ppermute | solution.py:43
  22.7 5.9 %collective-permute-start.12 = (bf16[32,256]{1,0:T(8,128)(2,1)S(1)}, bf16[32,256]{1,0:T(8,128)(2,1)S(1)}, u32[]{:S(2)}, u32[]{:S(2)}) collective-permute-start(bf16[32,256]{1,0:T(8,128)(2,1)S(1)} %get-tuple-element.81), channel_id=1, source_target_pairs={{0,1},{1,0},{2,3},{3,2},{4,5},{5,4},{6,7},{7,6},{8,9},{9,8},{10,11... | collective-permute-start | bytes 49160 | tf_op jit(solution)/shard_map/ppermute | solution.py:43
  27.7 4.0 %collective-permute-start.16 = (bf16[32,256]{1,0:T(8,128)(2,1)S(1)}, bf16[32,256]{1,0:T(8,128)(2,1)S(1)}, u32[]{:S(2)}, u32[]{:S(2)}) collective-permute-start(bf16[32,256]{1,0:T(8,128)(2,1)S(1)} %get-tuple-element.85), channel_id=1, source_target_pairs={{0,1},{1,0},{2,3},{3,2},{4,5},{5,4},{6,7},{7,6},{8,16},{9,17},{10,... | collective-permute-start | bytes 49160 | tf_op jit(solution)/shard_map/ppermute | solution.py:43
  32.4 4.6 %collective-permute-start.18 = (bf16[32,256]{1,0:T(8,128)(2,1)S(1)}, bf16[32,256]{1,0:T(8,128)(2,1)S(1)}, u32[]{:S(2)}, u32[]{:S(2)}) collective-permute-start(bf16[32,256]{1,0:T(8,128)(2,1)S(1)} %get-tuple-element.88), channel_id=1, source_target_pairs={{0,1},{1,0},{2,3},{3,2},{4,5},{5,4},{6,7},{7,6},{8,9},{9,8},{10,11... | collective-permute-start | bytes 49160 | tf_op jit(solution)/shard_map/ppermute | solution.py:43
  39.8 4.9 %collective-permute-start.24 = (bf16[32,256]{1,0:T(8,128)(2,1)S(1)}, bf16[32,256]{1,0:T(8,128)(2,1)S(1)}, u32[]{:S(2)}, u32[]{:S(2)}) collective-permute-start(bf16[32,256]{1,0:T(8,128)(2,1)S(1)} %get-tuple-element.96), channel_id=1, source_target_pairs={{0,1},{1,0},{2,3},{3,2},{4,5},{5,4},{6,7},{7,6},{8,9},{9,8},{10,11... | collective-permute-start | bytes 49160 | tf_op jit(solution)/shard_map/ppermute | solution.py:43
  46.8 5.5 %collective-permute-start.30 = (bf16[32,256]{1,0:T(8,128)(2,1)S(1)}, bf16[32,256]{1,0:T(8,128)(2,1)S(1)}, u32[]{:S(2)}, u32[]{:S(2)}) collective-permute-start(bf16[32,256]{1,0:T(8,128)(2,1)S(1)} %get-tuple-element.102), channel_id=1, source_target_pairs={{0,1},{1,0},{2,3},{3,2},{4,5},{5,4},{6,7},{7,6},{8,9},{9,8},{10,11... | collective-permute-start | bytes 49160 | tf_op jit(solution)/shard_map/ppermute | solution.py:43
  48.8 4.1 %collective-permute-start.31 = (bf16[32,256]{1,0:T(8,128)(2,1)S(1)}, bf16[32,256]{1,0:T(8,128)(2,1)S(1)}, u32[]{:S(2)}, u32[]{:S(2)}) collective-permute-start(bf16[32,256]{1,0:T(8,128)(2,1)S(1)} %get-tuple-element.103), channel_id=1, source_target_pairs={{0,8},{1,2},{2,1},{3,4},{4,3},{5,6},{6,5},{7,15},{8,0},{9,10},{10,... | collective-permute-start | bytes 49160 | tf_op jit(solution)/shard_map/ppermute | solution.py:43
  48.8 4.1 %collective-permute-start.32 = (bf16[32,256]{1,0:T(8,128)(2,1)S(1)}, bf16[32,256]{1,0:T(8,128)(2,1)S(1)}, u32[]{:S(2)}, u32[]{:S(2)}) collective-permute-start(bf16[32,256]{1,0:T(8,128)(2,1)S(1)} %get-tuple-element.104), channel_id=1, source_target_pairs={{0,64},{1,65},{2,66},{3,67},{4,68},{5,69},{6,70},{7,71},{8,72},{9,... | collective-permute-start | bytes 49160 | tf_op jit(solution)/shard_map/ppermute | solution.py:43
  54.3 6.5 %collective-permute-start.36 = (bf16[32,256]{1,0:T(8,128)(2,1)S(1)}, bf16[32,256]{1,0:T(8,128)(2,1)S(1)}, u32[]{:S(2)}, u32[]{:S(2)}) collective-permute-start(bf16[32,256]{1,0:T(8,128)(2,1)S(1)} %get-tuple-element.109), channel_id=1, source_target_pairs={{0,1},{1,0},{2,3},{3,2},{4,5},{5,4},{6,7},{7,6},{8,9},{9,8},{10,11... | collective-permute-start | bytes 49160 | tf_op jit(solution)/shard_map/ppermute | solution.py:43
  56.4 4.3 %collective-permute-start.37 = (bf16[32,256]{1,0:T(8,128)(2,1)S(1)}, bf16[32,256]{1,0:T(8,128)(2,1)S(1)}, u32[]{:S(2)}, u32[]{:S(2)}) collective-permute-start(bf16[32,256]{1,0:T(8,128)(2,1)S(1)} %get-tuple-element.110), channel_id=1, source_target_pairs={{0,8},{1,2},{2,1},{3,4},{4,3},{5,6},{6,5},{7,15},{8,0},{9,10},{10,... | collective-permute-start | bytes 49160 | tf_op jit(solution)/shard_map/ppermute | solution.py:43
  56.4 4.3 %collective-permute-start.38 = (bf16[32,256]{1,0:T(8,128)(2,1)S(1)}, bf16[32,256]{1,0:T(8,128)(2,1)S(1)}, u32[]{:S(2)}, u32[]{:S(2)}) collective-permute-start(bf16[32,256]{1,0:T(8,128)(2,1)S(1)} %get-tuple-element.111), channel_id=1, source_target_pairs={{0,64},{1,65},{2,66},{3,67},{4,68},{5,69},{6,70},{7,71},{8,72},{9,... | collective-permute-start | bytes 49160 | tf_op jit(solution)/shard_map/ppermute | solution.py:43
  62.8 5.5 %collective-permute-start.42 = (bf16[32,256]{1,0:T(8,128)(2,1)S(1)}, bf16[32,256]{1,0:T(8,128)(2,1)S(1)}, u32[]{:S(2)}, u32[]{:S(2)}) collective-permute-start(bf16[32,256]{1,0:T(8,128)(2,1)S(1)} %get-tuple-element.116), channel_id=1, source_target_pairs={{0,1},{1,0},{2,3},{3,2},{4,5},{5,4},{6,7},{7,6},{8,9},{9,8},{10,11... | collective-permute-start | bytes 49160 | tf_op jit(solution)/shard_map/ppermute | solution.py:43
  64.5 4.2 %collective-permute-start.43 = (bf16[32,256]{1,0:T(8,128)(2,1)S(1)}, bf16[32,256]{1,0:T(8,128)(2,1)S(1)}, u32[]{:S(2)}, u32[]{:S(2)}) collective-permute-start(bf16[32,256]{1,0:T(8,128)(2,1)S(1)} %get-tuple-element.117), channel_id=1, source_target_pairs={{0,8},{1,2},{2,1},{3,4},{4,3},{5,6},{6,5},{7,15},{8,0},{9,10},{10,... | collective-permute-start | bytes 49160 | tf_op jit(solution)/shard_map/ppermute | solution.py:43
  64.5 4.2 %collective-permute-start.44 = (bf16[32,256]{1,0:T(8,128)(2,1)S(1)}, bf16[32,256]{1,0:T(8,128)(2,1)S(1)}, u32[]{:S(2)}, u32[]{:S(2)}) collective-permute-start(bf16[32,256]{1,0:T(8,128)(2,1)S(1)} %get-tuple-element.118), channel_id=1, source_target_pairs={{0,64},{1,65},{2,66},{3,67},{4,68},{5,69},{6,70},{7,71},{8,72},{9,... | collective-permute-start | bytes 49160 | tf_op jit(solution)/shard_map/ppermute | solution.py:43
  70.1 6.0 %collective-permute-start.48 = (bf16[32,256]{1,0:T(8,128)(2,1)S(1)}, bf16[32,256]{1,0:T(8,128)(2,1)S(1)}, u32[]{:S(2)}, u32[]{:S(2)}) collective-permute-start(bf16[32,256]{1,0:T(8,128)(2,1)S(1)} %get-tuple-element.122), channel_id=1, source_target_pairs={{0,1},{1,0},{2,3},{3,2},{4,5},{5,4},{6,7},{7,6},{8,9},{9,8},{10,11... | collective-permute-start | bytes 49160 | tf_op jit(solution)/shard_map/ppermute | solution.py:43
  72.1 4.6 %collective-permute-start.49 = (bf16[32,256]{1,0:T(8,128)(2,1)S(1)}, bf16[32,256]{1,0:T(8,128)(2,1)S(1)}, u32[]{:S(2)}, u32[]{:S(2)}) collective-permute-start(bf16[32,256]{1,0:T(8,128)(2,1)S(1)} %get-tuple-element.123), channel_id=1, source_target_pairs={{0,8},{1,2},{2,1},{3,4},{4,3},{5,6},{6,5},{7,15},{8,0},{9,10},{10,... | collective-permute-start | bytes 49160 | tf_op jit(solution)/shard_map/ppermute | solution.py:43
  72.1 4.6 %collective-permute-start.50 = (bf16[32,256]{1,0:T(8,128)(2,1)S(1)}, bf16[32,256]{1,0:T(8,128)(2,1)S(1)}, u32[]{:S(2)}, u32[]{:S(2)}) collective-permute-start(bf16[32,256]{1,0:T(8,128)(2,1)S(1)} %get-tuple-element.124), channel_id=1, source_target_pairs={{0,64},{1,65},{2,66},{3,67},{4,68},{5,69},{6,70},{7,71},{8,72},{9,... | collective-permute-start | bytes 49160 | tf_op jit(solution)/shard_map/ppermute | solution.py:43
  (34 other events, 107.2 us)

commit v5 on v4

--- a/solution.py
+++ b/solution.py
@@ -12,7 +12,7 @@
 EPSILON = 1e-06
 SCALE = 2.0**-12
 AXES = ("gx", "gy", "gz")
-ASIDE = (1, 2, 1)
+ASIDE = (1, 0, 1)
 ORDER = (4, 5, 0, 1, 3, 2)
 EARLY = (2, 0)
 LATE = 1
@@ -296,10 +296,9 @@
             rotated_b = -sines[earlier] * column[earlier] + cosines[earlier] * column[earlier + 1]
             column[earlier] = rotated_a
             column[earlier + 1] = rotated_b
-        radius = jnp.sqrt(
+        inverse = lax.rsqrt(
             column[section] * column[section] + column[section + 1] * column[section + 1]
         )
-        inverse = 1.0 / radius
         cosine = column[section] * inverse
         sine_val = column[section + 1] * inverse
         column[section] = inverse
@@ -318,8 +317,9 @@
 
 
 def combine(gram):
-    beta = jnp.sqrt(gram(0, 0) + EPSILON)
-    inverse_beta = 1.0 / beta
+    square = gram(0, 0) + EPSILON
+    inverse_beta = lax.rsqrt(square)
+    beta = square * inverse_beta
     made_of = [[inverse_beta]]
     columns = []
     for k in range(ITERS):
@@ -343,9 +343,9 @@
             square = square + rest[a] * functools.reduce(
                 jnp.add, [gram(a, b) * rest[b] for b in range(k + 2)]
             )
-        height = jnp.sqrt(jnp.maximum(square, 0.0) + EPSILON)
-        columns.append(heights + [height])
-        inverse = 1.0 / height
+        square = jnp.maximum(square, 0.0) + EPSILON
+        inverse = lax.rsqrt(square)
+        columns.append(heights + [square * inverse])
         made_of.append([r * inverse for r in rest])
     weights, remainder = rotate_solve(columns, beta)
     shares = [

time: 107 us -> 106 us (level)
  no operation moved by 1% of the time
where the time goes in v5:
time: 106 us; the launch traced here: 105 us
  starting transfers between devices  49.8 us (47%)
  blocking collectives  24.7 us (23%)
  Pallas kernels  16.8 us (16%)
  waiting for transfers between devices  9.04 us (9%)
  local copies, waits for them, and re-layouts  3.41 us (3%)
    ppermute x54, starting transfers between devices, trade(): lax.ppermute(slots[slot], AXES, partners(slot))  49.8 us
    all_to_all x2, blocking collectives, all_sum(): array = jnp.sum(lax.all_to_all(spread, axis, 0, 0), axis=0)  24.7 us
    pallas_call x27, Pallas kernels, call(): pl.pallas_call(kernel, out_shape=tuple((make(shape, dtype) for shape, dty...  16.8 us
    ppermute x54, waiting for transfers between devices, trade(): lax.ppermute(slots[slot], AXES, partners(slot))  9.04 us
    unnamed x8, local copies, waits for them, and re-layouts  3.39 us
  transfers between devices with their start and end apart: 54, of which 15 were waited for; matrix products, arithmetic and copies ran while one was open for 0% of the time, Pallas kernels for 7%

profile of v5, /device:TPU:10, one launch (start us, length us, event | category | flops | bytes accessed | tf_op | source)
XLA Modules:
  0.0 104.6 jit_solution(16927409764914598181)
XLA Ops:
  0.6 2.1 %first.1 = (f32[16,512]{1,0:T(8,128)S(1)}, f32[24,256]{1,0:T(8,128)S(1)}, f32[24,256]{1,0:T(8,128)S(1)}, f32[24,256]{1,0:T(8,128)S(1)}, f32[24,256]{1,0:T(8,128)...) custom-call(s32[6,1,256]{2,1,0:T(1,128)} %bitcast.24, f32[16,512]{1,0:T(8,128)} %bitcast.22, bf16[512,2048]{1,0:T(8,128)(2,1)} %bitcast.19), custom_call_target="tpu_custom_call" | custom-call | bytes 2136064 | tf_op jit(solution)/shard_map/first/pallas_call | solution.py:383
  2.7 2.0 %collective-permute-start = (f32[24,256]{1,0:T(8,128)S(1)}, f32[24,256]{1,0:T(8,128)S(1)}, u32[]{:S(2)}, u32[]{:S(2)}) collective-permute-start(f32[24,256]{1,0:T(8,128)S(1)} %get-tuple-element.68), channel_id=1, source_target_pairs={{0,1},{1,0},{2,3},{3,2},{4,5},{5,4},{6,7},{7,6},{8,9},{9,8},{10,11... | collective-permute-start | bytes 73736 | tf_op jit(solution)/shard_map/ppermute | solution.py:43
  5.2 2.4 %collective-permute-start.3 = (f32[24,256]{1,0:T(8,128)S(1)}, f32[24,256]{1,0:T(8,128)S(1)}, u32[]{:S(2)}, u32[]{:S(2)}) collective-permute-start(f32[24,256]{1,0:T(8,128)S(1)} %get-tuple-element.71), channel_id=1, source_target_pairs={{0,8},{1,9},{2,10},{3,11},{4,12},{5,13},{6,14},{7,15},{8,0},{9,1},... | collective-permute-start | bytes 73736 | tf_op jit(solution)/shard_map/ppermute | solution.py:43
  7.7 1.5 %collective-permute-start.5 = (f32[24,256]{1,0:T(8,128)S(1)}, f32[24,256]{1,0:T(8,128)S(1)}, u32[]{:S(2)}, u32[]{:S(2)}) collective-permute-start(f32[24,256]{1,0:T(8,128)S(1)} %get-tuple-element.73), channel_id=1, source_target_pairs={{0,8},{1,9},{2,10},{3,11},{4,12},{5,13},{6,14},{7,15},{8,0},{9,1},... | collective-permute-start | bytes 73736 | tf_op jit(solution)/shard_map/ppermute | solution.py:43
  9.2 3.4 %copy-done = bf16[1,1,1,2048,2048]{4,3,2,1,0:T(8,128)(2,1)S(1)} copy-done((bf16[1,1,1,2048,2048]{4,3,2,1,0:T(8,128)(2,1)S(1)}, bf16[1,1,1,2048,2048]{4,3,2,1,0:T(8,128)(2,1)}, u32[]{:S(2)}) %copy-start) | copy-done | bytes 8388632
  13.8 3.9 %collective-permute-start.6 = (bf16[32,256]{1,0:T(8,128)(2,1)S(1)}, bf16[32,256]{1,0:T(8,128)(2,1)S(1)}, u32[]{:S(2)}, u32[]{:S(2)}) collective-permute-start(bf16[32,256]{1,0:T(8,128)(2,1)S(1)} %get-tuple-element.75), channel_id=1, source_target_pairs={{0,1},{1,0},{2,3},{3,2},{4,5},{5,4},{6,7},{7,6},{8,9},{9,8},{10,11... | collective-permute-start | bytes 49160 | tf_op jit(solution)/shard_map/ppermute | solution.py:43
  22.7 4.2 %collective-permute-start.12 = (bf16[32,256]{1,0:T(8,128)(2,1)S(1)}, bf16[32,256]{1,0:T(8,128)(2,1)S(1)}, u32[]{:S(2)}, u32[]{:S(2)}) collective-permute-start(bf16[32,256]{1,0:T(8,128)(2,1)S(1)} %get-tuple-element.81), channel_id=1, source_target_pairs={{0,1},{1,0},{2,3},{3,2},{4,5},{5,4},{6,7},{7,6},{8,9},{9,8},{10,11... | collective-permute-start | bytes 49160 | tf_op jit(solution)/shard_map/ppermute | solution.py:43
  32.4 1.9 %collective-permute-start.18 = (bf16[32,256]{1,0:T(8,128)(2,1)S(1)}, bf16[32,256]{1,0:T(8,128)(2,1)S(1)}, u32[]{:S(2)}, u32[]{:S(2)}) collective-permute-start(bf16[32,256]{1,0:T(8,128)(2,1)S(1)} %get-tuple-element.88), channel_id=1, source_target_pairs={{0,1},{1,0},{2,3},{3,2},{4,5},{5,4},{6,7},{7,6},{8,9},{9,8},{10,11... | collective-permute-start | bytes 49160 | tf_op jit(solution)/shard_map/ppermute | solution.py:43
  40.1 1.4 %collective-permute-start.24 = (bf16[32,256]{1,0:T(8,128)(2,1)S(1)}, bf16[32,256]{1,0:T(8,128)(2,1)S(1)}, u32[]{:S(2)}, u32[]{:S(2)}) collective-permute-start(bf16[32,256]{1,0:T(8,128)(2,1)S(1)} %get-tuple-element.96), channel_id=1, source_target_pairs={{0,1},{1,0},{2,3},{3,2},{4,5},{5,4},{6,7},{7,6},{8,9},{9,8},{10,11... | collective-permute-start | bytes 49160 | tf_op jit(solution)/shard_map/ppermute | solution.py:43
  41.7 1.5 %collective-permute-start.27 = (bf16[32,256]{1,0:T(8,128)(2,1)S(1)}, bf16[32,256]{1,0:T(8,128)(2,1)S(1)}, u32[]{:S(2)}, u32[]{:S(2)}) collective-permute-start(bf16[32,256]{1,0:T(8,128)(2,1)S(1)} %get-tuple-element.99), channel_id=1, source_target_pairs={{0,8},{1,9},{2,10},{3,11},{4,12},{5,13},{6,14},{7,15},{8,0},{9,1},... | collective-permute-start | bytes 49160 | tf_op jit(solution)/shard_map/ppermute | solution.py:43
  43.2 1.2 %collective-permute-start.28 = (bf16[32,256]{1,0:T(8,128)(2,1)S(1)}, bf16[32,256]{1,0:T(8,128)(2,1)S(1)}, u32[]{:S(2)}, u32[]{:S(2)}) collective-permute-start(bf16[32,256]{1,0:T(8,128)(2,1)S(1)} %get-tuple-element.100), channel_id=1, source_target_pairs={{0,64},{1,65},{2,66},{3,67},{4,68},{5,69},{6,70},{7,71},{8,16},{9,... | collective-permute-start | bytes 49160 | tf_op jit(solution)/shard_map/ppermute | solution.py:43
  46.8 1.9 %collective-permute-start.30 = (bf16[32,256]{1,0:T(8,128)(2,1)S(1)}, bf16[32,256]{1,0:T(8,128)(2,1)S(1)}, u32[]{:S(2)}, u32[]{:S(2)}) collective-permute-start(bf16[32,256]{1,0:T(8,128)(2,1)S(1)} %get-tuple-element.102), channel_id=1, source_target_pairs={{0,1},{1,0},{2,3},{3,2},{4,5},{5,4},{6,7},{7,6},{8,9},{9,8},{10,11... | collective-permute-start | bytes 49160 | tf_op jit(solution)/shard_map/ppermute | solution.py:43
  50.4 1.5 %collective-permute-start.34 = (bf16[32,256]{1,0:T(8,128)(2,1)S(1)}, bf16[32,256]{1,0:T(8,128)(2,1)S(1)}, u32[]{:S(2)}, u32[]{:S(2)}) collective-permute-start(bf16[32,256]{1,0:T(8,128)(2,1)S(1)} %get-tuple-element.106), channel_id=1, source_target_pairs={{0,64},{1,65},{2,66},{3,67},{4,68},{5,69},{6,70},{7,71},{8,16},{9,... | collective-permute-start | bytes 49160 | tf_op jit(solution)/shard_map/ppermute | solution.py:43
  54.3 1.9 %collective-permute-start.36 = (bf16[32,256]{1,0:T(8,128)(2,1)S(1)}, bf16[32,256]{1,0:T(8,128)(2,1)S(1)}, u32[]{:S(2)}, u32[]{:S(2)}) collective-permute-start(bf16[32,256]{1,0:T(8,128)(2,1)S(1)} %get-tuple-element.109), channel_id=1, source_target_pairs={{0,1},{1,0},{2,3},{3,2},{4,5},{5,4},{6,7},{7,6},{8,9},{9,8},{10,11... | collective-permute-start | bytes 49160 | tf_op jit(solution)/shard_map/ppermute | solution.py:43
  56.2 1.2 %collective-permute-start.38 = (bf16[32,256]{1,0:T(8,128)(2,1)S(1)}, bf16[32,256]{1,0:T(8,128)(2,1)S(1)}, u32[]{:S(2)}, u32[]{:S(2)}) collective-permute-start(bf16[32,256]{1,0:T(8,128)(2,1)S(1)} %get-tuple-element.111), channel_id=1, source_target_pairs={{0,64},{1,65},{2,66},{3,67},{4,68},{5,69},{6,70},{7,71},{8,72},{9,... | collective-permute-start | bytes 49160 | tf_op jit(solution)/shard_map/ppermute | solution.py:43
  58.3 1.7 %collective-permute-start.40 = (bf16[32,256]{1,0:T(8,128)(2,1)S(1)}, bf16[32,256]{1,0:T(8,128)(2,1)S(1)}, u32[]{:S(2)}, u32[]{:S(2)}) collective-permute-start(bf16[32,256]{1,0:T(8,128)(2,1)S(1)} %get-tuple-element.113), channel_id=1, source_target_pairs={{0,64},{1,65},{2,66},{3,67},{4,68},{5,69},{6,70},{7,71},{8,16},{9,... | collective-permute-start | bytes 49160 | tf_op jit(solution)/shard_map/ppermute | solution.py:43
  62.0 2.2 %collective-permute-start.42 = (bf16[32,256]{1,0:T(8,128)(2,1)S(1)}, bf16[32,256]{1,0:T(8,128)(2,1)S(1)}, u32[]{:S(2)}, u32[]{:S(2)}) collective-permute-start(bf16[32,256]{1,0:T(8,128)(2,1)S(1)} %get-tuple-element.116), channel_id=1, source_target_pairs={{0,1},{1,0},{2,3},{3,2},{4,5},{5,4},{6,7},{7,6},{8,9},{9,8},{10,11... | collective-permute-start | bytes 49160 | tf_op jit(solution)/shard_map/ppermute | solution.py:43
  65.2 1.2 %collective-permute-start.45 = (bf16[32,256]{1,0:T(8,128)(2,1)S(1)}, bf16[32,256]{1,0:T(8,128)(2,1)S(1)}, u32[]{:S(2)}, u32[]{:S(2)}) collective-permute-start(bf16[32,256]{1,0:T(8,128)(2,1)S(1)} %get-tuple-element.119), channel_id=1, source_target_pairs={{0,8},{1,9},{2,10},{3,11},{4,12},{5,13},{6,14},{7,15},{8,0},{9,1},... | collective-permute-start | bytes 49160 | tf_op jit(solution)/shard_map/ppermute | solution.py:43
  66.4 1.7 %collective-permute-start.46 = (bf16[32,256]{1,0:T(8,128)(2,1)S(1)}, bf16[32,256]{1,0:T(8,128)(2,1)S(1)}, u32[]{:S(2)}, u32[]{:S(2)}) collective-permute-start(bf16[32,256]{1,0:T(8,128)(2,1)S(1)} %get-tuple-element.120), channel_id=1, source_target_pairs={{0,64},{1,65},{2,66},{3,67},{4,68},{5,69},{6,70},{7,71},{8,16},{9,... | collective-permute-start | bytes 49160 | tf_op jit(solution)/shard_map/ppermute | solution.py:43
  70.2 2.1 %collective-permute-start.48 = (bf16[32,256]{1,0:T(8,128)(2,1)S(1)}, bf16[32,256]{1,0:T(8,128)(2,1)S(1)}, u32[]{:S(2)}, u32[]{:S(2)}) collective-permute-start(bf16[32,256]{1,0:T(8,128)(2,1)S(1)} %get-tuple-element.122), channel_id=1, source_target_pairs={{0,1},{1,0},{2,3},{3,2},{4,5},{5,4},{6,7},{7,6},{8,9},{9,8},{10,11... | collective-permute-start | bytes 49160 | tf_op jit(solution)/shard_map/ppermute | solution.py:43
  74.4 1.5 %collective-permute-start.52 = (bf16[32,256]{1,0:T(8,128)(2,1)S(1)}, bf16[32,256]{1,0:T(8,128)(2,1)S(1)}, u32[]{:S(2)}, u32[]{:S(2)}) collective-permute-start(bf16[32,256]{1,0:T(8,128)(2,1)S(1)} %get-tuple-element.126), channel_id=1, source_target_pairs={{0,64},{1,65},{2,66},{3,67},{4,68},{5,69},{6,70},{7,71},{8,16},{9,... | collective-permute-start | bytes 49160 | tf_op jit(solution)/shard_map/ppermute | solution.py:43
  77.9 11.9 %all_to_all.10 = f32[32,8,128]{2,1,0:T(8,128)S(1)} all-to-all(f32[32,8,128]{2,1,0:T(8,128)S(1)} %broadcast_in_dim.6), channel_id=1, replica_groups=mesh['gx'=4,'gy'=8,'gz'=8] {'gx','gy'}, dimensions={0} | all-to-all | bytes 262144 | tf_op jit(solution)/shard_map/all_to_all | solution.py:403
  89.8 12.8 %all_to_all.11 = f32[8,8,128]{2,1,0:T(8,128)S(1)} all-to-all(f32[8,8,128]{2,1,0:T(8,128)S(1)} %broadcast_in_dim.7), channel_id=1, replica_groups=mesh['gx'=4,'gy'=8,'gz'=8] {'gz'}, dimensions={0} | all-to-all | bytes 65536 | tf_op jit(solution)/shard_map/all_to_all | solution.py:403
  102.6 2.0 %last.1 = (f32[16,512]{1,0:T(8,128)}, f32[1,16]{1,0:T(1,128)}) custom-call(f32[8,128]{1,0:T(8,128)S(1)} %reduce_sum.19.refs_0_, f32[16,512]{1,0:T(8,128)S(1)} %get-tuple-element.74.refs_0_.vector_ref.refs_1_, f32[16,512]{1,0:T(8,128)S(1)} %get-tuple-element.95.refs_0_.vector_ref.refs_2_, f32[16,512]{1,0:T(8,128)S(1)} %get-tuple-element.115.refs_0_.vector_ref.refs_3_), custom_call_target="tpu_custom_call" | custom-call | bytes 102400 | tf_op jit(solution)/shard_map/last/pallas_call | solution.py:383
  (125 shorter events, 34.6 us)
Async XLA Ops:
  2.7 5.0 %collective-permute-start = (f32[24,256]{1,0:T(8,128)S(1)}, f32[24,256]{1,0:T(8,128)S(1)}, u32[]{:S(2)}, u32[]{:S(2)}) collective-permute-start(f32[24,256]{1,0:T(8,128)S(1)} %get-tuple-element.68), channel_id=1, source_target_pairs={{0,1},{1,0},{2,3},{3,2},{4,5},{5,4},{6,7},{7,6},{8,9},{9,8},{10,11... | collective-permute-start | bytes 73736 | tf_op jit(solution)/shard_map/ppermute | solution.py:43
  4.8 7.9 %collective-permute-start.1 = (f32[24,256]{1,0:T(8,128)S(1)}, f32[24,256]{1,0:T(8,128)S(1)}, u32[]{:S(2)}, u32[]{:S(2)}) collective-permute-start(f32[24,256]{1,0:T(8,128)S(1)} %get-tuple-element.69), channel_id=1, source_target_pairs={{0,8},{1,2},{2,1},{3,4},{4,3},{5,6},{6,5},{7,15},{8,0},{9,10},{10,... | collective-permute-start | bytes 73736 | tf_op jit(solution)/shard_map/ppermute | solution.py:43
  4.8 7.9 %collective-permute-start.2 = (f32[24,256]{1,0:T(8,128)S(1)}, f32[24,256]{1,0:T(8,128)S(1)}, u32[]{:S(2)}, u32[]{:S(2)}) collective-permute-start(f32[24,256]{1,0:T(8,128)S(1)} %get-tuple-element.70), channel_id=1, source_target_pairs={{0,64},{1,65},{2,66},{3,67},{4,68},{5,69},{6,70},{7,71},{8,72},{9,... | collective-permute-start | bytes 73736 | tf_op jit(solution)/shard_map/ppermute | solution.py:43
  5.2 7.4 %collective-permute-start.3 = (f32[24,256]{1,0:T(8,128)S(1)}, f32[24,256]{1,0:T(8,128)S(1)}, u32[]{:S(2)}, u32[]{:S(2)}) collective-permute-start(f32[24,256]{1,0:T(8,128)S(1)} %get-tuple-element.71), channel_id=1, source_target_pairs={{0,8},{1,9},{2,10},{3,11},{4,12},{5,13},{6,14},{7,15},{8,0},{9,1},... | collective-permute-start | bytes 73736 | tf_op jit(solution)/shard_map/ppermute | solution.py:43
  7.6 5.0 %collective-permute-start.4 = (f32[24,256]{1,0:T(8,128)S(1)}, f32[24,256]{1,0:T(8,128)S(1)}, u32[]{:S(2)}, u32[]{:S(2)}) collective-permute-start(f32[24,256]{1,0:T(8,128)S(1)} %get-tuple-element.72), channel_id=1, source_target_pairs={{0,64},{1,65},{2,66},{3,67},{4,68},{5,69},{6,70},{7,71},{8,16},{9,... | collective-permute-start | bytes 73736 | tf_op jit(solution)/shard_map/ppermute | solution.py:43
  7.7 5.0 %collective-permute-start.5 = (f32[24,256]{1,0:T(8,128)S(1)}, f32[24,256]{1,0:T(8,128)S(1)}, u32[]{:S(2)}, u32[]{:S(2)}) collective-permute-start(f32[24,256]{1,0:T(8,128)S(1)} %get-tuple-element.73), channel_id=1, source_target_pairs={{0,8},{1,9},{2,10},{3,11},{4,12},{5,13},{6,14},{7,15},{8,0},{9,1},... | collective-permute-start | bytes 73736 | tf_op jit(solution)/shard_map/ppermute | solution.py:43
  13.8 5.6 %collective-permute-start.6 = (bf16[32,256]{1,0:T(8,128)(2,1)S(1)}, bf16[32,256]{1,0:T(8,128)(2,1)S(1)}, u32[]{:S(2)}, u32[]{:S(2)}) collective-permute-start(bf16[32,256]{1,0:T(8,128)(2,1)S(1)} %get-tuple-element.75), channel_id=1, source_target_pairs={{0,1},{1,0},{2,3},{3,2},{4,5},{5,4},{6,7},{7,6},{8,9},{9,8},{10,11... | collective-permute-start | bytes 49160 | tf_op jit(solution)/shard_map/ppermute | solution.py:43
  18.4 3.9 %collective-permute-start.10 = (bf16[32,256]{1,0:T(8,128)(2,1)S(1)}, bf16[32,256]{1,0:T(8,128)(2,1)S(1)}, u32[]{:S(2)}, u32[]{:S(2)}) collective-permute-start(bf16[32,256]{1,0:T(8,128)(2,1)S(1)} %get-tuple-element.79), channel_id=1, source_target_pairs={{0,64},{1,65},{2,66},{3,67},{4,68},{5,69},{6,70},{7,71},{8,16},{9,... | collective-permute-start | bytes 49160 | tf_op jit(solution)/shard_map/ppermute | solution.py:43
  22.7 6.2 %collective-permute-start.12 = (bf16[32,256]{1,0:T(8,128)(2,1)S(1)}, bf16[32,256]{1,0:T(8,128)(2,1)S(1)}, u32[]{:S(2)}, u32[]{:S(2)}) collective-permute-start(bf16[32,256]{1,0:T(8,128)(2,1)S(1)} %get-tuple-element.81), channel_id=1, source_target_pairs={{0,1},{1,0},{2,3},{3,2},{4,5},{5,4},{6,7},{7,6},{8,9},{9,8},{10,11... | collective-permute-start | bytes 49160 | tf_op jit(solution)/shard_map/ppermute | solution.py:43
  27.7 4.0 %collective-permute-start.16 = (bf16[32,256]{1,0:T(8,128)(2,1)S(1)}, bf16[32,256]{1,0:T(8,128)(2,1)S(1)}, u32[]{:S(2)}, u32[]{:S(2)}) collective-permute-start(bf16[32,256]{1,0:T(8,128)(2,1)S(1)} %get-tuple-element.85), channel_id=1, source_target_pairs={{0,64},{1,65},{2,66},{3,67},{4,68},{5,69},{6,70},{7,71},{8,16},{9,... | collective-permute-start | bytes 49160 | tf_op jit(solution)/shard_map/ppermute | solution.py:43
  32.4 4.8 %collective-permute-start.18 = (bf16[32,256]{1,0:T(8,128)(2,1)S(1)}, bf16[32,256]{1,0:T(8,128)(2,1)S(1)}, u32[]{:S(2)}, u32[]{:S(2)}) collective-permute-start(bf16[32,256]{1,0:T(8,128)(2,1)S(1)} %get-tuple-element.88), channel_id=1, source_target_pairs={{0,1},{1,0},{2,3},{3,2},{4,5},{5,4},{6,7},{7,6},{8,9},{9,8},{10,11... | collective-permute-start | bytes 49160 | tf_op jit(solution)/shard_map/ppermute | solution.py:43
  40.1 4.3 %collective-permute-start.24 = (bf16[32,256]{1,0:T(8,128)(2,1)S(1)}, bf16[32,256]{1,0:T(8,128)(2,1)S(1)}, u32[]{:S(2)}, u32[]{:S(2)}) collective-permute-start(bf16[32,256]{1,0:T(8,128)(2,1)S(1)} %get-tuple-element.96), channel_id=1, source_target_pairs={{0,1},{1,0},{2,3},{3,2},{4,5},{5,4},{6,7},{7,6},{8,9},{9,8},{10,11... | collective-permute-start | bytes 49160 | tf_op jit(solution)/shard_map/ppermute | solution.py:43
  46.8 5.2 %collective-permute-start.30 = (bf16[32,256]{1,0:T(8,128)(2,1)S(1)}, bf16[32,256]{1,0:T(8,128)(2,1)S(1)}, u32[]{:S(2)}, u32[]{:S(2)}) collective-permute-start(bf16[32,256]{1,0:T(8,128)(2,1)S(1)} %get-tuple-element.102), channel_id=1, source_target_pairs={{0,1},{1,0},{2,3},{3,2},{4,5},{5,4},{6,7},{7,6},{8,9},{9,8},{10,11... | collective-permute-start | bytes 49160 | tf_op jit(solution)/shard_map/ppermute | solution.py:43
  48.7 3.9 %collective-permute-start.31 = (bf16[32,256]{1,0:T(8,128)(2,1)S(1)}, bf16[32,256]{1,0:T(8,128)(2,1)S(1)}, u32[]{:S(2)}, u32[]{:S(2)}) collective-permute-start(bf16[32,256]{1,0:T(8,128)(2,1)S(1)} %get-tuple-element.103), channel_id=1, source_target_pairs={{0,8},{1,2},{2,1},{3,4},{4,3},{5,6},{6,5},{7,15},{8,0},{9,10},{10,... | collective-permute-start | bytes 49160 | tf_op jit(solution)/shard_map/ppermute | solution.py:43
  48.7 3.9 %collective-permute-start.32 = (bf16[32,256]{1,0:T(8,128)(2,1)S(1)}, bf16[32,256]{1,0:T(8,128)(2,1)S(1)}, u32[]{:S(2)}, u32[]{:S(2)}) collective-permute-start(bf16[32,256]{1,0:T(8,128)(2,1)S(1)} %get-tuple-element.104), channel_id=1, source_target_pairs={{0,64},{1,65},{2,66},{3,67},{4,68},{5,69},{6,70},{7,71},{8,72},{9,... | collective-permute-start | bytes 49160 | tf_op jit(solution)/shard_map/ppermute | solution.py:43
  54.3 5.7 %collective-permute-start.36 = (bf16[32,256]{1,0:T(8,128)(2,1)S(1)}, bf16[32,256]{1,0:T(8,128)(2,1)S(1)}, u32[]{:S(2)}, u32[]{:S(2)}) collective-permute-start(bf16[32,256]{1,0:T(8,128)(2,1)S(1)} %get-tuple-element.109), channel_id=1, source_target_pairs={{0,1},{1,0},{2,3},{3,2},{4,5},{5,4},{6,7},{7,6},{8,9},{9,8},{10,11... | collective-permute-start | bytes 49160 | tf_op jit(solution)/shard_map/ppermute | solution.py:43
  56.2 3.8 %collective-permute-start.37 = (bf16[32,256]{1,0:T(8,128)(2,1)S(1)}, bf16[32,256]{1,0:T(8,128)(2,1)S(1)}, u32[]{:S(2)}, u32[]{:S(2)}) collective-permute-start(bf16[32,256]{1,0:T(8,128)(2,1)S(1)} %get-tuple-element.110), channel_id=1, source_target_pairs={{0,8},{1,2},{2,1},{3,4},{4,3},{5,6},{6,5},{7,15},{8,0},{9,10},{10,... | collective-permute-start | bytes 49160 | tf_op jit(solution)/shard_map/ppermute | solution.py:43
  56.2 3.8 %collective-permute-start.38 = (bf16[32,256]{1,0:T(8,128)(2,1)S(1)}, bf16[32,256]{1,0:T(8,128)(2,1)S(1)}, u32[]{:S(2)}, u32[]{:S(2)}) collective-permute-start(bf16[32,256]{1,0:T(8,128)(2,1)S(1)} %get-tuple-element.111), channel_id=1, source_target_pairs={{0,64},{1,65},{2,66},{3,67},{4,68},{5,69},{6,70},{7,71},{8,72},{9,... | collective-permute-start | bytes 49160 | tf_op jit(solution)/shard_map/ppermute | solution.py:43
  62.0 6.2 %collective-permute-start.42 = (bf16[32,256]{1,0:T(8,128)(2,1)S(1)}, bf16[32,256]{1,0:T(8,128)(2,1)S(1)}, u32[]{:S(2)}, u32[]{:S(2)}) collective-permute-start(bf16[32,256]{1,0:T(8,128)(2,1)S(1)} %get-tuple-element.116), channel_id=1, source_target_pairs={{0,1},{1,0},{2,3},{3,2},{4,5},{5,4},{6,7},{7,6},{8,9},{9,8},{10,11... | collective-permute-start | bytes 49160 | tf_op jit(solution)/shard_map/ppermute | solution.py:43
  64.2 4.5 %collective-permute-start.43 = (bf16[32,256]{1,0:T(8,128)(2,1)S(1)}, bf16[32,256]{1,0:T(8,128)(2,1)S(1)}, u32[]{:S(2)}, u32[]{:S(2)}) collective-permute-start(bf16[32,256]{1,0:T(8,128)(2,1)S(1)} %get-tuple-element.117), channel_id=1, source_target_pairs={{0,8},{1,2},{2,1},{3,4},{4,3},{5,6},{6,5},{7,15},{8,0},{9,10},{10,... | collective-permute-start | bytes 49160 | tf_op jit(solution)/shard_map/ppermute | solution.py:43
  64.2 4.5 %collective-permute-start.44 = (bf16[32,256]{1,0:T(8,128)(2,1)S(1)}, bf16[32,256]{1,0:T(8,128)(2,1)S(1)}, u32[]{:S(2)}, u32[]{:S(2)}) collective-permute-start(bf16[32,256]{1,0:T(8,128)(2,1)S(1)} %get-tuple-element.118), channel_id=1, source_target_pairs={{0,64},{1,65},{2,66},{3,67},{4,68},{5,69},{6,70},{7,71},{8,72},{9,... | collective-permute-start | bytes 49160 | tf_op jit(solution)/shard_map/ppermute | solution.py:43
  70.2 5.7 %collective-permute-start.48 = (bf16[32,256]{1,0:T(8,128)(2,1)S(1)}, bf16[32,256]{1,0:T(8,128)(2,1)S(1)}, u32[]{:S(2)}, u32[]{:S(2)}) collective-permute-start(bf16[32,256]{1,0:T(8,128)(2,1)S(1)} %get-tuple-element.122), channel_id=1, source_target_pairs={{0,1},{1,0},{2,3},{3,2},{4,5},{5,4},{6,7},{7,6},{8,9},{9,8},{10,11... | collective-permute-start | bytes 49160 | tf_op jit(solution)/shard_map/ppermute | solution.py:43
  72.3 4.2 %collective-permute-start.49 = (bf16[32,256]{1,0:T(8,128)(2,1)S(1)}, bf16[32,256]{1,0:T(8,128)(2,1)S(1)}, u32[]{:S(2)}, u32[]{:S(2)}) collective-permute-start(bf16[32,256]{1,0:T(8,128)(2,1)S(1)} %get-tuple-element.123), channel_id=1, source_target_pairs={{0,8},{1,2},{2,1},{3,4},{4,3},{5,6},{6,5},{7,15},{8,0},{9,10},{10,... | collective-permute-start | bytes 49160 | tf_op jit(solution)/shard_map/ppermute | solution.py:43
  72.3 4.2 %collective-permute-start.50 = (bf16[32,256]{1,0:T(8,128)(2,1)S(1)}, bf16[32,256]{1,0:T(8,128)(2,1)S(1)}, u32[]{:S(2)}, u32[]{:S(2)}) collective-permute-start(bf16[32,256]{1,0:T(8,128)(2,1)S(1)} %get-tuple-element.124), channel_id=1, source_target_pairs={{0,64},{1,65},{2,66},{3,67},{4,68},{5,69},{6,70},{7,71},{8,72},{9,... | collective-permute-start | bytes 49160 | tf_op jit(solution)/shard_map/ppermute | solution.py:43
  (34 other events, 107.2 us)

commit v6 on v5

--- a/solution.py
+++ b/solution.py
@@ -262,13 +262,18 @@
 
 def next_kernel(*refs):
     sum_ref, got, places_ref, restricted_ref = refs[0], refs[1:3], refs[3], refs[4]
-    vector_ref, next_ref, slot_refs = refs[5], refs[6], refs[7:]
+    vector_ref, slot_refs = refs[5], refs[6:]
     vector = (sum_ref[...] + added(ORDER[4:], got, places_ref)) * SCALE
     vector_ref[...] = vector
-    products = joined(jnp.dot(split(vector), restricted_ref[...], preferred_element_type=F32))
-    owned = vector.shape[1]
-    next_ref[...] = products[:, :owned]
-    put_split(by_slot(products[:, owned:]), slot_refs)
+    faces = restricted_ref[:, vector.shape[1] :]
+    put_split(by_slot(joined(jnp.dot(split(vector), faces, preferred_element_type=F32))), slot_refs)
+
+
+def own_part_kernel(vector_ref, restricted_ref, own_ref):
+    owned = vector_ref.shape[1]
+    own_ref[...] = joined(
+        jnp.dot(split(vector_ref[...]), restricted_ref[:, :owned], preferred_element_type=F32)
+    )
 
 
 def gram_kernel(*refs):
@@ -465,12 +470,13 @@
         got = ordered(trade(slots))
         (own,) = call(early_kernel, (own, *got[:4], places), (block,), "early")
         if section + 1 < ITERS:
-            vector, own, *slots = call(
+            vector, *slots = call(
                 next_kernel,
                 (own, *got[4:], places, restricted),
-                (block,) * 2 + (parcel,) * 6,
+                (block,) + (parcel,) * 6,
                 "next",
             )
+            (own,) = call(own_part_kernel, (vector, restricted), (block,), "own_part")
             basis.append(vector)
     (gram,) = call(
         gram_kernel, (own, *got[4:], places, *basis), (((rows // 2, 128), F32),), "gram"

time: 106 us -> 106 us (level)
    pallas_call x27 -> x29, Pallas kernels: 16.8 us -> 16.9 us  [call(): pl.pallas_call(kernel, out_shape=tuple((make(shape, dtype) for shape, dty...]
  transfers between devices with their start and end apart: 54 -> 54, of which waited for: 15 -> 15; matrix products, arithmetic and copies ran while one was open for 0% -> 0% of each run, Pallas kernels for 7% -> 8%
where the time goes in v6:
time: 106 us; the launch traced here: 104 us
  starting transfers between devices  49.8 us (47%)
  blocking collectives  24.7 us (23%)
  Pallas kernels  16.9 us (16%)
  waiting for transfers between devices  8.68 us (8%)
  local copies, waits for them, and re-layouts  3.41 us (3%)
    ppermute x54, starting transfers between devices, trade(): lax.ppermute(slots[slot], AXES, partners(slot))  49.8 us
    all_to_all x2, blocking collectives, all_sum(): array = jnp.sum(lax.all_to_all(spread, axis, 0, 0), axis=0)  24.7 us
    pallas_call x29, Pallas kernels, call(): pl.pallas_call(kernel, out_shape=tuple((make(shape, dtype) for shape, dty...  16.9 us
    ppermute x54, waiting for transfers between devices, trade(): lax.ppermute(slots[slot], AXES, partners(slot))  8.68 us
    unnamed x8, local copies, waits for them, and re-layouts  3.39 us
  transfers between devices with their start and end apart: 54, of which 15 were waited for; matrix products, arithmetic and copies ran while one was open for 0% of the time, Pallas kernels for 8%

profile of v6, /device:TPU:10, one launch (start us, length us, event | category | flops | bytes accessed | tf_op | source)
XLA Modules:
  0.0 104.4 jit_solution(4596510570619755852)
XLA Ops:
  0.6 2.1 %first.1 = (f32[16,512]{1,0:T(8,128)S(1)}, f32[24,256]{1,0:T(8,128)S(1)}, f32[24,256]{1,0:T(8,128)S(1)}, f32[24,256]{1,0:T(8,128)S(1)}, f32[24,256]{1,0:T(8,128)...) custom-call(s32[6,1,256]{2,1,0:T(1,128)} %bitcast.26, f32[16,512]{1,0:T(8,128)} %bitcast.24, bf16[512,2048]{1,0:T(8,128)(2,1)} %bitcast.19), custom_call_target="tpu_custom_call" | custom-call | bytes 2136064 | tf_op jit(solution)/shard_map/first/pallas_call | solution.py:388
  2.7 2.0 %collective-permute-start = (f32[24,256]{1,0:T(8,128)S(1)}, f32[24,256]{1,0:T(8,128)S(1)}, u32[]{:S(2)}, u32[]{:S(2)}) collective-permute-start(f32[24,256]{1,0:T(8,128)S(1)} %get-tuple-element.66), channel_id=1, source_target_pairs={{0,1},{1,0},{2,3},{3,2},{4,5},{5,4},{6,7},{7,6},{8,9},{9,8},{10,11... | collective-permute-start | bytes 73736 | tf_op jit(solution)/shard_map/ppermute | solution.py:43
  5.2 2.4 %collective-permute-start.3 = (f32[24,256]{1,0:T(8,128)S(1)}, f32[24,256]{1,0:T(8,128)S(1)}, u32[]{:S(2)}, u32[]{:S(2)}) collective-permute-start(f32[24,256]{1,0:T(8,128)S(1)} %get-tuple-element.69), channel_id=1, source_target_pairs={{0,8},{1,9},{2,10},{3,11},{4,12},{5,13},{6,14},{7,15},{8,0},{9,1},... | collective-permute-start | bytes 73736 | tf_op jit(solution)/shard_map/ppermute | solution.py:43
  7.7 1.5 %collective-permute-start.5 = (f32[24,256]{1,0:T(8,128)S(1)}, f32[24,256]{1,0:T(8,128)S(1)}, u32[]{:S(2)}, u32[]{:S(2)}) collective-permute-start(f32[24,256]{1,0:T(8,128)S(1)} %get-tuple-element.71), channel_id=1, source_target_pairs={{0,8},{1,9},{2,10},{3,11},{4,12},{5,13},{6,14},{7,15},{8,0},{9,1},... | collective-permute-start | bytes 73736 | tf_op jit(solution)/shard_map/ppermute | solution.py:43
  9.2 3.4 %copy-done = bf16[1,1,1,2048,2048]{4,3,2,1,0:T(8,128)(2,1)S(1)} copy-done((bf16[1,1,1,2048,2048]{4,3,2,1,0:T(8,128)(2,1)S(1)}, bf16[1,1,1,2048,2048]{4,3,2,1,0:T(8,128)(2,1)}, u32[]{:S(2)}) %copy-start) | copy-done | bytes 8388632
  13.8 3.9 %collective-permute-start.6 = (bf16[32,256]{1,0:T(8,128)(2,1)S(1)}, bf16[32,256]{1,0:T(8,128)(2,1)S(1)}, u32[]{:S(2)}, u32[]{:S(2)}) collective-permute-start(bf16[32,256]{1,0:T(8,128)(2,1)S(1)} %get-tuple-element.73), channel_id=1, source_target_pairs={{0,1},{1,0},{2,3},{3,2},{4,5},{5,4},{6,7},{7,6},{8,9},{9,8},{10,11... | collective-permute-start | bytes 49160 | tf_op jit(solution)/shard_map/ppermute | solution.py:43
  22.7 4.2 %collective-permute-start.12 = (bf16[32,256]{1,0:T(8,128)(2,1)S(1)}, bf16[32,256]{1,0:T(8,128)(2,1)S(1)}, u32[]{:S(2)}, u32[]{:S(2)}) collective-permute-start(bf16[32,256]{1,0:T(8,128)(2,1)S(1)} %get-tuple-element.79), channel_id=1, source_target_pairs={{0,1},{1,0},{2,3},{3,2},{4,5},{5,4},{6,7},{7,6},{8,9},{9,8},{10,11... | collective-permute-start | bytes 49160 | tf_op jit(solution)/shard_map/ppermute | solution.py:43
  32.3 1.9 %collective-permute-start.18 = (bf16[32,256]{1,0:T(8,128)(2,1)S(1)}, bf16[32,256]{1,0:T(8,128)(2,1)S(1)}, u32[]{:S(2)}, u32[]{:S(2)}) collective-permute-start(bf16[32,256]{1,0:T(8,128)(2,1)S(1)} %get-tuple-element.86), channel_id=1, source_target_pairs={{0,1},{1,0},{2,3},{3,2},{4,5},{5,4},{6,7},{7,6},{8,9},{9,8},{10,11... | collective-permute-start | bytes 49160 | tf_op jit(solution)/shard_map/ppermute | solution.py:43
  40.0 1.4 %collective-permute-start.24 = (bf16[32,256]{1,0:T(8,128)(2,1)S(1)}, bf16[32,256]{1,0:T(8,128)(2,1)S(1)}, u32[]{:S(2)}, u32[]{:S(2)}) collective-permute-start(bf16[32,256]{1,0:T(8,128)(2,1)S(1)} %get-tuple-element.94), channel_id=1, source_target_pairs={{0,1},{1,0},{2,3},{3,2},{4,5},{5,4},{6,7},{7,6},{8,9},{9,8},{10,11... | collective-permute-start | bytes 49160 | tf_op jit(solution)/shard_map/ppermute | solution.py:43
  41.7 1.5 %collective-permute-start.27 = (bf16[32,256]{1,0:T(8,128)(2,1)S(1)}, bf16[32,256]{1,0:T(8,128)(2,1)S(1)}, u32[]{:S(2)}, u32[]{:S(2)}) collective-permute-start(bf16[32,256]{1,0:T(8,128)(2,1)S(1)} %get-tuple-element.97), channel_id=1, source_target_pairs={{0,8},{1,9},{2,10},{3,11},{4,12},{5,13},{6,14},{7,15},{8,0},{9,1},... | collective-permute-start | bytes 49160 | tf_op jit(solution)/shard_map/ppermute | solution.py:43
  43.1 1.2 %collective-permute-start.28 = (bf16[32,256]{1,0:T(8,128)(2,1)S(1)}, bf16[32,256]{1,0:T(8,128)(2,1)S(1)}, u32[]{:S(2)}, u32[]{:S(2)}) collective-permute-start(bf16[32,256]{1,0:T(8,128)(2,1)S(1)} %get-tuple-element.98), channel_id=1, source_target_pairs={{0,64},{1,65},{2,66},{3,67},{4,68},{5,69},{6,70},{7,71},{8,16},{9,... | collective-permute-start | bytes 49160 | tf_op jit(solution)/shard_map/ppermute | solution.py:43
  46.7 1.9 %collective-permute-start.30 = (bf16[32,256]{1,0:T(8,128)(2,1)S(1)}, bf16[32,256]{1,0:T(8,128)(2,1)S(1)}, u32[]{:S(2)}, u32[]{:S(2)}) collective-permute-start(bf16[32,256]{1,0:T(8,128)(2,1)S(1)} %get-tuple-element.100), channel_id=1, source_target_pairs={{0,1},{1,0},{2,3},{3,2},{4,5},{5,4},{6,7},{7,6},{8,9},{9,8},{10,11... | collective-permute-start | bytes 49160 | tf_op jit(solution)/shard_map/ppermute | solution.py:43
  50.4 1.5 %collective-permute-start.34 = (bf16[32,256]{1,0:T(8,128)(2,1)S(1)}, bf16[32,256]{1,0:T(8,128)(2,1)S(1)}, u32[]{:S(2)}, u32[]{:S(2)}) collective-permute-start(bf16[32,256]{1,0:T(8,128)(2,1)S(1)} %get-tuple-element.104), channel_id=1, source_target_pairs={{0,64},{1,65},{2,66},{3,67},{4,68},{5,69},{6,70},{7,71},{8,16},{9,... | collective-permute-start | bytes 49160 | tf_op jit(solution)/shard_map/ppermute | solution.py:43
  54.1 1.9 %collective-permute-start.36 = (bf16[32,256]{1,0:T(8,128)(2,1)S(1)}, bf16[32,256]{1,0:T(8,128)(2,1)S(1)}, u32[]{:S(2)}, u32[]{:S(2)}) collective-permute-start(bf16[32,256]{1,0:T(8,128)(2,1)S(1)} %get-tuple-element.107), channel_id=1, source_target_pairs={{0,1},{1,0},{2,3},{3,2},{4,5},{5,4},{6,7},{7,6},{8,9},{9,8},{10,11... | collective-permute-start | bytes 49160 | tf_op jit(solution)/shard_map/ppermute | solution.py:43
  56.0 1.2 %collective-permute-start.38 = (bf16[32,256]{1,0:T(8,128)(2,1)S(1)}, bf16[32,256]{1,0:T(8,128)(2,1)S(1)}, u32[]{:S(2)}, u32[]{:S(2)}) collective-permute-start(bf16[32,256]{1,0:T(8,128)(2,1)S(1)} %get-tuple-element.109), channel_id=1, source_target_pairs={{0,64},{1,65},{2,66},{3,67},{4,68},{5,69},{6,70},{7,71},{8,72},{9,... | collective-permute-start | bytes 49160 | tf_op jit(solution)/shard_map/ppermute | solution.py:43
  58.1 1.7 %collective-permute-start.40 = (bf16[32,256]{1,0:T(8,128)(2,1)S(1)}, bf16[32,256]{1,0:T(8,128)(2,1)S(1)}, u32[]{:S(2)}, u32[]{:S(2)}) collective-permute-start(bf16[32,256]{1,0:T(8,128)(2,1)S(1)} %get-tuple-element.111), channel_id=1, source_target_pairs={{0,64},{1,65},{2,66},{3,67},{4,68},{5,69},{6,70},{7,71},{8,16},{9,... | collective-permute-start | bytes 49160 | tf_op jit(solution)/shard_map/ppermute | solution.py:43
  61.8 2.2 %collective-permute-start.42 = (bf16[32,256]{1,0:T(8,128)(2,1)S(1)}, bf16[32,256]{1,0:T(8,128)(2,1)S(1)}, u32[]{:S(2)}, u32[]{:S(2)}) collective-permute-start(bf16[32,256]{1,0:T(8,128)(2,1)S(1)} %get-tuple-element.114), channel_id=1, source_target_pairs={{0,1},{1,0},{2,3},{3,2},{4,5},{5,4},{6,7},{7,6},{8,9},{9,8},{10,11... | collective-permute-start | bytes 49160 | tf_op jit(solution)/shard_map/ppermute | solution.py:43
  65.0 1.2 %collective-permute-start.45 = (bf16[32,256]{1,0:T(8,128)(2,1)S(1)}, bf16[32,256]{1,0:T(8,128)(2,1)S(1)}, u32[]{:S(2)}, u32[]{:S(2)}) collective-permute-start(bf16[32,256]{1,0:T(8,128)(2,1)S(1)} %get-tuple-element.117), channel_id=1, source_target_pairs={{0,8},{1,9},{2,10},{3,11},{4,12},{5,13},{6,14},{7,15},{8,0},{9,1},... | collective-permute-start | bytes 49160 | tf_op jit(solution)/shard_map/ppermute | solution.py:43
  66.2 1.7 %collective-permute-start.46 = (bf16[32,256]{1,0:T(8,128)(2,1)S(1)}, bf16[32,256]{1,0:T(8,128)(2,1)S(1)}, u32[]{:S(2)}, u32[]{:S(2)}) collective-permute-start(bf16[32,256]{1,0:T(8,128)(2,1)S(1)} %get-tuple-element.118), channel_id=1, source_target_pairs={{0,64},{1,65},{2,66},{3,67},{4,68},{5,69},{6,70},{7,71},{8,16},{9,... | collective-permute-start | bytes 49160 | tf_op jit(solution)/shard_map/ppermute | solution.py:43
  70.0 2.1 %collective-permute-start.48 = (bf16[32,256]{1,0:T(8,128)(2,1)S(1)}, bf16[32,256]{1,0:T(8,128)(2,1)S(1)}, u32[]{:S(2)}, u32[]{:S(2)}) collective-permute-start(bf16[32,256]{1,0:T(8,128)(2,1)S(1)} %get-tuple-element.120), channel_id=1, source_target_pairs={{0,1},{1,0},{2,3},{3,2},{4,5},{5,4},{6,7},{7,6},{8,9},{9,8},{10,11... | collective-permute-start | bytes 49160 | tf_op jit(solution)/shard_map/ppermute | solution.py:43
  74.2 1.5 %collective-permute-start.52 = (bf16[32,256]{1,0:T(8,128)(2,1)S(1)}, bf16[32,256]{1,0:T(8,128)(2,1)S(1)}, u32[]{:S(2)}, u32[]{:S(2)}) collective-permute-start(bf16[32,256]{1,0:T(8,128)(2,1)S(1)} %get-tuple-element.124), channel_id=1, source_target_pairs={{0,64},{1,65},{2,66},{3,67},{4,68},{5,69},{6,70},{7,71},{8,16},{9,... | collective-permute-start | bytes 49160 | tf_op jit(solution)/shard_map/ppermute | solution.py:43
  77.7 11.9 %all_to_all.10 = f32[32,8,128]{2,1,0:T(8,128)S(1)} all-to-all(f32[32,8,128]{2,1,0:T(8,128)S(1)} %broadcast_in_dim.6), channel_id=1, replica_groups=mesh['gx'=4,'gy'=8,'gz'=8] {'gx','gy'}, dimensions={0} | all-to-all | bytes 262144 | tf_op jit(solution)/shard_map/all_to_all | solution.py:408
  89.7 12.8 %all_to_all.11 = f32[8,8,128]{2,1,0:T(8,128)S(1)} all-to-all(f32[8,8,128]{2,1,0:T(8,128)S(1)} %broadcast_in_dim.7), channel_id=1, replica_groups=mesh['gx'=4,'gy'=8,'gz'=8] {'gz'}, dimensions={0} | all-to-all | bytes 65536 | tf_op jit(solution)/shard_map/all_to_all | solution.py:408
  102.4 2.0 %last.1 = (f32[16,512]{1,0:T(8,128)}, f32[1,16]{1,0:T(1,128)}) custom-call(f32[8,128]{1,0:T(8,128)S(1)} %reduce_sum.19.refs_0_, f32[16,512]{1,0:T(8,128)S(1)} %get-tuple-element.72.refs_0_.vector_ref.refs_1_, f32[16,512]{1,0:T(8,128)S(1)} %get-tuple-element.93.refs_0_.vector_ref.refs_2_, f32[16,512]{1,0:T(8,128)S(1)} %get-tuple-element.113.refs_0_.vector_ref.refs_3_), custom_call_target="tpu_custom_call" | custom-call | bytes 102400 | tf_op jit(solution)/shard_map/last/pallas_call | solution.py:388
  (127 shorter events, 34.4 us)
Async XLA Ops:
  2.7 5.0 %collective-permute-start = (f32[24,256]{1,0:T(8,128)S(1)}, f32[24,256]{1,0:T(8,128)S(1)}, u32[]{:S(2)}, u32[]{:S(2)}) collective-permute-start(f32[24,256]{1,0:T(8,128)S(1)} %get-tuple-element.66), channel_id=1, source_target_pairs={{0,1},{1,0},{2,3},{3,2},{4,5},{5,4},{6,7},{7,6},{8,9},{9,8},{10,11... | collective-permute-start | bytes 73736 | tf_op jit(solution)/shard_map/ppermute | solution.py:43
  4.8 7.9 %collective-permute-start.1 = (f32[24,256]{1,0:T(8,128)S(1)}, f32[24,256]{1,0:T(8,128)S(1)}, u32[]{:S(2)}, u32[]{:S(2)}) collective-permute-start(f32[24,256]{1,0:T(8,128)S(1)} %get-tuple-element.67), channel_id=1, source_target_pairs={{0,8},{1,2},{2,1},{3,4},{4,3},{5,6},{6,5},{7,15},{8,0},{9,10},{10,... | collective-permute-start | bytes 73736 | tf_op jit(solution)/shard_map/ppermute | solution.py:43
  4.8 7.9 %collective-permute-start.2 = (f32[24,256]{1,0:T(8,128)S(1)}, f32[24,256]{1,0:T(8,128)S(1)}, u32[]{:S(2)}, u32[]{:S(2)}) collective-permute-start(f32[24,256]{1,0:T(8,128)S(1)} %get-tuple-element.68), channel_id=1, source_target_pairs={{0,64},{1,65},{2,66},{3,67},{4,68},{5,69},{6,70},{7,71},{8,72},{9,... | collective-permute-start | bytes 73736 | tf_op jit(solution)/shard_map/ppermute | solution.py:43
  5.2 7.4 %collective-permute-start.3 = (f32[24,256]{1,0:T(8,128)S(1)}, f32[24,256]{1,0:T(8,128)S(1)}, u32[]{:S(2)}, u32[]{:S(2)}) collective-permute-start(f32[24,256]{1,0:T(8,128)S(1)} %get-tuple-element.69), channel_id=1, source_target_pairs={{0,8},{1,9},{2,10},{3,11},{4,12},{5,13},{6,14},{7,15},{8,0},{9,1},... | collective-permute-start | bytes 73736 | tf_op jit(solution)/shard_map/ppermute | solution.py:43
  7.6 5.0 %collective-permute-start.4 = (f32[24,256]{1,0:T(8,128)S(1)}, f32[24,256]{1,0:T(8,128)S(1)}, u32[]{:S(2)}, u32[]{:S(2)}) collective-permute-start(f32[24,256]{1,0:T(8,128)S(1)} %get-tuple-element.70), channel_id=1, source_target_pairs={{0,64},{1,65},{2,66},{3,67},{4,68},{5,69},{6,70},{7,71},{8,16},{9,... | collective-permute-start | bytes 73736 | tf_op jit(solution)/shard_map/ppermute | solution.py:43
  7.7 5.0 %collective-permute-start.5 = (f32[24,256]{1,0:T(8,128)S(1)}, f32[24,256]{1,0:T(8,128)S(1)}, u32[]{:S(2)}, u32[]{:S(2)}) collective-permute-start(f32[24,256]{1,0:T(8,128)S(1)} %get-tuple-element.71), channel_id=1, source_target_pairs={{0,8},{1,9},{2,10},{3,11},{4,12},{5,13},{6,14},{7,15},{8,0},{9,1},... | collective-permute-start | bytes 73736 | tf_op jit(solution)/shard_map/ppermute | solution.py:43
  13.8 5.6 %collective-permute-start.6 = (bf16[32,256]{1,0:T(8,128)(2,1)S(1)}, bf16[32,256]{1,0:T(8,128)(2,1)S(1)}, u32[]{:S(2)}, u32[]{:S(2)}) collective-permute-start(bf16[32,256]{1,0:T(8,128)(2,1)S(1)} %get-tuple-element.73), channel_id=1, source_target_pairs={{0,1},{1,0},{2,3},{3,2},{4,5},{5,4},{6,7},{7,6},{8,9},{9,8},{10,11... | collective-permute-start | bytes 49160 | tf_op jit(solution)/shard_map/ppermute | solution.py:43
  18.4 3.9 %collective-permute-start.10 = (bf16[32,256]{1,0:T(8,128)(2,1)S(1)}, bf16[32,256]{1,0:T(8,128)(2,1)S(1)}, u32[]{:S(2)}, u32[]{:S(2)}) collective-permute-start(bf16[32,256]{1,0:T(8,128)(2,1)S(1)} %get-tuple-element.77), channel_id=1, source_target_pairs={{0,64},{1,65},{2,66},{3,67},{4,68},{5,69},{6,70},{7,71},{8,16},{9,... | collective-permute-start | bytes 49160 | tf_op jit(solution)/shard_map/ppermute | solution.py:43
  22.7 6.2 %collective-permute-start.12 = (bf16[32,256]{1,0:T(8,128)(2,1)S(1)}, bf16[32,256]{1,0:T(8,128)(2,1)S(1)}, u32[]{:S(2)}, u32[]{:S(2)}) collective-permute-start(bf16[32,256]{1,0:T(8,128)(2,1)S(1)} %get-tuple-element.79), channel_id=1, source_target_pairs={{0,1},{1,0},{2,3},{3,2},{4,5},{5,4},{6,7},{7,6},{8,9},{9,8},{10,11... | collective-permute-start | bytes 49160 | tf_op jit(solution)/shard_map/ppermute | solution.py:43
  27.7 4.0 %collective-permute-start.16 = (bf16[32,256]{1,0:T(8,128)(2,1)S(1)}, bf16[32,256]{1,0:T(8,128)(2,1)S(1)}, u32[]{:S(2)}, u32[]{:S(2)}) collective-permute-start(bf16[32,256]{1,0:T(8,128)(2,1)S(1)} %get-tuple-element.83), channel_id=1, source_target_pairs={{0,64},{1,65},{2,66},{3,67},{4,68},{5,69},{6,70},{7,71},{8,16},{9,... | collective-permute-start | bytes 49160 | tf_op jit(solution)/shard_map/ppermute | solution.py:43
  32.3 4.8 %collective-permute-start.18 = (bf16[32,256]{1,0:T(8,128)(2,1)S(1)}, bf16[32,256]{1,0:T(8,128)(2,1)S(1)}, u32[]{:S(2)}, u32[]{:S(2)}) collective-permute-start(bf16[32,256]{1,0:T(8,128)(2,1)S(1)} %get-tuple-element.86), channel_id=1, source_target_pairs={{0,1},{1,0},{2,3},{3,2},{4,5},{5,4},{6,7},{7,6},{8,9},{9,8},{10,11... | collective-permute-start | bytes 49160 | tf_op jit(solution)/shard_map/ppermute | solution.py:43
  40.0 4.3 %collective-permute-start.24 = (bf16[32,256]{1,0:T(8,128)(2,1)S(1)}, bf16[32,256]{1,0:T(8,128)(2,1)S(1)}, u32[]{:S(2)}, u32[]{:S(2)}) collective-permute-start(bf16[32,256]{1,0:T(8,128)(2,1)S(1)} %get-tuple-element.94), channel_id=1, source_target_pairs={{0,1},{1,0},{2,3},{3,2},{4,5},{5,4},{6,7},{7,6},{8,9},{9,8},{10,11... | collective-permute-start | bytes 49160 | tf_op jit(solution)/shard_map/ppermute | solution.py:43
  46.7 5.2 %collective-permute-start.30 = (bf16[32,256]{1,0:T(8,128)(2,1)S(1)}, bf16[32,256]{1,0:T(8,128)(2,1)S(1)}, u32[]{:S(2)}, u32[]{:S(2)}) collective-permute-start(bf16[32,256]{1,0:T(8,128)(2,1)S(1)} %get-tuple-element.100), channel_id=1, source_target_pairs={{0,1},{1,0},{2,3},{3,2},{4,5},{5,4},{6,7},{7,6},{8,9},{9,8},{10,11... | collective-permute-start | bytes 49160 | tf_op jit(solution)/shard_map/ppermute | solution.py:43
  48.6 3.9 %collective-permute-start.31 = (bf16[32,256]{1,0:T(8,128)(2,1)S(1)}, bf16[32,256]{1,0:T(8,128)(2,1)S(1)}, u32[]{:S(2)}, u32[]{:S(2)}) collective-permute-start(bf16[32,256]{1,0:T(8,128)(2,1)S(1)} %get-tuple-element.101), channel_id=1, source_target_pairs={{0,8},{1,2},{2,1},{3,4},{4,3},{5,6},{6,5},{7,15},{8,0},{9,10},{10,... | collective-permute-start | bytes 49160 | tf_op jit(solution)/shard_map/ppermute | solution.py:43
  48.6 3.9 %collective-permute-start.32 = (bf16[32,256]{1,0:T(8,128)(2,1)S(1)}, bf16[32,256]{1,0:T(8,128)(2,1)S(1)}, u32[]{:S(2)}, u32[]{:S(2)}) collective-permute-start(bf16[32,256]{1,0:T(8,128)(2,1)S(1)} %get-tuple-element.102), channel_id=1, source_target_pairs={{0,64},{1,65},{2,66},{3,67},{4,68},{5,69},{6,70},{7,71},{8,72},{9,... | collective-permute-start | bytes 49160 | tf_op jit(solution)/shard_map/ppermute | solution.py:43
  54.1 5.7 %collective-permute-start.36 = (bf16[32,256]{1,0:T(8,128)(2,1)S(1)}, bf16[32,256]{1,0:T(8,128)(2,1)S(1)}, u32[]{:S(2)}, u32[]{:S(2)}) collective-permute-start(bf16[32,256]{1,0:T(8,128)(2,1)S(1)} %get-tuple-element.107), channel_id=1, source_target_pairs={{0,1},{1,0},{2,3},{3,2},{4,5},{5,4},{6,7},{7,6},{8,9},{9,8},{10,11... | collective-permute-start | bytes 49160 | tf_op jit(solution)/shard_map/ppermute | solution.py:43
  56.0 4.0 %collective-permute-start.37 = (bf16[32,256]{1,0:T(8,128)(2,1)S(1)}, bf16[32,256]{1,0:T(8,128)(2,1)S(1)}, u32[]{:S(2)}, u32[]{:S(2)}) collective-permute-start(bf16[32,256]{1,0:T(8,128)(2,1)S(1)} %get-tuple-element.108), channel_id=1, source_target_pairs={{0,8},{1,2},{2,1},{3,4},{4,3},{5,6},{6,5},{7,15},{8,0},{9,10},{10,... | collective-permute-start | bytes 49160 | tf_op jit(solution)/shard_map/ppermute | solution.py:43
  56.0 4.0 %collective-permute-start.38 = (bf16[32,256]{1,0:T(8,128)(2,1)S(1)}, bf16[32,256]{1,0:T(8,128)(2,1)S(1)}, u32[]{:S(2)}, u32[]{:S(2)}) collective-permute-start(bf16[32,256]{1,0:T(8,128)(2,1)S(1)} %get-tuple-element.109), channel_id=1, source_target_pairs={{0,64},{1,65},{2,66},{3,67},{4,68},{5,69},{6,70},{7,71},{8,72},{9,... | collective-permute-start | bytes 49160 | tf_op jit(solution)/shard_map/ppermute | solution.py:43
  61.8 6.2 %collective-permute-start.42 = (bf16[32,256]{1,0:T(8,128)(2,1)S(1)}, bf16[32,256]{1,0:T(8,128)(2,1)S(1)}, u32[]{:S(2)}, u32[]{:S(2)}) collective-permute-start(bf16[32,256]{1,0:T(8,128)(2,1)S(1)} %get-tuple-element.114), channel_id=1, source_target_pairs={{0,1},{1,0},{2,3},{3,2},{4,5},{5,4},{6,7},{7,6},{8,9},{9,8},{10,11... | collective-permute-start | bytes 49160 | tf_op jit(solution)/shard_map/ppermute | solution.py:43
  64.0 4.5 %collective-permute-start.43 = (bf16[32,256]{1,0:T(8,128)(2,1)S(1)}, bf16[32,256]{1,0:T(8,128)(2,1)S(1)}, u32[]{:S(2)}, u32[]{:S(2)}) collective-permute-start(bf16[32,256]{1,0:T(8,128)(2,1)S(1)} %get-tuple-element.115), channel_id=1, source_target_pairs={{0,8},{1,2},{2,1},{3,4},{4,3},{5,6},{6,5},{7,15},{8,0},{9,10},{10,... | collective-permute-start | bytes 49160 | tf_op jit(solution)/shard_map/ppermute | solution.py:43
  64.0 4.5 %collective-permute-start.44 = (bf16[32,256]{1,0:T(8,128)(2,1)S(1)}, bf16[32,256]{1,0:T(8,128)(2,1)S(1)}, u32[]{:S(2)}, u32[]{:S(2)}) collective-permute-start(bf16[32,256]{1,0:T(8,128)(2,1)S(1)} %get-tuple-element.116), channel_id=1, source_target_pairs={{0,64},{1,65},{2,66},{3,67},{4,68},{5,69},{6,70},{7,71},{8,72},{9,... | collective-permute-start | bytes 49160 | tf_op jit(solution)/shard_map/ppermute | solution.py:43
  70.0 5.7 %collective-permute-start.48 = (bf16[32,256]{1,0:T(8,128)(2,1)S(1)}, bf16[32,256]{1,0:T(8,128)(2,1)S(1)}, u32[]{:S(2)}, u32[]{:S(2)}) collective-permute-start(bf16[32,256]{1,0:T(8,128)(2,1)S(1)} %get-tuple-element.120), channel_id=1, source_target_pairs={{0,1},{1,0},{2,3},{3,2},{4,5},{5,4},{6,7},{7,6},{8,9},{9,8},{10,11... | collective-permute-start | bytes 49160 | tf_op jit(solution)/shard_map/ppermute | solution.py:43
  72.1 4.2 %collective-permute-start.49 = (bf16[32,256]{1,0:T(8,128)(2,1)S(1)}, bf16[32,256]{1,0:T(8,128)(2,1)S(1)}, u32[]{:S(2)}, u32[]{:S(2)}) collective-permute-start(bf16[32,256]{1,0:T(8,128)(2,1)S(1)} %get-tuple-element.121), channel_id=1, source_target_pairs={{0,8},{1,2},{2,1},{3,4},{4,3},{5,6},{6,5},{7,15},{8,0},{9,10},{10,... | collective-permute-start | bytes 49160 | tf_op jit(solution)/shard_map/ppermute | solution.py:43
  72.1 4.2 %collective-permute-start.50 = (bf16[32,256]{1,0:T(8,128)(2,1)S(1)}, bf16[32,256]{1,0:T(8,128)(2,1)S(1)}, u32[]{:S(2)}, u32[]{:S(2)}) collective-permute-start(bf16[32,256]{1,0:T(8,128)(2,1)S(1)} %get-tuple-element.122), channel_id=1, source_target_pairs={{0,64},{1,65},{2,66},{3,67},{4,68},{5,69},{6,70},{7,71},{8,72},{9,... | collective-permute-start | bytes 49160 | tf_op jit(solution)/shard_map/ppermute | solution.py:43
  (34 other events, 107.4 us)
